TPU v7x, 512 devices: a whole 4x4x16 slice. The times are simulated.
512 devices in a mesh: kgrp: 16 (over y, x), energy: 32 (over z, core).
Axes of the slice: x: 4, y: 4, z: 16, core: 2. Of those that a mesh axis runs over, the one named last changes fastest.
Arguments:
- greens: float32 [2, 2, 2, 1024, 4096], P(None, None, None, 'kgrp', 'energy'), may hold values from -6 to 6
- current: float32 [2, 2, 2, 1024, 4096], P(None, None, None, ('kgrp', 'energy')), may hold values from -6 to 6
- past_inputs: float32 [5, 2, 2, 2, 1024, 4096], P(None, None, None, None, ('kgrp', 'energy')), may hold values from -6 to 6
- past_residuals: float32 [5, 2, 2, 2, 1024, 4096], P(None, None, None, None, ('kgrp', 'energy')), may hold values from -40 to 40
- slot_order: int32 [5], replicated, may hold values from 0 to 4, each once
- neighbour: int32 [1024, 5], P('kgrp'), may hold values from 0 to 1023, as said below
- momentum_class: int32 [1024], P('kgrp'), may hold values from 0 to 3
- stencil_weight: float32 [5], replicated, may hold values from 0.1 to 0.4
- acoustic_coupling: float32 [4], replicated, may hold values from 0.3 to 1.5
- optical_coupling: float32 [2], replicated, may hold values from 0.2 to 0.6
- occupation: float32 [2], replicated, may hold values from 0.1 to 1
- phonon_shift: int32 [2], replicated, may hold values from 32 to 96, as said below
Outputs:
- mixed: float32 [2, 2, 2, 1024, 4096], P(None, None, None, ('kgrp', 'energy'))
Inputs may be any that keep to these rules, and one draw needn't show every extreme that they name: `neighbour`: each index names a momentum of the row's own group of 64 consecutive momenta or of the group just before or after it, counted periodically over all groups. `phonon_shift`: the larger of the two shifts is exactly 96.
All inputs are finite; a program needn't handle non-finite values.
Results may differ from a plain program's by a relative error of at most 0.000053.
Values sent between devices are 32-bit elements; how exact they have to be, the bound alone decides.
A program may use at most 64 MiB of HBM per device.

v0:
```python
import jax
import jax.numpy as jnp
from jax import lax
from jax.sharding import PartitionSpec as P

SHIFT_MAX = 96
HIST = 5


mixing_share = 0.5
ridge_share = 0.1


def padded_2(block, sides, width, periodic):
    for axis, dim in sides:
        count = lax.axis_size(axis)
        forward = [(i, i + 1) for i in range(count - 1)]
        if periodic:
            forward.append((count - 1, 0))
        backward = [(target, source) for source, target in forward]
        low = lax.ppermute(
            lax.slice_in_dim(block, block.shape[dim] - width, None, axis=dim), axis, forward
        )
        high = lax.ppermute(lax.slice_in_dim(block, 0, width, axis=dim), axis, backward)
        block = jnp.concatenate([low, block, high], axis=dim)
    return block


def emit(padded, margin, length, coupling_row, optical, occupation, shifts):
    lesser = padded[0]
    greater = padded[1]

    def energy_view(source, offset):
        return lax.dynamic_slice_in_dim(source, margin + offset, length, axis=source.ndim - 1)

    sigma_less = coupling_row[:, None] * energy_view(lesser, 0)
    sigma_more = coupling_row[:, None] * energy_view(greater, 0)
    for column in range(2):
        strength = optical[column]
        number = occupation[column]
        offset = shifts[column]
        sigma_less = sigma_less + strength * (
            (number + 1.0) * energy_view(lesser, offset) + number * energy_view(lesser, -offset)
        )
        sigma_more = sigma_more + strength * (
            (number + 1.0) * energy_view(greater, -offset) + number * energy_view(greater, offset)
        )
    return jnp.stack([sigma_less, sigma_more])


def solve_spd(matrix, vector):
    factor = jnp.linalg.cholesky(matrix)
    size_n = matrix.shape[0]
    forward = []
    for column in range(size_n):
        summed = vector[column]
        for earlier in range(column):
            summed = summed - factor[column, earlier] * forward[earlier]
        forward.append(summed / factor[column, column])
    backward = [None] * size_n
    for column in range(size_n - 1, -1, -1):
        summed = forward[column]
        for earlier in range(column + 1, size_n):
            summed = summed - factor[earlier, column] * backward[earlier]
        backward[column] = summed / factor[column, column]
    return jnp.stack(backward)


def mix_weights(products):
    size_n = products.shape[0] - 1
    differ_rows = jnp.eye(size_n, size_n + 1, dtype=jnp.float32) - jnp.eye(
        size_n, size_n + 1, k=1, dtype=jnp.float32
    )
    system = jnp.dot(
        jnp.dot(differ_rows, products, precision=lax.Precision.HIGHEST),
        differ_rows.T,
        precision=lax.Precision.HIGHEST,
    )
    target = jnp.dot(differ_rows, products[:, 0], precision=lax.Precision.HIGHEST)
    ridge = ridge_share * jnp.trace(system) / size_n + 1e-06
    gamma = solve_spd(system + ridge * jnp.eye(size_n, dtype=jnp.float32), target)
    unit = jnp.zeros((size_n + 1,), jnp.float32).at[0].set(1.0)
    return unit - jnp.dot(differ_rows.T, gamma, precision=lax.Precision.HIGHEST)


def per_device(
    greens,
    current,
    past_inputs,
    past_residuals,
    slot_order,
    neighbour,
    momentum_class,
    stencil_weight,
    acoustic_coupling,
    optical_coupling,
    occupation,
    phonon_shift,
):
    group_len = greens.shape[3]
    slice_len = greens.shape[4]
    group_id = lax.axis_index("kgrp")
    total_k = group_len * lax.axis_size("kgrp")
    history = past_residuals.reshape(HIST, -1)
    extended = padded_2(greens, (("kgrp", 3),), group_len, True)
    local_index = (neighbour - group_id * group_len + group_len) % total_k
    smeared = jnp.zeros_like(greens)
    for column in range(5):
        smeared = smeared + stencil_weight[column] * jnp.take(
            extended, local_index[:, column], axis=3
        )
    classes = acoustic_coupling.shape[0]
    coupling_row = jnp.sum(
        jnp.where(
            momentum_class[:, None] == jnp.arange(classes, dtype=jnp.int32)[None, :],
            acoustic_coupling[None, :],
            0.0,
        ),
        axis=1,
    )
    padded = padded_2(smeared, (("energy", 4),), SHIFT_MAX, False)
    sigma_slice = emit(
        padded, SHIFT_MAX, slice_len, coupling_row, optical_coupling, occupation, phonon_shift
    )
    sigma_new = lax.all_to_all(sigma_slice, "energy", split_axis=3, concat_axis=4, tiled=True)
    residual_now = sigma_new - current
    fresh = residual_now.reshape(-1)
    new_local = jnp.concatenate(
        [jnp.sum(fresh * fresh)[None], jnp.dot(history, fresh, precision=lax.Precision.HIGHEST)]
    )
    old_products, new_products = lax.psum(
        (jnp.dot(history, history.T, precision=lax.Precision.HIGHEST), new_local),
        ("kgrp", "energy"),
    )
    entries = float(fresh.shape[0] * lax.axis_size("kgrp") * lax.axis_size("energy"))
    reorder = (slot_order[:, None] == jnp.arange(HIST, dtype=jnp.int32)[None, :]).astype(
        jnp.float32
    )
    old_aged = jnp.dot(
        jnp.dot(reorder, old_products, precision=lax.Precision.HIGHEST),
        reorder.T,
        precision=lax.Precision.HIGHEST,
    )
    new_aged = jnp.dot(reorder, new_products[1:], precision=lax.Precision.HIGHEST)
    top_row = jnp.concatenate([new_products[:1], new_aged])[None, :]
    lower_rows = jnp.concatenate([new_aged[:, None], old_aged], axis=1)
    products = jnp.concatenate([top_row, lower_rows], axis=0) / entries
    weights = mix_weights(products)
    slot_weights = jnp.dot(reorder.T, weights[1:], precision=lax.Precision.HIGHEST)
    mixed = weights[0] * (current + mixing_share * residual_now)
    for column in range(HIST):
        mixed = mixed + slot_weights[column] * (
            past_inputs[column] + mixing_share * past_residuals[column]
        )
    return mixed


def solution(mesh):
    return jax.shard_map(
        per_device,
        mesh=mesh,
        in_specs=(
            P(None, None, None, "kgrp", "energy"),
            P(None, None, None, ("kgrp", "energy"), None),
            P(None, None, None, None, ("kgrp", "energy"), None),
            P(None, None, None, None, ("kgrp", "energy"), None),
            P(),
            P("kgrp", None),
            P("kgrp"),
            P(),
            P(),
            P(),
            P(),
            P(),
        ),
        out_specs=P(None, None, None, ("kgrp", "energy"), None),
        check_vma=False,
    )
```

profile of v0, /device:TPU:1, one launch (start us, length us, event | category | flops | bytes accessed | tf_op | source)
XLA Modules:
  0.0 223.4 jit_solution(8509440534947344868)
XLA Ops:
  0.0 1.2 copy.61
  1.2 3.9 %collective-permute-start = (f32[2,2,2,64,128]{4,2,3,1,0:T(2,128)S(1)}, f32[2,2,2,64,128]{4,2,3,1,0:T(2,128)S(1)}, u32[]{:S(2)}, u32[]{:S(2)}) collective-permute-start(f32[2,2,2,64,128]{4,2,3,1,0:T(2,128)S(1)} %copy.61), channel_id=1, source_target_pairs={{0,32},{32,64},{64,96},{96,128},{128,160},{160,192},{192,224},{224... | collective-permute-start | bytes 786440 | tf_op jit(solution)/shard_map/ppermute | solution.py:21
  5.2 5.6 %collective-permute-start.1 = (f32[2,2,2,64,128]{4,2,3,1,0:T(2,128)S(1)}, f32[2,2,2,64,128]{4,2,3,1,0:T(2,128)S(1)}, u32[]{:S(2)}, u32[]{:S(2)}) collective-permute-start(f32[2,2,2,64,128]{4,2,3,1,0:T(2,128)S(1)} %copy.61), channel_id=1, source_target_pairs={{32,0},{64,32},{96,64},{128,96},{160,128},{192,160},{224,192},{256... | collective-permute-start | bytes 786440 | tf_op jit(solution)/shard_map/ppermute | solution.py:24
  10.8 0.7 add_select_fusion
  11.6 1.4 fusion.50
  12.9 1.3 fusion.49
  19.3 1.5 fusion.51
  21.2 0.9 gather_fusion.1
  22.1 0.9 gather_fusion.2
  23.0 0.9 gather_fusion.3
  23.9 0.9 gather_fusion.4
  24.8 0.9 gather_fusion
  25.8 3.5 %fusion.11 = f32[2,2,2,64,128]{4,3,2,1,0:T(8,128)S(1)} fusion(f32[64,2,2,2,128]{4,3,2,1,0:T(2,128)S(1)} %gather_fusion.4, f32[64,2,2,2,128]{4,3,2,1,0:T(2,128)S(1)} %gather_fusion.3, f32[64,2,2,2,128]{4,3,2,1,0:T(2,128)S(1)} %gather_fusion.2, f32[64,2,2,2,128]{4,3,2,1,0:T(2,128)S(1)} %gather_fusion.1, f32[64,2,2,2,128]{4,3,2,1,0:T(2,128)S(1)} %gather_fusion, ...), kind=kLoop, calls=%fused_computation.23 | loop fusion | flops 917504 | bytes 1573204 | tf_op jit(solution)/shard_map/add | solution.py:109
  29.5 4.5 %collective-permute-start.2 = (f32[2,2,2,64,96]{4,3,2,1,0:T(8,128)S(1)}, f32[2,2,2,64,96]{4,3,2,1,0:T(8,128)S(1)}, u32[]{:S(2)}, u32[]{:S(2)}) collective-permute-start(f32[2,2,2,64,96]{4,3,2,1,0:T(8,128)S(1)} %get-tuple-element.36), channel_id=1, source_target_pairs={{0,1},{1,2},{2,3},{3,4},{4,5},{5,6},{6,7},{7,8},{8,9},{9,10},{10,1... | collective-permute-start | bytes 589832 | tf_op jit(solution)/shard_map/ppermute | solution.py:21
  34.0 5.2 %collective-permute-start.3 = (f32[2,2,2,64,96]{4,3,2,1,0:T(8,128)S(1)}, f32[2,2,2,64,96]{4,3,2,1,0:T(8,128)S(1)}, u32[]{:S(2)}, u32[]{:S(2)}) collective-permute-start(f32[2,2,2,64,96]{4,3,2,1,0:T(8,128)S(1)} %get-tuple-element.37), channel_id=1, source_target_pairs={{1,0},{2,1},{3,2},{4,3},{5,4},{6,5},{7,6},{8,7},{9,8},{10,9},{11,1... | collective-permute-start | bytes 589832 | tf_op jit(solution)/shard_map/ppermute | solution.py:24
  39.9 1.8 collective-permute-done.3
  42.2 3.0 %fusion.21 = (f32[1,2,2,64,128]{4,3,2,1,0:T(8,128)S(1)}, f32[1,2,2,64,128]{4,3,2,1,0:T(8,128)S(1)}) fusion(f32[2,2,64,320]{3,2,1,0:T(8,128)S(1)} %get-tuple-element.31, f32[1,2,2,64,320]{4,3,2,1,0:T(8,128)S(1)} %get-tuple-element.30, s32[]{:T(128)S(6)} %select_n.48, s32[]{:T(128)S(6)} %select_n.47, s32[]{:T(128)S(6)} %select_n.46, s32[]{:T(128)S(6)} %select_n.45, ...), kind=kLoop, calls=%fused_computation.45 | loop fusion | flops 720896 | bytes 1573160 | tf_op jit(solution)/shard_map/stack | solution.py:48
  45.2 0.9 copy.69
  46.1 15.2 %all-to-all-start = ((f32[2,2,2,64,128]{4,2,1,0,3:T(2,128)}), f32[2,2,2,64,128]{4,2,1,0,3:T(2,128)S(1)}, u32[]{:S(2)}, u32[]{:S(2)}) async-start(f32[2,2,2,64,128]{4,2,1,0,3:T(2,128)} %copy.69), calls=%async_computation | async-start | bytes 524288 | tf_op jit(solution)/shard_map/all_to_all | solution.py:125
  61.4 5.2 %fusion.4 = f32[5,5]{1,0:T(8,128)S(1)} fusion(f32[5,2,2,2,2,4096]{5,4,3,2,1,0:T(2,128)S(1)} %copy-done), kind=kOutput, calls=%fused_computation.9 | convolution fusion | flops 19660800 | bytes 1310820 | tf_op jit(solution)/shard_map/dot_general | solution.py:132
  66.5 16.8 %all-to-all-done = f32[2,2,2,64,128]{4,2,1,0,3:T(2,128)S(1)} async-done(((f32[2,2,2,64,128]{4,2,1,0,3:T(2,128)}), f32[2,2,2,64,128]{4,2,1,0,3:T(2,128)S(1)}, u32[]{:S(2)}, u32[]{:S(2)}) %all-to-all-start) | async-done | bytes 262176 | tf_op jit(solution)/shard_map/all_to_all | solution.py:125
  83.6 0.9 multiply_reduce_fusion
  84.5 4.8 %fusion.7 = f32[5]{0:T(128)S(1)} fusion(f32[5,2,2,2,2,4096]{5,4,3,2,1,0:T(2,128)S(1)} %copy-done, f32[2,2,2,2,4096,1]{4,3,2,1,0,5:T(2,128)S(1)} %get-tuple-element.35), kind=kOutput, calls=%fused_computation.12 | convolution fusion | flops 3932160 | bytes 1572884 | tf_op jit(solution)/shard_map/dot_general | solution.py:129
  89.2 0.7 pad_maximum_fusion.2
  90.0 99.0 %all-reduce = (f32[5,5]{1,0:T(8,128)S(1)}, f32[6]{0:T(128)S(1)}) all-reduce(f32[5,5]{1,0:T(8,128)S(1)} %fusion.4, f32[6]{0:T(128)S(1)} %pad_maximum_fusion.2), channel_id=1, replica_groups=mesh['kgrp'=16,'energy'=32] {'kgrp','energy'}, use_global_device_ids=true, to_apply=%region_3.5 | all-reduce | flops 31 | bytes 248 | tf_op jit(solution)/shard_map/psum | solution.py:131
  190.3 0.8 select_reduce_fusion.1
  192.3 0.6 compare_reduce_fusion
  193.0 0.6 select_select_fusion
  193.6 0.7 fusion.45
  194.3 0.7 fusion.47
  217.7 0.7 fusion.46
  218.4 5.0 %bitcast_add_fusion = f32[2,2,2,2,4096]{4,3,2,1,0:T(2,128)} fusion(f32[5,2,2,2,2,4096]{5,4,3,2,1,0:T(2,128)S(1)} %copy-done, f32[5,2,2,2,2,4096]{5,4,3,2,1,0:T(2,128)S(1)} %copy-done.1, f32[2,2,2,2,4096]{4,3,2,1,0:T(2,128)S(1)} %copy-done.3, f32[]{:T(128)} %bitcast.88, f32[]{:T(128)} %bitcast.86, f32[]{:T(128)} %bitcast.84, f32[]{:T(128)} %bitcast.82, ...), kind=kLoop, calls=%fused_computation.17 | loop fusion | flops 1572864 | bytes 3407896 | tf_op jit(solution)/shard_map/add | solution.py:152
  (52 shorter events, 4.2 us)
Async XLA Ops:
  0.0 20.9 %copy-start.2 = (f32[2,2,2,64,128]{4,3,2,1,0:T(8,128)S(1)}, f32[2,2,2,64,128]{4,3,2,1,0:T(8,128)}, u32[]{:S(2)}) copy-start(f32[2,2,2,64,128]{4,3,2,1,0:T(8,128)} %param.16) | copy-start | bytes 786436
  1.2 19.6 %collective-permute-start = (f32[2,2,2,64,128]{4,2,3,1,0:T(2,128)S(1)}, f32[2,2,2,64,128]{4,2,3,1,0:T(2,128)S(1)}, u32[]{:S(2)}, u32[]{:S(2)}) collective-permute-start(f32[2,2,2,64,128]{4,2,3,1,0:T(2,128)S(1)} %copy.61), channel_id=1, source_target_pairs={{0,32},{32,64},{64,96},{96,128},{128,160},{160,192},{192,224},{224... | collective-permute-start | bytes 786440 | tf_op jit(solution)/shard_map/ppermute | solution.py:21
  5.2 15.9 %collective-permute-start.1 = (f32[2,2,2,64,128]{4,2,3,1,0:T(2,128)S(1)}, f32[2,2,2,64,128]{4,2,3,1,0:T(2,128)S(1)}, u32[]{:S(2)}, u32[]{:S(2)}) collective-permute-start(f32[2,2,2,64,128]{4,2,3,1,0:T(2,128)S(1)} %copy.61), channel_id=1, source_target_pairs={{32,0},{64,32},{96,64},{128,96},{160,128},{192,160},{224,192},{256... | collective-permute-start | bytes 786440 | tf_op jit(solution)/shard_map/ppermute | solution.py:24
  25.7 13.4 %copy-start.4 = (f32[2]{0:T(128)S(1)}, f32[2]{0:T(128)}, u32[]{:S(2)}) copy-start(f32[2]{0:T(128)} %param.25) | copy-start | bytes 28
  25.8 14.0 %copy-start.5 = (f32[4]{0:T(128)S(1)}, f32[4]{0:T(128)}, u32[]{:S(2)}) copy-start(f32[4]{0:T(128)} %param.24) | copy-start | bytes 52
  25.8 14.0 %copy-start.6 = (s32[64]{0:T(128)S(1)}, s32[64]{0:T(128)}, u32[]{:S(2)}) copy-start(s32[64]{0:T(128)} %param.22) | copy-start | bytes 772
  29.5 10.4 %collective-permute-start.2 = (f32[2,2,2,64,96]{4,3,2,1,0:T(8,128)S(1)}, f32[2,2,2,64,96]{4,3,2,1,0:T(8,128)S(1)}, u32[]{:S(2)}, u32[]{:S(2)}) collective-permute-start(f32[2,2,2,64,96]{4,3,2,1,0:T(8,128)S(1)} %get-tuple-element.36), channel_id=1, source_target_pairs={{0,1},{1,2},{2,3},{3,4},{4,5},{5,6},{6,7},{7,8},{8,9},{9,10},{10,1... | collective-permute-start | bytes 589832 | tf_op jit(solution)/shard_map/ppermute | solution.py:21
  34.0 7.7 %collective-permute-start.3 = (f32[2,2,2,64,96]{4,3,2,1,0:T(8,128)S(1)}, f32[2,2,2,64,96]{4,3,2,1,0:T(8,128)S(1)}, u32[]{:S(2)}, u32[]{:S(2)}) collective-permute-start(f32[2,2,2,64,96]{4,3,2,1,0:T(8,128)S(1)} %get-tuple-element.37), channel_id=1, source_target_pairs={{1,0},{2,1},{3,2},{4,3},{5,4},{6,5},{7,6},{8,7},{9,8},{10,9},{11,1... | collective-permute-start | bytes 589832 | tf_op jit(solution)/shard_map/ppermute | solution.py:24
  42.2 19.2 %copy-start = (f32[5,2,2,2,2,4096]{5,4,3,2,1,0:T(2,128)S(1)}, f32[5,2,2,2,2,4096]{5,4,3,2,1,0:T(2,128)}, u32[]{:S(2)}) copy-start(f32[5,2,2,2,2,4096]{5,4,3,2,1,0:T(2,128)} %param.19) | copy-start | bytes 3932164
  46.1 37.2 %all-to-all-start = ((f32[2,2,2,64,128]{4,2,1,0,3:T(2,128)}), f32[2,2,2,64,128]{4,2,1,0,3:T(2,128)S(1)}, u32[]{:S(2)}, u32[]{:S(2)}) async-start(f32[2,2,2,64,128]{4,2,1,0,3:T(2,128)} %copy.69), calls=%async_computation | async-start | bytes 524288 | tf_op jit(solution)/shard_map/all_to_all | solution.py:125
  61.4 22.2 %copy-start.3 = (f32[2,2,2,2,4096]{4,3,2,1,0:T(2,128)S(1)}, f32[2,2,2,2,4096]{4,3,2,1,0:T(2,128)}, u32[]{:S(2)}) copy-start(f32[2,2,2,2,4096]{4,3,2,1,0:T(2,128)} %param.17) | copy-start | bytes 786436
  84.5 104.5 %copy-start.7 = (s32[5]{0:T(128)S(1)}, s32[5]{0:T(128)}, u32[]{:S(2)}) copy-start(s32[5]{0:T(128)} %param.20) | copy-start | bytes 64
  84.5 132.9 %copy-start.8 = (f32[6]{0:T(128)S(1)}, f32[6]{0:T(128)}, u32[]{:S(2)}) copy-start(f32[6]{0:T(128)} %constant.127.clone.1) | copy-start | bytes 76
  84.5 133.9 %copy-start.1 = (f32[5,2,2,2,2,4096]{5,4,3,2,1,0:T(2,128)S(1)}, f32[5,2,2,2,2,4096]{5,4,3,2,1,0:T(2,128)}, u32[]{:S(2)}) copy-start(f32[5,2,2,2,2,4096]{5,4,3,2,1,0:T(2,128)} %param.18) | copy-start | bytes 3932164
where the time goes:
time: 224 us; the launch traced here: 223 us
  blocking collectives  99 us (44%)
  starting transfers between devices  34.5 us (15%)
  between operations  28.3 us (13%)
  waiting for transfers between devices  18.6 us (8%)
  other arithmetic  16.3 us (7%)
  local copies, waits for them, and re-layouts  14.7 us (7%)
  matrix products  12 us (5%)
    psum x1, blocking collectives, per_device(): lax.psum((jnp.dot(history, history.T, precision=lax.Precision.HIGHEST), n...  99 us
    all_to_all x1, waiting for transfers between devices, per_device(): lax.all_to_all(sigma_slice, 'energy', split_axis=3, concat_axis=4, tiled=...  16.8 us
    all_to_all x1, starting transfers between devices, per_device(): lax.all_to_all(sigma_slice, 'energy', split_axis=3, concat_axis=4, tiled=...  15.2 us
    ppermute x2, starting transfers between devices, padded_2(): lax.ppermute(lax.slice_in_dim(block, 0, width, axis=dim), axis, backward)  10.8 us
    ppermute x2, starting transfers between devices, padded_2(): lax.ppermute(lax.slice_in_dim(block, block.shape[dim] - width, None, axis...  8.46 us
    dot_general x1, matrix products, per_device(): jnp.dot(history, history.T, precision=lax.Precision.HIGHEST)  5.16 us
    add x1, other arithmetic, per_device(): mixed + slot_weights[column] * (past_inputs[column] + mixing_share * past...  4.95 us
    dot_general x1, matrix products, per_device(): jnp.dot(history, fresh, precision=lax.Precision.HIGHEST)  4.76 us
  transfers between devices with their start and end apart: 5, of which 2 were waited for; matrix products, arithmetic and copies ran while one was open for 5% of the time, Pallas kernels for 0%

commit v1 on v0

v1 whole, which is shorter than its diff:
```python
import functools

import jax
import jax.numpy as jnp
from jax import lax
from jax.experimental import pallas as pl
from jax.experimental.pallas import tpu as pltpu
from jax.sharding import PartitionSpec as P

SHIFT_MAX = 96
HIST = 5

mixing_share = 0.5
ridge_share = 0.1

MESH = pl.DeviceIdType.MESH


def padded_2(block, sides, width, periodic):
    for axis, dim in sides:
        count = lax.axis_size(axis)
        forward = [(i, i + 1) for i in range(count - 1)]
        if periodic:
            forward.append((count - 1, 0))
        backward = [(target, source) for source, target in forward]
        low = lax.ppermute(
            lax.slice_in_dim(block, block.shape[dim] - width, None, axis=dim), axis, forward
        )
        high = lax.ppermute(lax.slice_in_dim(block, 0, width, axis=dim), axis, backward)
        block = jnp.concatenate([low, block, high], axis=dim)
    return block


def emit(padded, margin, length, coupling_row, optical, occupation, shifts):
    lesser = padded[0]
    greater = padded[1]

    def energy_view(source, offset):
        return lax.dynamic_slice_in_dim(source, margin + offset, length, axis=source.ndim - 1)

    sigma_less = coupling_row[:, None] * energy_view(lesser, 0)
    sigma_more = coupling_row[:, None] * energy_view(greater, 0)
    for column in range(2):
        strength = optical[column]
        number = occupation[column]
        offset = shifts[column]
        sigma_less = sigma_less + strength * (
            (number + 1.0) * energy_view(lesser, offset) + number * energy_view(lesser, -offset)
        )
        sigma_more = sigma_more + strength * (
            (number + 1.0) * energy_view(greater, -offset) + number * energy_view(greater, offset)
        )
    return jnp.stack([sigma_less, sigma_more])


def _pick(mask, x, axis):
    return jnp.sum(jnp.where(mask, x, 0.0), axis=axis, keepdims=True)


def _weights_from_products(prod):
    size_n = HIST
    row = lax.broadcasted_iota(jnp.int32, prod.shape, 0)
    col = lax.broadcasted_iota(jnp.int32, prod.shape, 1)
    rows, cols = prod.shape
    down = pltpu.roll(prod, rows - 1, 0)
    right = pltpu.roll(prod, cols - 1, 1)
    diag = pltpu.roll(down, cols - 1, 1)
    inside = (row < size_n) & (col < size_n)
    system = jnp.where(inside, prod - right - down + diag, 0.0)
    target = _pick((col == 0) & (row < size_n), prod - down, 1)
    eye = inside & (row == col)
    trace = jnp.sum(jnp.where(eye, system, 0.0), keepdims=True)
    ridge = ridge_share * trace / size_n + 1e-06
    a = system + jnp.where(eye, ridge, 0.0)
    lower = jnp.zeros_like(a)
    upper = jnp.zeros_like(a)
    for j in range(size_n):
        pivot = jnp.sqrt(_pick((row == j) & (col == j), a, None).reshape(1, 1))
        lcol = jnp.where(row[:, :1] >= j, _pick(col == j, a, 1) / pivot, 0.0)
        lrow = jnp.where(col[:1, :] >= j, _pick(row == j, a, 0) / pivot, 0.0)
        lower = lower + jnp.where(col == j, lcol, 0.0)
        upper = upper + jnp.where(row == j, lrow, 0.0)
        a = a - lcol * lrow
    row1 = row[:, :1]
    rest = target
    forward = jnp.zeros_like(target)
    for i in range(size_n):
        lii = _pick((row == i) & (col == i), lower, None).reshape(1, 1)
        yi = _pick(row1 == i, rest, 0) / lii
        forward = forward + jnp.where(row1 == i, yi, 0.0)
        rest = rest - jnp.where(row1 > i, _pick(col == i, lower, 1), 0.0) * yi
    rest = forward
    gamma = jnp.zeros_like(target)
    for i in range(size_n - 1, -1, -1):
        lii = _pick((row == i) & (col == i), lower, None).reshape(1, 1)
        gi = _pick(row1 == i, rest, 0) / lii
        gamma = gamma + jnp.where(row1 == i, gi, 0.0)
        rest = rest - jnp.where(row1 < i, _pick(col == i, upper, 1), 0.0) * gi
    before = pltpu.roll(gamma, 1, 0)
    weights = jnp.where(row1 == 0, 1.0, 0.0) - gamma + before
    return jnp.broadcast_to(weights, prod.shape)


def _allreduce_weights_kernel(nk, ne, entries, p_ref, w_ref, recv1, recv2, acc1, ss1, rs1, ss2, rs2):
    mk = lax.axis_index("kgrp")
    me = lax.axis_index("energy")
    barrier = pltpu.get_barrier_semaphore()
    for s in range(nk - 1):
        pl.semaphore_signal(barrier, 1, device_id=((mk + s + 1) % nk, me), device_id_type=MESH)
    for s in range(ne - 1):
        pl.semaphore_signal(barrier, 1, device_id=(mk, (me + s + 1) % ne), device_id_type=MESH)
    pl.semaphore_wait(barrier, nk - 1 + ne - 1)

    def exchange(src, recv, ssem, rsem, count, peer):
        copies = []
        for s in range(count - 1):
            c = pltpu.make_async_remote_copy(
                src_ref=src,
                dst_ref=recv.at[count - 2 - s],
                send_sem=ssem.at[s],
                recv_sem=rsem.at[count - 2 - s],
                device_id=peer(s),
                device_id_type=MESH,
            )
            c.start()
            copies.append(c)
        for s in range(count - 1):
            copies[s].wait_recv()
        for s in range(count - 1):
            copies[s].wait_send()

    def total(own, recv, mine, count):
        acc = jnp.zeros_like(own)
        for idx in range(count):
            slot = jnp.minimum((idx - mine - 1 + count) % count, count - 2)
            acc = acc + jnp.where(idx == mine, own, recv[slot])
        return acc

    exchange(p_ref, recv1, ss1, rs1, nk, lambda s: ((mk + s + 1) % nk, me))
    acc1[...] = total(p_ref[...], recv1, mk, nk)
    exchange(acc1, recv2, ss2, rs2, ne, lambda s: (mk, (me + s + 1) % ne))
    summed = total(acc1[...], recv2, me, ne)
    w_ref[...] = _weights_from_products(summed / entries)


def allreduce_weights(prod_tile, nk, ne, entries):
    return pl.pallas_call(
        functools.partial(_allreduce_weights_kernel, nk, ne, entries),
        out_shape=jax.ShapeDtypeStruct(prod_tile.shape, jnp.float32),
        in_specs=[pl.BlockSpec(memory_space=pltpu.VMEM)],
        out_specs=pl.BlockSpec(memory_space=pltpu.VMEM),
        scratch_shapes=[
            pltpu.VMEM((nk - 1,) + prod_tile.shape, jnp.float32),
            pltpu.VMEM((ne - 1,) + prod_tile.shape, jnp.float32),
            pltpu.VMEM(prod_tile.shape, jnp.float32),
            pltpu.SemaphoreType.DMA((nk - 1,)),
            pltpu.SemaphoreType.DMA((nk - 1,)),
            pltpu.SemaphoreType.DMA((ne - 1,)),
            pltpu.SemaphoreType.DMA((ne - 1,)),
        ],
        compiler_params=pltpu.CompilerParams(collective_id=0, has_side_effects=True),
    )(prod_tile)


def per_device(
    greens,
    current,
    past_inputs,
    past_residuals,
    slot_order,
    neighbour,
    momentum_class,
    stencil_weight,
    acoustic_coupling,
    optical_coupling,
    occupation,
    phonon_shift,
):
    group_len = greens.shape[3]
    rows_here = current.shape[3]
    group_id = lax.axis_index("kgrp")
    energy_id = lax.axis_index("energy")
    nk = lax.axis_size("kgrp")
    ne = lax.axis_size("energy")
    total_k = group_len * nk
    extended = padded_2(greens, (("kgrp", 3),), group_len, True)
    local_index = (neighbour - group_id * group_len + group_len) % total_k
    smeared = jnp.zeros_like(greens)
    for column in range(5):
        smeared = smeared + stencil_weight[column] * jnp.take(
            extended, local_index[:, column], axis=3
        )
    rows = lax.all_to_all(smeared, "energy", split_axis=3, concat_axis=4, tiled=True)
    classes = acoustic_coupling.shape[0]
    my_class = lax.dynamic_slice_in_dim(momentum_class, energy_id * rows_here, rows_here)
    coupling_row = jnp.sum(
        jnp.where(
            my_class[:, None] == jnp.arange(classes, dtype=jnp.int32)[None, :],
            acoustic_coupling[None, :],
            0.0,
        ),
        axis=1,
    )
    pad = [(0, 0)] * (rows.ndim - 1) + [(SHIFT_MAX, SHIFT_MAX)]
    padded = jnp.pad(rows, pad)
    sigma_new = emit(
        padded, SHIFT_MAX, rows.shape[-1], coupling_row, optical_coupling, occupation, phonon_shift
    )
    residual_now = sigma_new - current
    older_res = jnp.take(past_residuals, slot_order, axis=0)
    older_in = jnp.take(past_inputs, slot_order, axis=0)
    fresh = residual_now.reshape(1, -1)
    stacked = jnp.concatenate([fresh, older_res.reshape(HIST, -1)], axis=0)
    products = jnp.dot(stacked, stacked.T, precision=lax.Precision.HIGHEST)
    prod_tile = jnp.zeros((8, 128), jnp.float32).at[: HIST + 1, : HIST + 1].set(products)
    entries = float(fresh.shape[1] * nk * ne)
    weights = allreduce_weights(prod_tile, nk, ne, entries)[: HIST + 1, 0]
    mixed = weights[0] * (current + mixing_share * residual_now)
    for column in range(HIST):
        mixed = mixed + weights[column + 1] * (
            older_in[column] + mixing_share * older_res[column]
        )
    return mixed


def solution(mesh):
    return jax.shard_map(
        per_device,
        mesh=mesh,
        in_specs=(
            P(None, None, None, "kgrp", "energy"),
            P(None, None, None, ("kgrp", "energy"), None),
            P(None, None, None, None, ("kgrp", "energy"), None),
            P(None, None, None, None, ("kgrp", "energy"), None),
            P(),
            P("kgrp", None),
            P("kgrp"),
            P(),
            P(),
            P(),
            P(),
            P(),
        ),
        out_specs=P(None, None, None, ("kgrp", "energy"), None),
        check_vma=False,
    )
```

time: 224 us -> 127 us (0.57)
  blocking collectives: 99 us -> 0 us
  Pallas kernels: 0 us -> 28.4 us
  between operations: 28.3 us -> 5.18 us
  local copies, waits for them, and re-layouts: 14.7 us -> 24.1 us
  starting transfers between devices: 34.5 us -> 25.8 us
  other arithmetic: 16.3 us -> 21.9 us
  matrix products: 12 us -> 7.18 us
  waiting for transfers between devices: 18.6 us -> 13.9 us
    psum x1 -> x0, blocking collectives: 99 us -> none  [per_device(): lax.psum((jnp.dot(history, history.T, precision=lax.Precision.HIGHEST), n...]
    pallas_call x0 -> x1, Pallas kernels: none -> 28.4 us  [allreduce_weights(): pl.pallas_call(functools.partial(_allreduce_weights_kernel, nk, ne, entri...]
    ppermute x2 -> x1, starting transfers between devices: 8.46 us -> 1.92 us  [padded_2(): lax.ppermute(lax.slice_in_dim(block, block.shape[dim] - width, None, axis...]
    gather x0 -> x2, local copies, waits for them, and re-layouts: none -> 6.43 us  [the longest x1 3.21 us: per_device(): older_in = jnp.take(past_inputs, slot_order, axis=0)]
    dot_general x10 -> x1, matrix products: 12 us -> 7.18 us  [per_device(): products = jnp.dot(stacked, stacked.T, precision=lax.Precision.HIGHEST)]
    select_n x1 -> x2, other arithmetic: 0.65 us -> 5.43 us  [the longest x1 4.77 us: per_device(): older_in = jnp.take(past_inputs, slot_order, axis=0)]
    ppermute x2 -> x1, starting transfers between devices: 10.8 us -> 7.67 us  [padded_2(): lax.ppermute(lax.slice_in_dim(block, 0, width, axis=dim), axis, backward)]
    all_to_all x1, waiting for transfers between devices: 16.8 us -> 13.9 us  [per_device(): lax.all_to_all(smeared, 'energy', split_axis=3, concat_axis=4, tiled=True)]
  transfers between devices with their start and end apart: 5 -> 3, of which waited for: 2 -> 1; matrix products, arithmetic and copies ran while one was open for 5% -> 17% of each run, Pallas kernels for 0% -> 0%
where the time goes in v1:
time: 127 us
  Pallas kernels  28.4 us (22%)
  starting transfers between devices  25.8 us (20%)
  local copies, waits for them, and re-layouts  24.1 us (19%)
  other arithmetic  21.9 us (17%)
  waiting for transfers between devices  13.9 us (11%)
  matrix products  7.18 us (6%)
  between operations  5.18 us (4%)
    pallas_call x1, Pallas kernels, allreduce_weights(): pl.pallas_call(functools.partial(_allreduce_weights_kernel, nk, ne, entri...  28.4 us
    all_to_all x1, starting transfers between devices, per_device(): lax.all_to_all(smeared, 'energy', split_axis=3, concat_axis=4, tiled=True)  16.2 us
    all_to_all x1, waiting for transfers between devices, per_device(): lax.all_to_all(smeared, 'energy', split_axis=3, concat_axis=4, tiled=True)  13.9 us
    ppermute x1, starting transfers between devices, padded_2(): lax.ppermute(lax.slice_in_dim(block, 0, width, axis=dim), axis, backward)  7.67 us
    dot_general x1, matrix products, per_device(): products = jnp.dot(stacked, stacked.T, precision=lax.Precision.HIGHEST)  7.18 us
    add x1, other arithmetic, per_device(): mixed + weights[column + 1] * (older_in[column] + mixing_share * older_re...  7.08 us
    select_n x1, other arithmetic, per_device(): older_in = jnp.take(past_inputs, slot_order, axis=0)  4.77 us
    gather x5, local copies, waits for them, and re-layouts, per_device(): jnp.take(extended, local_index[:, column], axis=3)  4.57 us
  transfers between devices with their start and end apart: 3, of which 1 were waited for; matrix products, arithmetic and copies ran while one was open for 17% of the time, Pallas kernels for 0%

profile of v1, /device:TPU:1, one launch (start us, length us, event | category | flops | bytes accessed | tf_op | source)
XLA Modules:
  0.0 126.6 jit_solution(17077651036081461036)
XLA Ops:
  0.0 1.3 copy.18
  1.3 7.7 %collective-permute-start.1 = (f32[2,2,2,64,128]{4,2,3,1,0:T(2,128)S(1)}, f32[2,2,2,64,128]{4,2,3,1,0:T(2,128)S(1)}, u32[]{:S(2)}, u32[]{:S(2)}) collective-permute-start(f32[2,2,2,64,128]{4,2,3,1,0:T(2,128)S(1)} %copy.18), channel_id=1, source_target_pairs={{32,0},{64,32},{96,64},{128,96},{160,128},{192,160},{224,192},{256... | collective-permute-start | bytes 786440 | tf_op jit(solution)/shard_map/ppermute | solution.py:29
  8.9 1.9 %collective-permute-start = (f32[2,2,2,64,128]{4,2,3,1,0:T(2,128)S(1)}, f32[2,2,2,64,128]{4,2,3,1,0:T(2,128)}, u32[]{:S(2)}, u32[]{:S(2)}) collective-permute-start(f32[2,2,2,64,128]{4,2,3,1,0:T(2,128)S(1)} %copy.18), channel_id=1, source_target_pairs={{0,32},{32,64},{64,96},{96,128},{128,160},{160,192},{192,224},{224... | collective-permute-start | bytes 786440 | tf_op jit(solution)/shard_map/ppermute | solution.py:26
  10.9 0.7 compare_select_fusion
  11.5 1.3 %fusion.41 = (f32[1]{0:T(128)}, f32[1]{0:T(128)}) fusion(f32[2]{0:T(128)} %param.28), kind=kLoop, calls=%fused_computation.90 | loop fusion | bytes 16 | tf_op jit(solution)/shard_map/slice | solution.py:45
  12.9 1.3 %fusion.42 = (s32[1]{0:T(128)}, s32[1]{0:T(128)}) fusion(s32[2]{0:T(128)} %param.29), kind=kLoop, calls=%fused_computation.91 | loop fusion | bytes 16 | tf_op jit(solution)/shard_map/slice | solution.py:46
  14.2 1.5 %fusion.43 = (f32[1]{0:T(128)}, f32[1]{0:T(128)}, f32[1]{0:T(128)}, f32[1]{0:T(128)}, f32[1]{0:T(128)}) fusion(f32[5]{0:T(128)} %param.25), kind=kLoop, calls=%fused_computation.92 | loop fusion | bytes 40 | tf_op jit(solution)/shard_map/slice | solution.py:190
  15.7 0.7 add_select_fusion
  21.4 3.2 %gather_fusion.6 = f32[5,2,2,2,2,4096]{5,4,3,2,1,0:T(2,128)} fusion(f32[5,2,2,2,2,4096]{5,4,3,2,1,0:T(2,128)S(1)} %copy-done, s32[1024]{0:T(1024)S(1)} %pad_clamp_fusion), kind=kCustom, calls=%fused_computation.6.clone | custom fusion | bytes 2621460 | tf_op jit(solution)/shard_map/jit(_take)/gather | solution.py:211
  24.6 3.2 %gather_fusion.5 = f32[5,2,2,2,2,4096]{5,4,3,2,1,0:T(2,128)} fusion(f32[5,2,2,2,2,4096]{5,4,3,2,1,0:T(2,128)S(1)} %copy-done.1, s32[1024]{0:T(1024)S(1)} %pad_clamp_fusion), kind=kCustom, calls=%fused_computation.1.clone | custom fusion | bytes 2621460 | tf_op jit(solution)/shard_map/jit(_take)/gather | solution.py:210
  27.9 1.0 constant_dynamic-update-slice_fusion.2
  28.9 0.2 constant_dynamic-update-slice_fusion.1
  29.1 0.9 gather_fusion.4
  30.1 0.9 gather_fusion.3
  31.0 0.9 gather_fusion.2
  31.9 0.9 gather_fusion.1
  32.8 0.9 gather_fusion
  33.7 4.6 %fusion.24 = f32[2,2,2,64,128]{4,2,1,0,3:T(2,128)} fusion(f32[64,2,2,2,128]{4,3,2,1,0:T(2,128)S(1)} %gather_fusion.4, f32[64,2,2,2,128]{4,3,2,1,0:T(2,128)S(1)} %gather_fusion.3, f32[64,2,2,2,128]{4,3,2,1,0:T(2,128)S(1)} %gather_fusion.2, f32[64,2,2,2,128]{4,3,2,1,0:T(2,128)S(1)} %gather_fusion.1, f32[64,2,2,2,128]{4,3,2,1,0:T(2,128)S(1)} %gather_fusion, ...), kind=kLoop, calls=%fused_computation.40 | loop fusion | flops 917504 | bytes 1573204 | tf_op jit(solution)/shard_map/add | solution.py:190
  38.3 16.2 %all-to-all-start = ((f32[2,2,2,64,128]{4,2,1,0,3:T(2,128)}), f32[2,2,2,64,128]{4,2,1,0,3:T(2,128)S(1)}, u32[]{:S(2)}, u32[]{:S(2)}) async-start(f32[2,2,2,64,128]{4,2,1,0,3:T(2,128)} %fusion.24), calls=%async_computation | async-start | bytes 524288 | tf_op jit(solution)/shard_map/all_to_all | solution.py:193
  54.5 4.8 %broadcast_select_fusion = (f32[5,2,2,2,2,4096]{5,4,3,2,1,0:T(2,128)}, f32[5,2,2,2,2,4096]{5,4,3,2,1,0:T(2,128)S(1)}) fusion(f32[5,2,2,2,2,4096]{5,4,3,2,1,0:T(2,128)} %gather_fusion.6, pred[5]{0:T(512)(128)(4,1)S(1)} %compare_and_fusion, f32[5,2,2,2,2,4096]{5,4,3,2,1,0:T(2,128)} %gather_fusion.5), kind=kLoop, calls=%fused_computation.11 | loop fusion | flops 655360 | bytes 5242885 | tf_op jit(solution)/shard_map/jit(_take)/select_n | solution.py:211
  59.3 2.5 %reshape.142 = f32[5,65536]{1,0:T(8,128)} reshape(f32[5,2,2,2,2,4096]{5,4,3,2,1,0:T(2,128)S(1)} %get-tuple-element.61) | data formatting | bytes 2621440 | tf_op jit(solution)/shard_map/reshape | solution.py:213
  61.8 0.6 fusion.40
  62.4 0.2 fusion.35
  62.6 13.9 %all-to-all-done = f32[2,2,2,64,128]{4,2,1,0,3:T(2,128)S(1)} async-done(((f32[2,2,2,64,128]{4,2,1,0,3:T(2,128)}), f32[2,2,2,64,128]{4,2,1,0,3:T(2,128)S(1)}, u32[]{:S(2)}, u32[]{:S(2)}) %all-to-all-start) | async-done | bytes 262176 | tf_op jit(solution)/shard_map/all_to_all | solution.py:193
  76.7 0.6 pad_slice_fusion.1
  77.4 3.8 %fusion.33 = (f32[1,2,2,2,4096]{4,3,2,1,0:T(2,128)S(1)}, f32[1,2,2,2,4096]{4,3,2,1,0:T(2,128)S(1)}) fusion(f32[2,2,2,4288]{3,2,1,0:T(2,128)S(1)} %get-tuple-element.31, f32[1,2,2,2,4288]{4,3,2,1,0:T(2,128)S(1)} %get-tuple-element.29, s32[]{:T(128)S(6)} %select_n.50, s32[]{:T(128)S(6)} %select_n.49, s32[]{:T(128)S(6)} %select_n.48, s32[]{:T(128)S(6)} %select_n.47, ...), kind=kLoop, calls=%fused_computation.57 | loop fusion | flops 720896 | bytes 1572912 | tf_op jit(solution)/shard_map/stack | solution.py:53
  81.3 0.4 reshape.141
  81.8 7.2 %fusion = f32[6,6]{1,0:T(8,128)S(1)} fusion(f32[5,65536]{1,0:T(8,128)} %reshape.142, f32[1,65536]{1,0:T(1,128)S(1)} %reshape.141), kind=kOutput, calls=%fused_computation.7 | convolution fusion | flops 28704768 | bytes 1573008 | tf_op jit(solution)/shard_map/dot_general | solution.py:214
  88.9 0.6 scatter.4.p_ref
  89.6 28.4 %shard_map.118 = f32[8,128]{1,0:T(8,128)} custom-call(f32[8,128]{1,0:T(8,128)} %scatter.4.p_ref), custom_call_target="tpu_custom_call" | custom-call | tf_op jit(solution)/shard_map/pallas_call | solution.py:147
  118.0 1.5 %fusion.39 = (f32[1,1]{1,0:T(1,128)}, f32[1,1]{1,0:T(1,128)}, f32[1,1]{1,0:T(1,128)}, f32[1,1]{1,0:T(1,128)}, f32[1,1]{1,0:T(1,128)}, /*index=5*/f32[1,1]{1,0:T(1,128)}) fusion(f32[8,128]{1,0:T(8,128)} %shard_map.118), kind=kLoop, calls=%fused_computation.88 | loop fusion | bytes 48 | tf_op jit(solution)/shard_map/slice | solution.py:218
  119.5 7.1 %fusion.7 = f32[2,2,2,2,4096]{4,3,2,1,0:T(2,128)} fusion(f32[5,2,2,2,2,4096]{5,4,3,2,1,0:T(2,128)S(1)} %get-tuple-element.61, f32[5,2,2,2,2,4096]{5,4,3,2,1,0:T(2,128)} %get-tuple-element.60, f32[2,2,2,2,4096]{4,3,2,1,0:T(2,128)S(1)} %copy-done.4, f32[]{:T(128)} %bitcast.46, f32[]{:T(128)} %bitcast.44, f32[]{:T(128)} %bitcast.42, f32[]{:T(128)} %bitcast.40, ...), kind=kLoop, calls=%fused_computation.17 | loop fusion | flops 1638400 | bytes 3407896 | tf_op jit(solution)/shard_map/add | solution.py:220
  (31 shorter events, 0.6 us)
Async XLA Ops:
  0.0 21.4 %copy-start = (f32[5,2,2,2,2,4096]{5,4,3,2,1,0:T(2,128)S(1)}, f32[5,2,2,2,2,4096]{5,4,3,2,1,0:T(2,128)}, u32[]{:S(2)}) copy-start(f32[5,2,2,2,2,4096]{5,4,3,2,1,0:T(2,128)} %param.20) | copy-start | bytes 3932164
  1.3 27.8 %collective-permute-start.1 = (f32[2,2,2,64,128]{4,2,3,1,0:T(2,128)S(1)}, f32[2,2,2,64,128]{4,2,3,1,0:T(2,128)S(1)}, u32[]{:S(2)}, u32[]{:S(2)}) collective-permute-start(f32[2,2,2,64,128]{4,2,3,1,0:T(2,128)S(1)} %copy.18), channel_id=1, source_target_pairs={{32,0},{64,32},{96,64},{128,96},{160,128},{192,160},{224,192},{256... | collective-permute-start | bytes 786440 | tf_op jit(solution)/shard_map/ppermute | solution.py:29
  8.9 18.9 %collective-permute-start = (f32[2,2,2,64,128]{4,2,3,1,0:T(2,128)S(1)}, f32[2,2,2,64,128]{4,2,3,1,0:T(2,128)}, u32[]{:S(2)}, u32[]{:S(2)}) collective-permute-start(f32[2,2,2,64,128]{4,2,3,1,0:T(2,128)S(1)} %copy.18), channel_id=1, source_target_pairs={{0,32},{32,64},{64,96},{96,128},{128,160},{160,192},{192,224},{224... | collective-permute-start | bytes 786440 | tf_op jit(solution)/shard_map/ppermute | solution.py:26
  21.4 3.2 %copy-start.1 = (f32[5,2,2,2,2,4096]{5,4,3,2,1,0:T(2,128)S(1)}, f32[5,2,2,2,2,4096]{5,4,3,2,1,0:T(2,128)}, u32[]{:S(2)}) copy-start(f32[5,2,2,2,2,4096]{5,4,3,2,1,0:T(2,128)} %param.21) | copy-start | bytes 3932164
  24.6 3.2 %copy-start.6 = (s32[5]{0:T(128)S(1)}, s32[5]{0:T(128)}, u32[]{:S(2)}) copy-start(s32[5]{0:T(128)} %param.22) | copy-start | bytes 64
  24.6 4.2 %copy-start.2 = (f32[2,2,2,64,128]{4,3,2,1,0:T(8,128)S(1)}, f32[2,2,2,64,128]{4,3,2,1,0:T(8,128)}, u32[]{:S(2)}) copy-start(f32[2,2,2,64,128]{4,3,2,1,0:T(8,128)} %param.18) | copy-start | bytes 786436
  38.3 38.2 %all-to-all-start = ((f32[2,2,2,64,128]{4,2,1,0,3:T(2,128)}), f32[2,2,2,64,128]{4,2,1,0,3:T(2,128)S(1)}, u32[]{:S(2)}, u32[]{:S(2)}) async-start(f32[2,2,2,64,128]{4,2,1,0,3:T(2,128)} %fusion.24), calls=%async_computation | async-start | bytes 524288 | tf_op jit(solution)/shard_map/all_to_all | solution.py:193
  59.3 2.5 %copy-start.7 = (s32[64]{0:T(128)S(1)}, s32[64]{0:T(128)}, u32[]{:S(2)}) copy-start(s32[64]{0:T(128)} %param.24) | copy-start | bytes 772
  59.3 2.5 %copy-start.5 = (f32[2]{0:T(128)S(1)}, f32[2]{0:T(128)}, u32[]{:S(2)}) copy-start(f32[2]{0:T(128)} %param.27) | copy-start | bytes 28
  59.3 3.1 %copy-start.8 = (f32[4]{0:T(128)S(1)}, f32[4]{0:T(128)}, u32[]{:S(2)}) copy-start(f32[4]{0:T(128)} %param.26) | copy-start | bytes 52
  76.7 4.4 %copy-start.3 = (f32[2,2,2,2,4096]{4,3,2,1,0:T(2,128)S(1)}, f32[2,2,2,2,4096]{4,3,2,1,0:T(2,128)}, u32[]{:S(2)}) copy-start(f32[2,2,2,2,4096]{4,3,2,1,0:T(2,128)} %param.19) | copy-start | bytes 786436
  81.7 37.8 %copy-start.4 = (f32[2,2,2,2,4096]{4,3,2,1,0:T(2,128)S(1)}, f32[2,2,2,2,4096]{4,3,2,1,0:T(2,128)}, u32[]{:S(2)}) copy-start(f32[2,2,2,2,4096]{4,3,2,1,0:T(2,128)} %param.19) | copy-start | bytes 786436

commit v2 on v1

--- a/solution.py
+++ b/solution.py
@@ -101,7 +101,26 @@
     return jnp.broadcast_to(weights, prod.shape)
 
 
-def _allreduce_weights_kernel(nk, ne, entries, p_ref, w_ref, recv1, recv2, acc1, ss1, rs1, ss2, rs2):
+def _permute_square(prod, perm):
+    row = lax.broadcasted_iota(jnp.int32, prod.shape, 0)
+    col = lax.broadcasted_iota(jnp.int32, prod.shape, 1)
+    count = len(perm)
+    permcol = jnp.zeros((prod.shape[0], 1), jnp.int32)
+    permrow = jnp.zeros((1, prod.shape[1]), jnp.int32)
+    for i in range(count):
+        permcol = jnp.where(row[:, :1] == i, perm[i], permcol)
+        permrow = jnp.where(col[:1, :] == i, perm[i], permrow)
+    by_rows = jnp.zeros_like(prod)
+    for m in range(count):
+        by_rows = by_rows + jnp.where(permcol == m, _pick(row == m, prod, 0), 0.0)
+    by_rows = jnp.where(row < count, by_rows, 0.0)
+    both = jnp.zeros_like(prod)
+    for m in range(count):
+        both = both + jnp.where(permrow == m, _pick(col == m, by_rows, 1), 0.0)
+    return jnp.where(col < count, both, 0.0)
+
+
+def _allreduce_weights_kernel(nk, ne, entries, slot_ref, p_ref, w_ref, recv1, recv2, acc1, ss1, rs1, ss2, rs2):
     mk = lax.axis_index("kgrp")
     me = lax.axis_index("energy")
     barrier = pltpu.get_barrier_semaphore()
@@ -140,14 +159,24 @@
     acc1[...] = total(p_ref[...], recv1, mk, nk)
     exchange(acc1, recv2, ss2, rs2, ne, lambda s: (mk, (me + s + 1) % ne))
     summed = total(acc1[...], recv2, me, ne)
-    w_ref[...] = _weights_from_products(summed / entries)
-
-
-def allreduce_weights(prod_tile, nk, ne, entries):
+    perm = [0] + [slot_ref[i] + 1 for i in range(HIST)]
+    aged = _permute_square(summed / entries, perm)
+    weights = _weights_from_products(aged)[:, :1]
+    row1 = lax.broadcasted_iota(jnp.int32, weights.shape, 0)
+    by_slot = jnp.zeros_like(weights)
+    for i in range(HIST + 1):
+        by_slot = by_slot + jnp.where(row1 == perm[i], _pick(row1 == i, weights, 0), 0.0)
+    w_ref[...] = jnp.broadcast_to(by_slot, w_ref.shape)
+
+
+def allreduce_weights(slot_order, prod_tile, nk, ne, entries):
     return pl.pallas_call(
         functools.partial(_allreduce_weights_kernel, nk, ne, entries),
         out_shape=jax.ShapeDtypeStruct(prod_tile.shape, jnp.float32),
-        in_specs=[pl.BlockSpec(memory_space=pltpu.VMEM)],
+        in_specs=[
+            pl.BlockSpec(memory_space=pltpu.SMEM),
+            pl.BlockSpec(memory_space=pltpu.VMEM),
+        ],
         out_specs=pl.BlockSpec(memory_space=pltpu.VMEM),
         scratch_shapes=[
             pltpu.VMEM((nk - 1,) + prod_tile.shape, jnp.float32),
@@ -159,7 +188,7 @@
             pltpu.SemaphoreType.DMA((ne - 1,)),
         ],
         compiler_params=pltpu.CompilerParams(collective_id=0, has_side_effects=True),
-    )(prod_tile)
+    )(slot_order, prod_tile)
 
 
 def per_device(
@@ -183,13 +212,29 @@
     nk = lax.axis_size("kgrp")
     ne = lax.axis_size("energy")
     total_k = group_len * nk
-    extended = padded_2(greens, (("kgrp", 3),), group_len, True)
+    ends = padded_2(greens, (("kgrp", 3),), group_len, True)
+    low = ends[:, :, :, :group_len]
+    high = ends[:, :, :, 2 * group_len :]
     local_index = (neighbour - group_id * group_len + group_len) % total_k
-    smeared = jnp.zeros_like(greens)
-    for column in range(5):
-        smeared = smeared + stencil_weight[column] * jnp.take(
-            extended, local_index[:, column], axis=3
-        )
+    stencil = jnp.sum(
+        jnp.where(
+            local_index[:, :, None] == jnp.arange(3 * group_len, dtype=jnp.int32)[None, None, :],
+            stencil_weight[None, :, None],
+            0.0,
+        ),
+        axis=1,
+    )
+    lead = greens.shape[:3]
+    flat = lambda x: x.reshape((-1,) + x.shape[3:])
+    smeared = jnp.zeros_like(flat(greens))
+    for part, block in enumerate((low, greens, high)):
+        smeared = smeared + jnp.einsum(
+            "kr,bre->bke",
+            stencil[:, part * group_len : (part + 1) * group_len],
+            flat(block),
+            precision=lax.Precision.HIGHEST,
+        )
+    smeared = smeared.reshape(lead + smeared.shape[1:])
     rows = lax.all_to_all(smeared, "energy", split_axis=3, concat_axis=4, tiled=True)
     classes = acoustic_coupling.shape[0]
     my_class = lax.dynamic_slice_in_dim(momentum_class, energy_id * rows_here, rows_here)
@@ -207,18 +252,19 @@
         padded, SHIFT_MAX, rows.shape[-1], coupling_row, optical_coupling, occupation, phonon_shift
     )
     residual_now = sigma_new - current
-    older_res = jnp.take(past_residuals, slot_order, axis=0)
-    older_in = jnp.take(past_inputs, slot_order, axis=0)
-    fresh = residual_now.reshape(1, -1)
-    stacked = jnp.concatenate([fresh, older_res.reshape(HIST, -1)], axis=0)
-    products = jnp.dot(stacked, stacked.T, precision=lax.Precision.HIGHEST)
-    prod_tile = jnp.zeros((8, 128), jnp.float32).at[: HIST + 1, : HIST + 1].set(products)
-    entries = float(fresh.shape[1] * nk * ne)
-    weights = allreduce_weights(prod_tile, nk, ne, entries)[: HIST + 1, 0]
+    data_axes = tuple(range(1, past_residuals.ndim))
+    old_gram = jnp.sum(past_residuals[:, None] * past_residuals[None, :], axis=tuple(a + 1 for a in data_axes))
+    cross = jnp.sum(residual_now[None] * past_residuals, axis=data_axes)
+    self_term = jnp.sum(residual_now * residual_now)
+    top = jnp.concatenate([self_term[None], cross])
+    products = jnp.concatenate([top[None, :], jnp.concatenate([cross[:, None], old_gram], axis=1)], axis=0)
+    prod_tile = jnp.pad(products, ((0, 8 - HIST - 1), (0, 128 - HIST - 1)))
+    entries = float(residual_now.size * nk * ne)
+    weights = allreduce_weights(slot_order, prod_tile, nk, ne, entries)[: HIST + 1, 0]
     mixed = weights[0] * (current + mixing_share * residual_now)
     for column in range(HIST):
         mixed = mixed + weights[column + 1] * (
-            older_in[column] + mixing_share * older_res[column]
+            past_inputs[column] + mixing_share * past_residuals[column]
         )
     return mixed
 

time: 127 us -> 99.4 us (0.78)
  local copies, waits for them, and re-layouts: 24.1 us -> 5.23 us
  Pallas kernels: 28.4 us -> 23.2 us
  matrix products: 7.18 us -> 2.07 us
  waiting for transfers between devices: 13.9 us -> 18.6 us
  other arithmetic: 21.9 us -> 17.6 us
    gather x7 -> x0, local copies, waits for them, and re-layouts: 11 us -> none  [the longest x5 4.57 us: per_device(): jnp.take(extended, local_index[:, column], axis=3)]
    ppermute x1, waiting for transfers between devices: 0.01 us -> 6.64 us  [padded_2(): lax.ppermute(lax.slice_in_dim(block, block.shape[dim] - width, None, axis...]
    add x2 -> x1, other arithmetic: 11.6 us -> 5.74 us  [per_device(): mixed + weights[column + 1] * (past_inputs[column] + mixing_share * past_...]
    reduce_sum x0 -> x4, other arithmetic: none -> 5.69 us  [the longest x1 3.22 us: per_device(): jnp.sum(past_residuals[:, None] * past_residuals[None, :], axis=tuple((a...]
    select_n x2 -> x0, other arithmetic: 5.43 us -> none  [the longest x1 4.77 us: per_device(): older_in = jnp.take(past_inputs, slot_order, axis=0)]
    pallas_call x1, Pallas kernels: 28.4 us -> 23.2 us  [allreduce_weights(): pl.pallas_call(functools.partial(_allreduce_weights_kernel, nk, ne, entri...]
    dot_general x1 -> x3, matrix products: 7.18 us -> 2.07 us  [per_device(): jnp.einsum('kr,bre->bke', stencil[:, part * group_len:(part + 1) * group_...]
    unnamed x21 -> x16, local copies, waits for them, and re-layouts: 2.49 us -> 0.04 us
  transfers between devices with their start and end apart: 3 -> 3, of which waited for: 1 -> 3; matrix products, arithmetic and copies ran while one was open for 17% -> 9% of each run, Pallas kernels for 0% -> 0%
where the time goes in v2:
time: 99.4 us; the launch traced here: 98.7 us
  starting transfers between devices  26.9 us (27%)
  Pallas kernels  23.2 us (23%)
  waiting for transfers between devices  18.6 us (19%)
  other arithmetic  17.6 us (18%)
  local copies, waits for them, and re-layouts  5.23 us (5%)
  between operations  5.22 us (5%)
  matrix products  2.07 us (2%)
    pallas_call x1, Pallas kernels, allreduce_weights(): pl.pallas_call(functools.partial(_allreduce_weights_kernel, nk, ne, entri...  23.2 us
    all_to_all x1, starting transfers between devices, per_device(): lax.all_to_all(smeared, 'energy', split_axis=3, concat_axis=4, tiled=True)  17.3 us
    all_to_all x1, waiting for transfers between devices, per_device(): lax.all_to_all(smeared, 'energy', split_axis=3, concat_axis=4, tiled=True)  11.7 us
    ppermute x1, starting transfers between devices, padded_2(): lax.ppermute(lax.slice_in_dim(block, 0, width, axis=dim), axis, backward)  7.66 us
    ppermute x1, waiting for transfers between devices, padded_2(): lax.ppermute(lax.slice_in_dim(block, block.shape[dim] - width, None, axis...  6.64 us
    add x1, other arithmetic, per_device(): mixed + weights[column + 1] * (past_inputs[column] + mixing_share * past_...  5.74 us
    another operation x1, other arithmetic, emit(): return jnp.stack([sigma_less, sigma_more])  3.85 us
    reduce_sum x1, other arithmetic, per_device(): jnp.sum(past_residuals[:, None] * past_residuals[None, :], axis=tuple((a...  3.22 us
  transfers between devices with their start and end apart: 3, of which 3 were waited for; matrix products, arithmetic and copies ran while one was open for 9% of the time, Pallas kernels for 0%

profile of v2, /device:TPU:1, one launch (start us, length us, event | category | flops | bytes accessed | tf_op | source)
XLA Modules:
  0.0 98.7 jit_solution(17655933613395078060)
XLA Ops:
  0.0 7.7 %collective-permute-start.1 = (f32[2,2,2,64,128]{4,3,2,1,0:T(8,128)}, f32[2,2,2,64,128]{4,3,2,1,0:T(8,128)S(1)}, u32[]{:S(2)}, u32[]{:S(2)}) collective-permute-start(f32[2,2,2,64,128]{4,3,2,1,0:T(8,128)} %param.12), channel_id=1, source_target_pairs={{32,0},{64,32},{96,64},{128,96},{160,128},{192,160},{224,192},{256... | collective-permute-start | bytes 786440 | tf_op jit(solution)/shard_map/ppermute | solution.py:29
  7.7 1.9 %collective-permute-start = (f32[2,2,2,64,128]{4,3,2,1,0:T(8,128)}, f32[2,2,2,64,128]{4,3,2,1,0:T(8,128)S(1)}, u32[]{:S(2)}, u32[]{:S(2)}) collective-permute-start(f32[2,2,2,64,128]{4,3,2,1,0:T(8,128)} %param.12), channel_id=1, source_target_pairs={{0,32},{32,64},{64,96},{96,128},{128,160},{160,192},{192,224},{224... | collective-permute-start | bytes 786440 | tf_op jit(solution)/shard_map/ppermute | solution.py:26
  9.6 0.7 add_select_fusion
  10.3 0.8 select_reduce_fusion
  11.1 1.4 %fusion.8 = f32[64,8,128]{2,0,1:T(8,128)S(1)} fusion(f32[8,64,128]{2,1,0:T(8,128)} %bitcast.81, f32[64,192]{1,0:T(8,128)S(1)} %select_reduce_fusion), kind=kOutput, calls=%fused_computation.26 | convolution fusion | flops 50331648 | bytes 557056 | tf_op jit(solution)/shard_map/kr,bre->bke/dot_general | solution.py:231
  12.5 0.3 collective-permute-done.1
  12.7 0.0 copy-start
  12.8 0.4 fusion.7
  13.1 6.6 %collective-permute-done = f32[2,2,2,64,128]{4,3,2,1,0:T(8,128)S(1)} collective-permute-done((f32[2,2,2,64,128]{4,3,2,1,0:T(8,128)}, f32[2,2,2,64,128]{4,3,2,1,0:T(8,128)S(1)}, u32[]{:S(2)}, u32[]{:S(2)}) %collective-permute-start) | collective-permute-done | bytes 262176 | tf_op jit(solution)/shard_map/ppermute | solution.py:26
  19.8 0.4 fusion
  20.1 0.9 copy.20
  21.0 17.3 %all-to-all-start = ((f32[2,2,2,64,128]{4,2,1,0,3:T(2,128)}), f32[2,2,2,64,128]{4,2,1,0,3:T(2,128)S(1)}, u32[]{:S(2)}, u32[]{:S(2)}) async-start(f32[2,2,2,64,128]{4,2,1,0,3:T(2,128)} %copy.20), calls=%async_computation | async-start | bytes 524288 | tf_op jit(solution)/shard_map/all_to_all | solution.py:238
  38.3 0.6 fusion.22
  42.7 0.6 fusion.21
  44.6 0.1 dynamic_slice.33
  44.7 0.6 fusion.20
  45.3 0.2 fusion.16
  45.5 3.2 %multiply_reduce_fusion = f32[5,5]{1,0:T(8,128)S(1)} fusion(f32[5,2,2,2,2,4096]{5,4,3,2,1,0:T(2,128)S(1)} %copy-done), kind=kLoop, calls=%fused_computation | loop fusion | flops 3276775 | bytes 1310820 | tf_op jit(solution)/shard_map/reduce_sum | solution.py:256
  48.7 11.7 %all-to-all-done = f32[2,2,2,64,128]{4,2,1,0,3:T(2,128)S(1)} async-done(((f32[2,2,2,64,128]{4,2,1,0,3:T(2,128)}), f32[2,2,2,64,128]{4,2,1,0,3:T(2,128)S(1)}, u32[]{:S(2)}, u32[]{:S(2)}) %all-to-all-start) | async-done | bytes 262176 | tf_op jit(solution)/shard_map/all_to_all | solution.py:238
  60.3 0.1 copy.21
  60.4 0.1 all_to_all.16
  60.6 0.0 copy-start.2
  60.6 0.6 pad_slice_fusion.1
  61.2 3.9 %fusion.6 = (f32[1,2,2,2,4096]{4,3,2,1,0:T(2,128)S(1)}, f32[1,2,2,2,4096]{4,3,2,1,0:T(2,128)S(1)}) fusion(f32[2,2,2,4288]{3,2,1,0:T(2,128)S(1)} %get-tuple-element.9, f32[1,2,2,2,4288]{4,3,2,1,0:T(2,128)S(1)} %get-tuple-element.7, s32[]{:T(128)S(6)} %select_n.41, s32[]{:T(128)S(6)} %select_n.40, s32[]{:T(128)S(6)} %select_n.39, s32[]{:T(128)S(6)} %select_n.38, ...), kind=kLoop, calls=%fused_computation.22 | loop fusion | flops 720896 | bytes 1572912 | tf_op jit(solution)/shard_map/stack | solution.py:53
  65.1 0.9 multiply_reduce_fusion.2
  66.0 0.8 multiply_reduce_fusion.1
  66.8 0.7 maximum_bitcast_fusion
  67.5 0.1 copy.22
  67.6 0.7 select_maximum_fusion.p_ref
  68.3 23.2 %shard_map.118 = f32[8,128]{1,0:T(8,128)} custom-call(s32[5]{0:T(128)} %slot_ref.1, f32[8,128]{1,0:T(8,128)} %select_maximum_fusion.p_ref), custom_call_target="tpu_custom_call" | custom-call | tf_op jit(solution)/shard_map/pallas_call | solution.py:173
  91.5 1.5 %fusion.19 = (f32[1,1]{1,0:T(1,128)}, f32[1,1]{1,0:T(1,128)}, f32[1,1]{1,0:T(1,128)}, f32[1,1]{1,0:T(1,128)}, f32[1,1]{1,0:T(1,128)}, /*index=5*/f32[1,1]{1,0:T(1,128)}) fusion(f32[8,128]{1,0:T(8,128)} %shard_map.118), kind=kLoop, calls=%fused_computation.46 | loop fusion | bytes 48 | tf_op jit(solution)/shard_map/slice | solution.py:264
  93.0 5.7 %bitcast_add_fusion = f32[2,2,2,2,4096]{4,3,2,1,0:T(2,128)} fusion(f32[5,2,2,2,2,4096]{5,4,3,2,1,0:T(2,128)S(1)} %copy-done, f32[5,2,2,2,2,4096]{5,4,3,2,1,0:T(2,128)S(1)} %copy-done.1, f32[2,2,2,2,4096]{4,3,2,1,0:T(2,128)S(1)} %copy-done.2, f32[2,2,2,2,4096]{4,3,2,1,0:T(2,128)S(1)} %get-tuple-element.6, f32[]{:T(128)} %bitcast.42, f32[]{:T(128)} %bitcast.40, ...), kind=kLoop, calls=%fused_computation.7 | loop fusion | flops 1507328 | bytes 3407896 | tf_op jit(solution)/shard_map/add | solution.py:266
  (14 shorter events, 0.0 us)
Async XLA Ops:
  0.0 12.7 %collective-permute-start.1 = (f32[2,2,2,64,128]{4,3,2,1,0:T(8,128)}, f32[2,2,2,64,128]{4,3,2,1,0:T(8,128)S(1)}, u32[]{:S(2)}, u32[]{:S(2)}) collective-permute-start(f32[2,2,2,64,128]{4,3,2,1,0:T(8,128)} %param.12), channel_id=1, source_target_pairs={{32,0},{64,32},{96,64},{128,96},{160,128},{192,160},{224,192},{256... | collective-permute-start | bytes 786440 | tf_op jit(solution)/shard_map/ppermute | solution.py:29
  7.7 12.1 %collective-permute-start = (f32[2,2,2,64,128]{4,3,2,1,0:T(8,128)}, f32[2,2,2,64,128]{4,3,2,1,0:T(8,128)S(1)}, u32[]{:S(2)}, u32[]{:S(2)}) collective-permute-start(f32[2,2,2,64,128]{4,3,2,1,0:T(8,128)} %param.12), channel_id=1, source_target_pairs={{0,32},{32,64},{64,96},{96,128},{128,160},{160,192},{192,224},{224... | collective-permute-start | bytes 786440 | tf_op jit(solution)/shard_map/ppermute | solution.py:26
  12.7 25.6 %copy-start.3 = (s32[2]{0:T(128)S(1)}, s32[2]{0:T(128)}, u32[]{:S(2)}) copy-start(s32[2]{0:T(128)} %param.23) | copy-start | bytes 28
  12.7 30.0 %copy-start.4 = (f32[2]{0:T(128)S(1)}, f32[2]{0:T(128)}, u32[]{:S(2)}) copy-start(f32[2]{0:T(128)} %param.22) | copy-start | bytes 28
  12.7 31.9 %copy-start.6 = (s32[64]{0:T(128)S(1)}, s32[64]{0:T(128)}, u32[]{:S(2)}) copy-start(s32[64]{0:T(128)} %param.18) | copy-start | bytes 772
  12.7 32.0 %copy-start.5 = (f32[2]{0:T(128)S(1)}, f32[2]{0:T(128)}, u32[]{:S(2)}) copy-start(f32[2]{0:T(128)} %param.21) | copy-start | bytes 28
  12.7 32.5 %copy-start.7 = (f32[4]{0:T(128)S(1)}, f32[4]{0:T(128)}, u32[]{:S(2)}) copy-start(f32[4]{0:T(128)} %param.20) | copy-start | bytes 52
  12.7 32.7 %copy-start = (f32[5,2,2,2,2,4096]{5,4,3,2,1,0:T(2,128)S(1)}, f32[5,2,2,2,2,4096]{5,4,3,2,1,0:T(2,128)}, u32[]{:S(2)}) copy-start(f32[5,2,2,2,2,4096]{5,4,3,2,1,0:T(2,128)} %param.15) | copy-start | bytes 3932164
  21.0 39.3 %all-to-all-start = ((f32[2,2,2,64,128]{4,2,1,0,3:T(2,128)}), f32[2,2,2,64,128]{4,2,1,0,3:T(2,128)S(1)}, u32[]{:S(2)}, u32[]{:S(2)}) async-start(f32[2,2,2,64,128]{4,2,1,0,3:T(2,128)} %copy.20), calls=%async_computation | async-start | bytes 524288 | tf_op jit(solution)/shard_map/all_to_all | solution.py:238
  60.6 4.5 %copy-start.2 = (f32[2,2,2,2,4096]{4,3,2,1,0:T(2,128)S(1)}, f32[2,2,2,2,4096]{4,3,2,1,0:T(2,128)}, u32[]{:S(2)}) copy-start(f32[2,2,2,2,4096]{4,3,2,1,0:T(2,128)} %param.13) | copy-start | bytes 786436
  65.1 27.9 %copy-start.1 = (f32[5,2,2,2,2,4096]{5,4,3,2,1,0:T(2,128)S(1)}, f32[5,2,2,2,2,4096]{5,4,3,2,1,0:T(2,128)}, u32[]{:S(2)}) copy-start(f32[5,2,2,2,2,4096]{5,4,3,2,1,0:T(2,128)} %param.14) | copy-start | bytes 3932164

commit v3 on v2

--- a/solution.py
+++ b/solution.py
@@ -169,6 +169,57 @@
     w_ref[...] = jnp.broadcast_to(by_slot, w_ref.shape)
 
 
+def _transpose_kernel(ne, x_ref, y_ref, ssem, rsem):
+    mk = lax.axis_index("kgrp")
+    me = lax.axis_index("energy")
+    width = x_ref.shape[-1]
+    barrier = pltpu.get_barrier_semaphore()
+    for s in range(ne - 1):
+        pl.semaphore_signal(barrier, 1, device_id=(mk, (me + s + 1) % ne), device_id_type=MESH)
+    pl.semaphore_wait(barrier, ne - 1)
+    copies = []
+    for s in range(ne - 1):
+        peer = (me + s + 1) % ne
+        c = pltpu.make_async_remote_copy(
+            src_ref=x_ref.at[peer],
+            dst_ref=y_ref.at[:, pl.ds(pl.multiple_of(me * width, width), width)],
+            send_sem=ssem.at[s],
+            recv_sem=rsem.at[ne - 2 - s],
+            device_id=(mk, peer),
+            device_id_type=MESH,
+        )
+        c.start()
+        copies.append(c)
+    y_ref[:, pl.ds(pl.multiple_of(me * width, width), width)] = x_ref[me]
+    for q in range(ne - 1):
+        source = (me + q + 1) % ne
+        pltpu.make_async_remote_copy(
+            src_ref=x_ref.at[me],
+            dst_ref=y_ref.at[:, pl.ds(pl.multiple_of(source * width, width), width)],
+            send_sem=ssem.at[q],
+            recv_sem=rsem.at[q],
+            device_id=(mk, source),
+            device_id_type=MESH,
+        ).wait_recv()
+    for s in range(ne - 1):
+        copies[s].wait_send()
+
+
+def energy_transpose(chunks, ne):
+    rows, width = chunks.shape[1:]
+    return pl.pallas_call(
+        functools.partial(_transpose_kernel, ne),
+        out_shape=jax.ShapeDtypeStruct((rows, ne * width), jnp.float32),
+        in_specs=[pl.BlockSpec(memory_space=pltpu.VMEM)],
+        out_specs=pl.BlockSpec(memory_space=pltpu.VMEM),
+        scratch_shapes=[
+            pltpu.SemaphoreType.DMA((ne - 1,)),
+            pltpu.SemaphoreType.DMA((ne - 1,)),
+        ],
+        compiler_params=pltpu.CompilerParams(collective_id=1, has_side_effects=True),
+    )(chunks)
+
+
 def allreduce_weights(slot_order, prod_tile, nk, ne, entries):
     return pl.pallas_call(
         functools.partial(_allreduce_weights_kernel, nk, ne, entries),
@@ -226,16 +277,17 @@
     )
     lead = greens.shape[:3]
     flat = lambda x: x.reshape((-1,) + x.shape[3:])
-    smeared = jnp.zeros_like(flat(greens))
+    stencil = stencil.reshape(ne, rows_here, 3 * group_len)
+    chunks = jnp.zeros((ne, flat(greens).shape[0], rows_here, greens.shape[4]), jnp.float32)
     for part, block in enumerate((low, greens, high)):
-        smeared = smeared + jnp.einsum(
-            "kr,bre->bke",
-            stencil[:, part * group_len : (part + 1) * group_len],
+        chunks = chunks + jnp.einsum(
+            "dkr,bre->dbke",
+            stencil[:, :, part * group_len : (part + 1) * group_len],
             flat(block),
             precision=lax.Precision.HIGHEST,
         )
-    smeared = smeared.reshape(lead + smeared.shape[1:])
-    rows = lax.all_to_all(smeared, "energy", split_axis=3, concat_axis=4, tiled=True)
+    chunks = chunks.reshape(ne, -1, greens.shape[4])
+    rows = energy_transpose(chunks, ne).reshape(lead + (rows_here, -1))
     classes = acoustic_coupling.shape[0]
     my_class = lax.dynamic_slice_in_dim(momentum_class, energy_id * rows_here, rows_here)
     coupling_row = jnp.sum(

time: 99.4 us -> 100 us (level)
  Pallas kernels: 23.2 us -> 57.1 us
  waiting for transfers between devices: 18.6 us -> 0.01 us
  starting transfers between devices: 26.9 us -> 9.58 us
  other arithmetic: 17.6 us -> 19.5 us
  local copies, waits for them, and re-layouts: 5.23 us -> 7.02 us
    pallas_call x0 -> x1, Pallas kernels: none -> 30.6 us  [energy_transpose(): pl.pallas_call(functools.partial(_transpose_kernel, ne), out_shape=jax.Sh...]
    all_to_all x1 -> x0, starting transfers between devices: 17.3 us -> none  [per_device(): lax.all_to_all(smeared, 'energy', split_axis=3, concat_axis=4, tiled=True)]
    all_to_all x1 -> x0, waiting for transfers between devices: 11.7 us -> none  [per_device(): lax.all_to_all(smeared, 'energy', split_axis=3, concat_axis=4, tiled=True)]
    ppermute x1, waiting for transfers between devices: 6.64 us -> 0.01 us  [padded_2(): lax.ppermute(lax.slice_in_dim(block, block.shape[dim] - width, None, axis...]
    pallas_call x1, Pallas kernels: 23.2 us -> 26.5 us  [allreduce_weights(): pl.pallas_call(functools.partial(_allreduce_weights_kernel, nk, ne, entri...]
    reduce_sum x1, other arithmetic: 3.22 us -> 5 us  [per_device(): jnp.sum(past_residuals[:, None] * past_residuals[None, :], axis=tuple((a...]
  transfers between devices with their start and end apart: 3 -> 2, of which waited for: 3 -> 0; matrix products, arithmetic and copies ran while one was open for 9% -> 10% of each run, Pallas kernels for 0% -> 0%
where the time goes in v3:
time: 100 us; the launch traced here: 99.6 us
  Pallas kernels  57.1 us (57%)
  other arithmetic  19.5 us (20%)
  starting transfers between devices  9.58 us (10%)
  local copies, waits for them, and re-layouts  7.02 us (7%)
  between operations  5.24 us (5%)
  matrix products  1.09 us (1%)
    pallas_call x1, Pallas kernels, energy_transpose(): pl.pallas_call(functools.partial(_transpose_kernel, ne), out_shape=jax.Sh...  30.6 us
    pallas_call x1, Pallas kernels, allreduce_weights(): pl.pallas_call(functools.partial(_allreduce_weights_kernel, nk, ne, entri...  26.5 us
    ppermute x1, starting transfers between devices, padded_2(): lax.ppermute(lax.slice_in_dim(block, 0, width, axis=dim), axis, backward)  7.66 us
    add x1, other arithmetic, per_device(): mixed + weights[column + 1] * (past_inputs[column] + mixing_share * past_...  5.72 us
    reduce_sum x1, other arithmetic, per_device(): jnp.sum(past_residuals[:, None] * past_residuals[None, :], axis=tuple((a...  5 us
    another operation x1, other arithmetic, emit(): return jnp.stack([sigma_less, sigma_more])  4.03 us
  transfers between devices with their start and end apart: 2, of which 0 were waited for; matrix products, arithmetic and copies ran while one was open for 10% of the time, Pallas kernels for 0%

profile of v3, /device:TPU:1, one launch (start us, length us, event | category | flops | bytes accessed | tf_op | source)
XLA Modules:
  0.0 99.6 jit_solution(17497306086220354792)
XLA Ops:
  0.0 7.7 %collective-permute-start.1 = (f32[2,2,2,64,128]{4,3,2,1,0:T(8,128)}, f32[2,2,2,64,128]{4,3,2,1,0:T(8,128)S(1)}, u32[]{:S(2)}, u32[]{:S(2)}) collective-permute-start(f32[2,2,2,64,128]{4,3,2,1,0:T(8,128)} %param.12), channel_id=1, source_target_pairs={{32,0},{64,32},{96,64},{128,96},{160,128},{192,160},{224,192},{256... | collective-permute-start | bytes 786440 | tf_op jit(solution)/shard_map/ppermute | solution.py:29
  7.7 1.9 %collective-permute-start = (f32[2,2,2,64,128]{4,3,2,1,0:T(8,128)}, f32[2,2,2,64,128]{4,3,2,1,0:T(8,128)S(1)}, u32[]{:S(2)}, u32[]{:S(2)}) collective-permute-start(f32[2,2,2,64,128]{4,3,2,1,0:T(8,128)} %param.12), channel_id=1, source_target_pairs={{0,32},{32,64},{64,96},{96,128},{128,160},{160,192},{192,224},{224... | collective-permute-start | bytes 786440 | tf_op jit(solution)/shard_map/ppermute | solution.py:26
  9.6 0.7 add_select_fusion
  10.3 0.8 select_reduce_fusion
  11.1 0.1 fusion.20
  11.2 1.3 %fusion.24 = (s32[1]{0:T(128)}, s32[1]{0:T(128)}) fusion(s32[2]{0:T(128)} %param.23), kind=kLoop, calls=%fused_computation.51 | loop fusion | bytes 16 | tf_op jit(solution)/shard_map/slice | solution.py:46
  12.6 0.0 copy-start.5
  12.6 5.0 %multiply_reduce_fusion = f32[5,5]{1,0:T(8,128)S(1)} fusion(f32[5,2,2,2,2,4096]{5,4,3,2,1,0:T(2,128)} %param.15), kind=kLoop, calls=%fused_computation | loop fusion | flops 3276775 | bytes 1310820 | tf_op jit(solution)/shard_map/reduce_sum | solution.py:308
  17.6 0.4 fusion.9
  18.0 0.6 fusion.23
  18.6 0.1 dynamic_slice.33
  18.6 0.2 fusion.17
  18.8 0.6 fusion.22
  24.5 0.0 collective-permute-done.1
  24.5 0.4 fusion.8
  24.9 0.4 fusion.1
  25.3 0.9 copy.25
  26.2 30.6 %shard_map.118 = f32[16,4096]{1,0:T(8,128)} custom-call(f32[32,16,128]{2,1,0:T(8,128)} %bitcast.86), custom_call_target="tpu_custom_call" | custom-call | tf_op jit(solution)/shard_map/pallas_call | solution.py:210
  56.8 1.1 %reshape.122 = f32[2,2,2,2,4096]{4,3,2,1,0:T(2,128)S(1)} reshape(f32[16,4096]{1,0:T(8,128)} %shard_map.118) | data formatting | bytes 524288 | tf_op jit(solution)/shard_map/reshape | solution.py:290
  57.9 0.0 copy-start.2
  58.0 0.6 pad_slice_fusion.1
  58.6 0.0 copy-start
  58.6 4.0 %fusion.7 = (f32[1,2,2,2,4096]{4,3,2,1,0:T(2,128)S(1)}, f32[1,2,2,2,4096]{4,3,2,1,0:T(2,128)S(1)}) fusion(f32[2,2,2,4288]{3,2,1,0:T(2,128)S(1)} %get-tuple-element.9, f32[1,2,2,2,4288]{4,3,2,1,0:T(2,128)S(1)} %get-tuple-element.7, s32[]{:T(128)S(6)} %select_n.41, s32[]{:T(128)S(6)} %select_n.40, s32[]{:T(128)S(6)} %select_n.39, s32[]{:T(128)S(6)} %select_n.38, ...), kind=kLoop, calls=%fused_computation.23 | loop fusion | flops 720896 | bytes 1572912 | tf_op jit(solution)/shard_map/stack | solution.py:53
  62.6 0.0 copy-start.1
  62.6 0.9 multiply_reduce_fusion.2
  63.5 0.8 multiply_reduce_fusion.1
  64.3 0.7 maximum_bitcast_fusion
  65.0 0.1 copy.26
  65.1 0.7 select_maximum_fusion.p_ref
  65.8 26.5 %shard_map.119 = f32[8,128]{1,0:T(8,128)} custom-call(s32[5]{0:T(128)} %slot_ref.1, f32[8,128]{1,0:T(8,128)} %select_maximum_fusion.p_ref), custom_call_target="tpu_custom_call" | custom-call | tf_op jit(solution)/shard_map/pallas_call | solution.py:224
  92.3 1.5 %fusion.21 = (f32[1,1]{1,0:T(1,128)}, f32[1,1]{1,0:T(1,128)}, f32[1,1]{1,0:T(1,128)}, f32[1,1]{1,0:T(1,128)}, f32[1,1]{1,0:T(1,128)}, /*index=5*/f32[1,1]{1,0:T(1,128)}) fusion(f32[8,128]{1,0:T(8,128)} %shard_map.119), kind=kLoop, calls=%fused_computation.48 | loop fusion | bytes 48 | tf_op jit(solution)/shard_map/slice | solution.py:316
  93.8 5.7 %bitcast_add_fusion = f32[2,2,2,2,4096]{4,3,2,1,0:T(2,128)} fusion(f32[5,2,2,2,2,4096]{5,4,3,2,1,0:T(2,128)S(1)} %copy-done, f32[5,2,2,2,2,4096]{5,4,3,2,1,0:T(2,128)S(1)} %copy-done.1, f32[2,2,2,2,4096]{4,3,2,1,0:T(2,128)S(1)} %copy-done.2, f32[2,2,2,2,4096]{4,3,2,1,0:T(2,128)S(1)} %get-tuple-element.6, f32[]{:T(128)} %bitcast.46, f32[]{:T(128)} %bitcast.44, ...), kind=kLoop, calls=%fused_computation.8 | loop fusion | flops 1507328 | bytes 3407896 | tf_op jit(solution)/shard_map/add | solution.py:318
  (14 shorter events, 0.1 us)
Async XLA Ops:
  0.0 24.5 %collective-permute-start.1 = (f32[2,2,2,64,128]{4,3,2,1,0:T(8,128)}, f32[2,2,2,64,128]{4,3,2,1,0:T(8,128)S(1)}, u32[]{:S(2)}, u32[]{:S(2)}) collective-permute-start(f32[2,2,2,64,128]{4,3,2,1,0:T(8,128)} %param.12), channel_id=1, source_target_pairs={{32,0},{64,32},{96,64},{128,96},{160,128},{192,160},{224,192},{256... | collective-permute-start | bytes 786440 | tf_op jit(solution)/shard_map/ppermute | solution.py:29
  7.7 17.2 %collective-permute-start = (f32[2,2,2,64,128]{4,3,2,1,0:T(8,128)}, f32[2,2,2,64,128]{4,3,2,1,0:T(8,128)S(1)}, u32[]{:S(2)}, u32[]{:S(2)}) collective-permute-start(f32[2,2,2,64,128]{4,3,2,1,0:T(8,128)} %param.12), channel_id=1, source_target_pairs={{0,32},{32,64},{64,96},{96,128},{128,160},{160,192},{192,224},{224... | collective-permute-start | bytes 786440 | tf_op jit(solution)/shard_map/ppermute | solution.py:26
  12.6 5.0 %copy-start.3 = (f32[2,2,2,64,128]{4,3,2,1,0:T(8,128)S(1)}, f32[2,2,2,64,128]{4,3,2,1,0:T(8,128)}, u32[]{:S(2)}) copy-start(f32[2,2,2,64,128]{4,3,2,1,0:T(8,128)} %param.12) | copy-start | bytes 786436
  12.6 5.4 %copy-start.4 = (f32[2]{0:T(128)S(1)}, f32[2]{0:T(128)}, u32[]{:S(2)}) copy-start(f32[2]{0:T(128)} %param.22) | copy-start | bytes 28
  12.6 6.0 %copy-start.6 = (s32[64]{0:T(128)S(1)}, s32[64]{0:T(128)}, u32[]{:S(2)}) copy-start(s32[64]{0:T(128)} %param.18) | copy-start | bytes 772
  12.6 6.1 %copy-start.7 = (f32[4]{0:T(128)S(1)}, f32[4]{0:T(128)}, u32[]{:S(2)}) copy-start(f32[4]{0:T(128)} %param.20) | copy-start | bytes 52
  12.6 6.2 %copy-start.5 = (f32[2]{0:T(128)S(1)}, f32[2]{0:T(128)}, u32[]{:S(2)}) copy-start(f32[2]{0:T(128)} %param.21) | copy-start | bytes 28
  57.9 4.7 %copy-start.2 = (f32[2,2,2,2,4096]{4,3,2,1,0:T(2,128)S(1)}, f32[2,2,2,2,4096]{4,3,2,1,0:T(2,128)}, u32[]{:S(2)}) copy-start(f32[2,2,2,2,4096]{4,3,2,1,0:T(2,128)} %param.13) | copy-start | bytes 786436
  58.6 5.0 %copy-start = (f32[5,2,2,2,2,4096]{5,4,3,2,1,0:T(2,128)S(1)}, f32[5,2,2,2,2,4096]{5,4,3,2,1,0:T(2,128)}, u32[]{:S(2)}) copy-start(f32[5,2,2,2,2,4096]{5,4,3,2,1,0:T(2,128)} %param.15) | copy-start | bytes 3932164
  62.6 31.2 %copy-start.1 = (f32[5,2,2,2,2,4096]{5,4,3,2,1,0:T(2,128)S(1)}, f32[5,2,2,2,2,4096]{5,4,3,2,1,0:T(2,128)}, u32[]{:S(2)}) copy-start(f32[5,2,2,2,2,4096]{5,4,3,2,1,0:T(2,128)} %param.14) | copy-start | bytes 3932164

commit v4 on v3

--- a/solution.py
+++ b/solution.py
@@ -120,7 +120,22 @@
     return jnp.where(col < count, both, 0.0)
 
 
-def _allreduce_weights_kernel(nk, ne, entries, slot_ref, p_ref, w_ref, recv1, recv2, acc1, ss1, rs1, ss2, rs2):
+def _local_products(res, hist):
+    shape = (8, 128)
+    row = lax.broadcasted_iota(jnp.int32, shape, 0)
+    col = lax.broadcasted_iota(jnp.int32, shape, 1)
+    vectors = [res] + [hist[m] for m in range(HIST)]
+    prod = jnp.zeros(shape, jnp.float32)
+    for i in range(HIST + 1):
+        for j in range(i, HIST + 1):
+            value = jnp.sum(vectors[i] * vectors[j], keepdims=True)
+            spot = ((row == i) & (col == j)) | ((row == j) & (col == i))
+            prod = jnp.where(spot, value, prod)
+    return prod
+
+
+def _mix_kernel(nk, ne, entries, slot_ref, res_ref, cur_ref, pin_ref, pres_ref, out_ref,
+                send1, recv1, recv2, acc1, ss1, rs1, ss2, rs2):
     mk = lax.axis_index("kgrp")
     me = lax.axis_index("energy")
     barrier = pltpu.get_barrier_semaphore()
@@ -128,6 +143,7 @@
         pl.semaphore_signal(barrier, 1, device_id=((mk + s + 1) % nk, me), device_id_type=MESH)
     for s in range(ne - 1):
         pl.semaphore_signal(barrier, 1, device_id=(mk, (me + s + 1) % ne), device_id_type=MESH)
+    send1[...] = _local_products(res_ref[...], pres_ref)
     pl.semaphore_wait(barrier, nk - 1 + ne - 1)
 
     def exchange(src, recv, ssem, rsem, count, peer):
@@ -155,18 +171,46 @@
             acc = acc + jnp.where(idx == mine, own, recv[slot])
         return acc
 
-    exchange(p_ref, recv1, ss1, rs1, nk, lambda s: ((mk + s + 1) % nk, me))
-    acc1[...] = total(p_ref[...], recv1, mk, nk)
+    exchange(send1, recv1, ss1, rs1, nk, lambda s: ((mk + s + 1) % nk, me))
+    acc1[...] = total(send1[...], recv1, mk, nk)
     exchange(acc1, recv2, ss2, rs2, ne, lambda s: (mk, (me + s + 1) % ne))
     summed = total(acc1[...], recv2, me, ne)
     perm = [0] + [slot_ref[i] + 1 for i in range(HIST)]
     aged = _permute_square(summed / entries, perm)
     weights = _weights_from_products(aged)[:, :1]
     row1 = lax.broadcasted_iota(jnp.int32, weights.shape, 0)
-    by_slot = jnp.zeros_like(weights)
+    slot_w = [None] * (HIST + 1)
     for i in range(HIST + 1):
-        by_slot = by_slot + jnp.where(row1 == perm[i], _pick(row1 == i, weights, 0), 0.0)
-    w_ref[...] = jnp.broadcast_to(by_slot, w_ref.shape)
+        w_i = _pick(row1 == i, weights, 0)
+        for m in range(HIST + 1):
+            term = jnp.where(perm[i] == m, w_i, 0.0)
+            slot_w[m] = term if slot_w[m] is None else slot_w[m] + term
+    mixed = slot_w[0] * (cur_ref[...] + mixing_share * res_ref[...])
+    for m in range(HIST):
+        mixed = mixed + slot_w[m + 1] * (pin_ref[m] + mixing_share * pres_ref[m])
+    out_ref[...] = mixed
+
+
+def mix_allreduce(slot_order, res, cur, pin, pres, nk, ne, entries):
+    tile = (8, 128)
+    vmem = pl.BlockSpec(memory_space=pltpu.VMEM)
+    return pl.pallas_call(
+        functools.partial(_mix_kernel, nk, ne, entries),
+        out_shape=jax.ShapeDtypeStruct(cur.shape, jnp.float32),
+        in_specs=[pl.BlockSpec(memory_space=pltpu.SMEM), vmem, vmem, vmem, vmem],
+        out_specs=vmem,
+        scratch_shapes=[
+            pltpu.VMEM(tile, jnp.float32),
+            pltpu.VMEM((nk - 1,) + tile, jnp.float32),
+            pltpu.VMEM((ne - 1,) + tile, jnp.float32),
+            pltpu.VMEM(tile, jnp.float32),
+            pltpu.SemaphoreType.DMA((nk - 1,)),
+            pltpu.SemaphoreType.DMA((nk - 1,)),
+            pltpu.SemaphoreType.DMA((ne - 1,)),
+            pltpu.SemaphoreType.DMA((ne - 1,)),
+        ],
+        compiler_params=pltpu.CompilerParams(collective_id=0, has_side_effects=True),
+    )(slot_order, res, cur, pin, pres)
 
 
 def _transpose_kernel(ne, x_ref, y_ref, ssem, rsem):
@@ -218,28 +262,6 @@
         ],
         compiler_params=pltpu.CompilerParams(collective_id=1, has_side_effects=True),
     )(chunks)
-
-
-def allreduce_weights(slot_order, prod_tile, nk, ne, entries):
-    return pl.pallas_call(
-        functools.partial(_allreduce_weights_kernel, nk, ne, entries),
-        out_shape=jax.ShapeDtypeStruct(prod_tile.shape, jnp.float32),
-        in_specs=[
-            pl.BlockSpec(memory_space=pltpu.SMEM),
-            pl.BlockSpec(memory_space=pltpu.VMEM),
-        ],
-        out_specs=pl.BlockSpec(memory_space=pltpu.VMEM),
-        scratch_shapes=[
-            pltpu.VMEM((nk - 1,) + prod_tile.shape, jnp.float32),
-            pltpu.VMEM((ne - 1,) + prod_tile.shape, jnp.float32),
-            pltpu.VMEM(prod_tile.shape, jnp.float32),
-            pltpu.SemaphoreType.DMA((nk - 1,)),
-            pltpu.SemaphoreType.DMA((nk - 1,)),
-            pltpu.SemaphoreType.DMA((ne - 1,)),
-            pltpu.SemaphoreType.DMA((ne - 1,)),
-        ],
-        compiler_params=pltpu.CompilerParams(collective_id=0, has_side_effects=True),
-    )(slot_order, prod_tile)
 
 
 def per_device(
@@ -304,20 +326,18 @@
         padded, SHIFT_MAX, rows.shape[-1], coupling_row, optical_coupling, occupation, phonon_shift
     )
     residual_now = sigma_new - current
-    data_axes = tuple(range(1, past_residuals.ndim))
-    old_gram = jnp.sum(past_residuals[:, None] * past_residuals[None, :], axis=tuple(a + 1 for a in data_axes))
-    cross = jnp.sum(residual_now[None] * past_residuals, axis=data_axes)
-    self_term = jnp.sum(residual_now * residual_now)
-    top = jnp.concatenate([self_term[None], cross])
-    products = jnp.concatenate([top[None, :], jnp.concatenate([cross[:, None], old_gram], axis=1)], axis=0)
-    prod_tile = jnp.pad(products, ((0, 8 - HIST - 1), (0, 128 - HIST - 1)))
+    lanes = current.shape[-1]
     entries = float(residual_now.size * nk * ne)
-    weights = allreduce_weights(slot_order, prod_tile, nk, ne, entries)[: HIST + 1, 0]
-    mixed = weights[0] * (current + mixing_share * residual_now)
-    for column in range(HIST):
-        mixed = mixed + weights[column + 1] * (
-            past_inputs[column] + mixing_share * past_residuals[column]
-        )
+    mixed = mix_allreduce(
+        slot_order,
+        residual_now.reshape(-1, lanes),
+        current.reshape(-1, lanes),
+        past_inputs.reshape(HIST, -1, lanes),
+        past_residuals.reshape(HIST, -1, lanes),
+        nk,
+        ne,
+        entries,
+    ).reshape(current.shape)
     return mixed
 
 

time: 100 us -> 95.6 us (0.956)
  other arithmetic: 19.5 us -> 6.34 us
  local copies, waits for them, and re-layouts: 7.02 us -> 15.9 us
  Pallas kernels: 57.1 us -> 56 us
    reshape x0 -> x5, local copies, waits for them, and re-layouts: none -> 8.45 us  [the longest x1 1.97 us: per_device(): past_residuals.reshape(HIST, -1, lanes)]
    reduce_sum x3 -> x0, other arithmetic: 6.67 us -> none  [the longest x1 5 us: per_device(): jnp.sum(past_residuals[:, None] * past_residuals[None, :], axis=tuple((a...]
    add x1 -> x0, other arithmetic: 5.72 us -> none  [per_device(): mixed + weights[column + 1] * (past_inputs[column] + mixing_share * past_...]
    ppermute x1, starting transfers between devices: 1.92 us -> 4.07 us  [padded_2(): lax.ppermute(lax.slice_in_dim(block, block.shape[dim] - width, None, axis...]
    ppermute x1, starting transfers between devices: 7.66 us -> 5.64 us  [padded_2(): lax.ppermute(lax.slice_in_dim(block, 0, width, axis=dim), axis, backward)]
    slice x1 -> x0, local copies, waits for them, and re-layouts: 1.51 us -> none  [per_device(): mixed = weights[0] * (current + mixing_share * residual_now)]
    pallas_call x1, Pallas kernels: 26.5 us -> 25.3 us  [mix_allreduce(): pl.pallas_call(functools.partial(_mix_kernel, nk, ne, entries), out_shape...]
  transfers between devices with their start and end apart: 2 -> 2, of which waited for: 0 -> 0; matrix products, arithmetic and copies ran while one was open for 10% -> 15% of each run, Pallas kernels for 0% -> 0%
where the time goes in v4:
time: 95.6 us; the launch traced here: 95 us
  Pallas kernels  56 us (59%)
  local copies, waits for them, and re-layouts  15.9 us (17%)
  starting transfers between devices  9.71 us (10%)
  other arithmetic  6.34 us (7%)
  between operations  4.99 us (5%)
  matrix products  2.05 us (2%)
    pallas_call x1, Pallas kernels, energy_transpose(): pl.pallas_call(functools.partial(_transpose_kernel, ne), out_shape=jax.Sh...  30.7 us
    pallas_call x1, Pallas kernels, mix_allreduce(): pl.pallas_call(functools.partial(_mix_kernel, nk, ne, entries), out_shape...  25.3 us
    ppermute x1, starting transfers between devices, padded_2(): lax.ppermute(lax.slice_in_dim(block, 0, width, axis=dim), axis, backward)  5.64 us
    ppermute x1, starting transfers between devices, padded_2(): lax.ppermute(lax.slice_in_dim(block, block.shape[dim] - width, None, axis...  4.07 us
    another operation x1, other arithmetic, emit(): return jnp.stack([sigma_less, sigma_more])  3.86 us
    dot_general x3, matrix products, per_device(): jnp.einsum('dkr,bre->dbke', stencil[:, :, part * group_len:(part + 1) * g...  2.05 us
    reshape x1, local copies, waits for them, and re-layouts, per_device(): past_residuals.reshape(HIST, -1, lanes)  1.97 us
    reshape x1, local copies, waits for them, and re-layouts, per_device(): past_inputs.reshape(HIST, -1, lanes)  1.97 us
  transfers between devices with their start and end apart: 2, of which 0 were waited for; matrix products, arithmetic and copies ran while one was open for 15% of the time, Pallas kernels for 0%

profile of v4, /device:TPU:1, one launch (start us, length us, event | category | flops | bytes accessed | tf_op | source)
XLA Modules:
  0.0 95.0 jit_solution(3028605206329706411)
XLA Ops:
  0.0 0.0 copy-start
  0.0 4.1 %collective-permute-start = (f32[2,2,2,64,128]{4,3,2,1,0:T(8,128)}, f32[2,2,2,64,128]{4,3,2,1,0:T(8,128)S(1)}, u32[]{:S(2)}, u32[]{:S(2)}) collective-permute-start(f32[2,2,2,64,128]{4,3,2,1,0:T(8,128)} %param.12), channel_id=1, source_target_pairs={{0,32},{32,64},{64,96},{96,128},{128,160},{160,192},{192,224},{224... | collective-permute-start | bytes 786440 | tf_op jit(solution)/shard_map/ppermute | solution.py:26
  4.1 5.6 %collective-permute-start.1 = (f32[2,2,2,64,128]{4,3,2,1,0:T(8,128)}, f32[2,2,2,64,128]{4,3,2,1,0:T(8,128)S(1)}, u32[]{:S(2)}, u32[]{:S(2)}) collective-permute-start(f32[2,2,2,64,128]{4,3,2,1,0:T(8,128)} %param.12), channel_id=1, source_target_pairs={{32,0},{64,32},{96,64},{128,96},{160,128},{192,160},{224,192},{256... | collective-permute-start | bytes 786440 | tf_op jit(solution)/shard_map/ppermute | solution.py:29
  9.7 1.3 %fusion.15 = (f32[1]{0:T(128)}, f32[1]{0:T(128)}) fusion(f32[2]{0:T(128)} %param.21), kind=kLoop, calls=%fused_computation.30 | loop fusion | bytes 16 | tf_op jit(solution)/shard_map/slice | solution.py:44
  11.1 0.7 add_select_fusion
  11.8 0.8 select_reduce_fusion
  12.6 0.1 fusion.14
  12.7 1.3 %fusion.9 = f32[32,2,8,128]{3,0,2,1:T(8,128)S(1)} fusion(f32[8,64,128,1]{2,1,0,3:T(8,128)} %bitcast.59, f32[32,2,64]{2,1,0:T(2,128)S(1)} %get-tuple-element.10), kind=kOutput, calls=%fused_computation.19 | convolution fusion | flops 50331648 | bytes 540672 | tf_op jit(solution)/shard_map/dkr,bre->dbke/dot_general | solution.py:305
  14.0 1.3 %fusion.16 = (f32[1]{0:T(128)}, f32[1]{0:T(128)}) fusion(f32[2]{0:T(128)} %param.22), kind=kLoop, calls=%fused_computation.31 | loop fusion | bytes 16 | tf_op jit(solution)/shard_map/slice | solution.py:45
  15.3 0.7 dynamic_slice.33
  16.1 0.8 fusion.11
  16.9 1.3 %fusion.17 = (s32[1]{0:T(128)}, s32[1]{0:T(128)}) fusion(s32[2]{0:T(128)} %param.23), kind=kLoop, calls=%fused_computation.32 | loop fusion | bytes 16 | tf_op jit(solution)/shard_map/slice | solution.py:46
  23.1 1.8 %reshape.99.cur_ref = f32[16,4096]{1,0:T(8,128)} reshape(f32[2,2,2,2,4096]{4,3,2,1,0:T(2,128)} %param.13) | data formatting | bytes 524288 | tf_op jit(solution)/shard_map/reshape | solution.py:334
  24.9 0.0 copy-done
  24.9 2.0 %reshape.100.pin_ref = f32[5,16,4096]{2,1,0:T(8,128)} reshape(f32[5,2,2,2,2,4096]{5,4,3,2,1,0:T(2,128)S(1)} %copy-done) | data formatting | bytes 2621440 | tf_op jit(solution)/shard_map/reshape | solution.py:335
  26.9 0.0 copy-done.1
  26.9 2.0 %reshape.101.pres_ref = f32[5,16,4096]{2,1,0:T(8,128)} reshape(f32[5,2,2,2,2,4096]{5,4,3,2,1,0:T(2,128)S(1)} %copy-done.1) | data formatting | bytes 2621440 | tf_op jit(solution)/shard_map/reshape | solution.py:336
  28.8 0.0 collective-permute-done.1
  28.8 0.4 fusion.8
  29.2 0.0 collective-permute-done
  29.2 0.4 fusion.1
  29.6 0.9 copy.23
  30.5 30.7 %shard_map.118 = f32[16,4096]{1,0:T(8,128)} custom-call(f32[32,16,128]{2,1,0:T(8,128)} %bitcast.58), custom_call_target="tpu_custom_call" | custom-call | tf_op jit(solution)/shard_map/pallas_call | solution.py:254
  61.2 1.1 %reshape.97 = f32[2,2,2,2,4096]{4,3,2,1,0:T(2,128)S(1)} reshape(f32[16,4096]{1,0:T(8,128)} %shard_map.118) | data formatting | bytes 524288 | tf_op jit(solution)/shard_map/reshape | solution.py:312
  62.3 0.0 copy-start.2
  62.4 0.6 pad_slice_fusion.1
  63.0 3.9 %fusion.7 = (f32[1,2,2,2,4096]{4,3,2,1,0:T(2,128)S(1)}, f32[1,2,2,2,4096]{4,3,2,1,0:T(2,128)S(1)}) fusion(f32[2,2,2,4288]{3,2,1,0:T(2,128)S(1)} %get-tuple-element.7, f32[1,2,2,2,4288]{4,3,2,1,0:T(2,128)S(1)} %get-tuple-element.5, s32[]{:T(128)S(6)} %select_n.41, s32[]{:T(128)S(6)} %select_n.40, s32[]{:T(128)S(6)} %select_n.39, s32[]{:T(128)S(6)} %select_n.38, ...), kind=kLoop, calls=%fused_computation.15 | loop fusion | flops 720896 | bytes 1572912 | tf_op jit(solution)/shard_map/stack | solution.py:53
  66.8 0.0 copy-done.2
  66.8 0.2 maximum_subtract_fusion
  67.0 0.9 reshape.98.res_ref
  67.9 25.3 %shard_map.119 = f32[16,4096]{1,0:T(8,128)} custom-call(s32[5]{0:T(128)} %slot_ref.1, f32[16,4096]{1,0:T(8,128)} %reshape.98.res_ref, f32[16,4096]{1,0:T(8,128)} %reshape.99.cur_ref, f32[5,16,4096]{2,1,0:T(8,128)} %reshape.100.pin_ref, f32[5,16,4096]{2,1,0:T(8,128)} %reshape.101.pres_ref), custom_call_target="tpu_custom_call" | custom-call | tf_op jit(solution)/shard_map/pallas_call | solution.py:197
  93.2 1.8 %reshape.102 = f32[2,2,2,2,4096]{4,3,2,1,0:T(2,128)} reshape(f32[16,4096]{1,0:T(8,128)} %shard_map.119) | data formatting | bytes 524288 | tf_op jit(solution)/shard_map/reshape | solution.py:340
  (2 shorter events, 0.0 us)
Async XLA Ops:
  0.0 24.9 %copy-start = (f32[5,2,2,2,2,4096]{5,4,3,2,1,0:T(2,128)S(1)}, f32[5,2,2,2,2,4096]{5,4,3,2,1,0:T(2,128)}, u32[]{:S(2)}) copy-start(f32[5,2,2,2,2,4096]{5,4,3,2,1,0:T(2,128)} %param.14) | copy-start | bytes 3932164
  0.0 29.2 %collective-permute-start = (f32[2,2,2,64,128]{4,3,2,1,0:T(8,128)}, f32[2,2,2,64,128]{4,3,2,1,0:T(8,128)S(1)}, u32[]{:S(2)}, u32[]{:S(2)}) collective-permute-start(f32[2,2,2,64,128]{4,3,2,1,0:T(8,128)} %param.12), channel_id=1, source_target_pairs={{0,32},{32,64},{64,96},{96,128},{128,160},{160,192},{192,224},{224... | collective-permute-start | bytes 786440 | tf_op jit(solution)/shard_map/ppermute | solution.py:26
  4.1 24.8 %collective-permute-start.1 = (f32[2,2,2,64,128]{4,3,2,1,0:T(8,128)}, f32[2,2,2,64,128]{4,3,2,1,0:T(8,128)S(1)}, u32[]{:S(2)}, u32[]{:S(2)}) collective-permute-start(f32[2,2,2,64,128]{4,3,2,1,0:T(8,128)} %param.12), channel_id=1, source_target_pairs={{32,0},{64,32},{96,64},{128,96},{160,128},{192,160},{224,192},{256... | collective-permute-start | bytes 786440 | tf_op jit(solution)/shard_map/ppermute | solution.py:29
  24.9 2.0 %copy-start.1 = (f32[5,2,2,2,2,4096]{5,4,3,2,1,0:T(2,128)S(1)}, f32[5,2,2,2,2,4096]{5,4,3,2,1,0:T(2,128)}, u32[]{:S(2)}) copy-start(f32[5,2,2,2,2,4096]{5,4,3,2,1,0:T(2,128)} %param.15) | copy-start | bytes 3932164
  62.3 4.5 %copy-start.2 = (f32[2,2,2,2,4096]{4,3,2,1,0:T(2,128)S(1)}, f32[2,2,2,2,4096]{4,3,2,1,0:T(2,128)}, u32[]{:S(2)}) copy-start(f32[2,2,2,2,4096]{4,3,2,1,0:T(2,128)} %param.13) | copy-start | bytes 786436

commit v5 on v4

--- a/solution.py
+++ b/solution.py
@@ -120,34 +120,88 @@
     return jnp.where(col < count, both, 0.0)
 
 
-def _local_products(res, hist):
+def _pair_sums(vectors, pairs):
     shape = (8, 128)
     row = lax.broadcasted_iota(jnp.int32, shape, 0)
     col = lax.broadcasted_iota(jnp.int32, shape, 1)
-    vectors = [res] + [hist[m] for m in range(HIST)]
     prod = jnp.zeros(shape, jnp.float32)
-    for i in range(HIST + 1):
-        for j in range(i, HIST + 1):
-            value = jnp.sum(vectors[i] * vectors[j], keepdims=True)
-            spot = ((row == i) & (col == j)) | ((row == j) & (col == i))
-            prod = jnp.where(spot, value, prod)
+    for i, j in pairs:
+        value = jnp.sum(vectors[i] * vectors[j], keepdims=True)
+        spot = ((row == i) & (col == j)) | ((row == j) & (col == i))
+        prod = jnp.where(spot, value, prod)
     return prod
 
 
-def _mix_kernel(nk, ne, entries, slot_ref, res_ref, cur_ref, pin_ref, pres_ref, out_ref,
-                send1, recv1, recv2, acc1, ss1, rs1, ss2, rs2):
+def _fused_kernel(nk, ne, entries, margin,
+                  slot_ref, shift_ref, class_ref, optical_ref, occ_ref, acoustic_ref,
+                  chunk_ref, cur_ref, pin_ref, pres_ref, out_ref,
+                  ypad, send1, recv1, recv2, acc1, ts, tr, ss1, rs1, ss2, rs2):
     mk = lax.axis_index("kgrp")
     me = lax.axis_index("energy")
+    width = chunk_ref.shape[-1]
+    rows, padded_len = ypad.shape
+    length = padded_len - 2 * margin
     barrier = pltpu.get_barrier_semaphore()
     for s in range(nk - 1):
         pl.semaphore_signal(barrier, 1, device_id=((mk + s + 1) % nk, me), device_id_type=MESH)
     for s in range(ne - 1):
         pl.semaphore_signal(barrier, 1, device_id=(mk, (me + s + 1) % ne), device_id_type=MESH)
-    send1[...] = _local_products(res_ref[...], pres_ref)
+    ypad[:, :margin] = jnp.zeros((rows, margin), jnp.float32)
+    ypad[:, margin + length :] = jnp.zeros((rows, margin), jnp.float32)
+    ypad[:, pl.ds(pl.multiple_of(margin + me * width, width), width)] = chunk_ref[me]
     pl.semaphore_wait(barrier, nk - 1 + ne - 1)
 
+    copies = []
+    for s in range(ne - 1):
+        peer = (me + s + 1) % ne
+        c = pltpu.make_async_remote_copy(
+            src_ref=chunk_ref.at[peer],
+            dst_ref=ypad.at[:, pl.ds(pl.multiple_of(margin + me * width, width), width)],
+            send_sem=ts.at[s],
+            recv_sem=tr.at[ne - 2 - s],
+            device_id=(mk, peer),
+            device_id_type=MESH,
+        )
+        c.start()
+        copies.append(c)
+    history = [pres_ref[m] for m in range(HIST)]
+    gram = _pair_sums([None] + history, [(i, j) for i in range(1, HIST + 1) for j in range(i, HIST + 1)])
+    for q in range(ne - 1):
+        source = (me + q + 1) % ne
+        pltpu.make_async_remote_copy(
+            src_ref=chunk_ref.at[me],
+            dst_ref=ypad.at[:, pl.ds(pl.multiple_of(margin + source * width, width), width)],
+            send_sem=ts.at[q],
+            recv_sem=tr.at[q],
+            device_id=(mk, source),
+            device_id_type=MESH,
+        ).wait_recv()
+    for s in range(ne - 1):
+        copies[s].wait_send()
+
+    y = ypad[...]
+    row = lax.broadcasted_iota(jnp.int32, (rows, 1), 0)
+    lesser = row < rows // 2
+    per_row = rows // 8
+    coupling = jnp.zeros((rows, 1), jnp.float32)
+    for r in range(per_row):
+        coupling = jnp.where(row % per_row == r, acoustic_ref[class_ref[me * per_row + r]], coupling)
+    sigma = coupling * y[:, margin : margin + length]
+    for m in range(2):
+        shift = shift_ref[m]
+        strength = optical_ref[m]
+        number = occ_ref[m]
+        ahead = pltpu.roll(y, padded_len - shift, 1)[:, margin : margin + length]
+        behind = pltpu.roll(y, shift, 1)[:, margin : margin + length]
+        up = jnp.where(lesser, number + 1.0, number)
+        down = jnp.where(lesser, number, number + 1.0)
+        sigma = sigma + strength * (up * ahead + down * behind)
+    res = sigma - cur_ref[...]
+    fresh = _pair_sums([res] + history, [(0, j) for j in range(HIST + 1)])
+    send1[...] = fresh + gram
+
     def exchange(src, recv, ssem, rsem, count, peer):
-        copies = []
+        out = []
         for s in range(count - 1):
             c = pltpu.make_async_remote_copy(
                 src_ref=src,
@@ -158,11 +212,11 @@
                 device_id_type=MESH,
             )
             c.start()
-            copies.append(c)
+            out.append(c)
         for s in range(count - 1):
-            copies[s].wait_recv()
+            out[s].wait_recv()
         for s in range(count - 1):
-            copies[s].wait_send()
+            out[s].wait_send()
 
     def total(own, recv, mine, count):
         acc = jnp.zeros_like(own)
@@ -185,83 +239,38 @@
         for m in range(HIST + 1):
             term = jnp.where(perm[i] == m, w_i, 0.0)
             slot_w[m] = term if slot_w[m] is None else slot_w[m] + term
-    mixed = slot_w[0] * (cur_ref[...] + mixing_share * res_ref[...])
+    mixed = slot_w[0] * (cur_ref[...] + mixing_share * res)
     for m in range(HIST):
         mixed = mixed + slot_w[m + 1] * (pin_ref[m] + mixing_share * pres_ref[m])
     out_ref[...] = mixed
 
 
-def mix_allreduce(slot_order, res, cur, pin, pres, nk, ne, entries):
+def fused_tail(scalars, chunks, cur, pin, pres, nk, ne, entries):
     tile = (8, 128)
+    margin = 128
+    rows = chunks.shape[1]
+    smem = pl.BlockSpec(memory_space=pltpu.SMEM)
     vmem = pl.BlockSpec(memory_space=pltpu.VMEM)
     return pl.pallas_call(
-        functools.partial(_mix_kernel, nk, ne, entries),
+        functools.partial(_fused_kernel, nk, ne, entries, margin),
         out_shape=jax.ShapeDtypeStruct(cur.shape, jnp.float32),
-        in_specs=[pl.BlockSpec(memory_space=pltpu.SMEM), vmem, vmem, vmem, vmem],
+        in_specs=[smem] * len(scalars) + [vmem] * 4,
         out_specs=vmem,
         scratch_shapes=[
+            pltpu.VMEM((rows, cur.shape[1] + 2 * margin), jnp.float32),
             pltpu.VMEM(tile, jnp.float32),
             pltpu.VMEM((nk - 1,) + tile, jnp.float32),
             pltpu.VMEM((ne - 1,) + tile, jnp.float32),
             pltpu.VMEM(tile, jnp.float32),
+            pltpu.SemaphoreType.DMA((ne - 1,)),
+            pltpu.SemaphoreType.DMA((ne - 1,)),
             pltpu.SemaphoreType.DMA((nk - 1,)),
             pltpu.SemaphoreType.DMA((nk - 1,)),
             pltpu.SemaphoreType.DMA((ne - 1,)),
             pltpu.SemaphoreType.DMA((ne - 1,)),
         ],
         compiler_params=pltpu.CompilerParams(collective_id=0, has_side_effects=True),
-    )(slot_order, res, cur, pin, pres)
-
-
-def _transpose_kernel(ne, x_ref, y_ref, ssem, rsem):
-    mk = lax.axis_index("kgrp")
-    me = lax.axis_index("energy")
-    width = x_ref.shape[-1]
-    barrier = pltpu.get_barrier_semaphore()
-    for s in range(ne - 1):
-        pl.semaphore_signal(barrier, 1, device_id=(mk, (me + s + 1) % ne), device_id_type=MESH)
-    pl.semaphore_wait(barrier, ne - 1)
-    copies = []
-    for s in range(ne - 1):
-        peer = (me + s + 1) % ne
-        c = pltpu.make_async_remote_copy(
-            src_ref=x_ref.at[peer],
-            dst_ref=y_ref.at[:, pl.ds(pl.multiple_of(me * width, width), width)],
-            send_sem=ssem.at[s],
-            recv_sem=rsem.at[ne - 2 - s],
-            device_id=(mk, peer),
-            device_id_type=MESH,
-        )
-        c.start()
-        copies.append(c)
-    y_ref[:, pl.ds(pl.multiple_of(me * width, width), width)] = x_ref[me]
-    for q in range(ne - 1):
-        source = (me + q + 1) % ne
-        pltpu.make_async_remote_copy(
-            src_ref=x_ref.at[me],
-            dst_ref=y_ref.at[:, pl.ds(pl.multiple_of(source * width, width), width)],
-            send_sem=ssem.at[q],
-            recv_sem=rsem.at[q],
-            device_id=(mk, source),
-            device_id_type=MESH,
-        ).wait_recv()
-    for s in range(ne - 1):
-        copies[s].wait_send()
-
-
-def energy_transpose(chunks, ne):
-    rows, width = chunks.shape[1:]
-    return pl.pallas_call(
-        functools.partial(_transpose_kernel, ne),
-        out_shape=jax.ShapeDtypeStruct((rows, ne * width), jnp.float32),
-        in_specs=[pl.BlockSpec(memory_space=pltpu.VMEM)],
-        out_specs=pl.BlockSpec(memory_space=pltpu.VMEM),
-        scratch_shapes=[
-            pltpu.SemaphoreType.DMA((ne - 1,)),
-            pltpu.SemaphoreType.DMA((ne - 1,)),
-        ],
-        compiler_params=pltpu.CompilerParams(collective_id=1, has_side_effects=True),
-    )(chunks)
+    )(*scalars, chunks, cur, pin, pres)
 
 
 def per_device(
@@ -309,28 +318,12 @@
             precision=lax.Precision.HIGHEST,
         )
     chunks = chunks.reshape(ne, -1, greens.shape[4])
-    rows = energy_transpose(chunks, ne).reshape(lead + (rows_here, -1))
-    classes = acoustic_coupling.shape[0]
-    my_class = lax.dynamic_slice_in_dim(momentum_class, energy_id * rows_here, rows_here)
-    coupling_row = jnp.sum(
-        jnp.where(
-            my_class[:, None] == jnp.arange(classes, dtype=jnp.int32)[None, :],
-            acoustic_coupling[None, :],
-            0.0,
-        ),
-        axis=1,
-    )
-    pad = [(0, 0)] * (rows.ndim - 1) + [(SHIFT_MAX, SHIFT_MAX)]
-    padded = jnp.pad(rows, pad)
-    sigma_new = emit(
-        padded, SHIFT_MAX, rows.shape[-1], coupling_row, optical_coupling, occupation, phonon_shift
-    )
-    residual_now = sigma_new - current
     lanes = current.shape[-1]
-    entries = float(residual_now.size * nk * ne)
-    mixed = mix_allreduce(
-        slot_order,
-        residual_now.reshape(-1, lanes),
+    entries = float(current.size * nk * ne)
+    scalars = (slot_order, phonon_shift, momentum_class, optical_coupling, occupation, acoustic_coupling)
+    mixed = fused_tail(
+        scalars,
+        chunks,
         current.reshape(-1, lanes),
         past_inputs.reshape(HIST, -1, lanes),
         past_residuals.reshape(HIST, -1, lanes),

time: 95.6 us -> 72.7 us (0.76)
  local copies, waits for them, and re-layouts: 15.9 us -> 8.64 us
  Pallas kernels: 56 us -> 50.5 us
  between operations: 4.99 us -> 0.08 us
  other arithmetic: 6.34 us -> 1.48 us
    pallas_call x2 -> x1, Pallas kernels: 56 us -> 50.5 us  [fused_tail(): pl.pallas_call(functools.partial(_fused_kernel, nk, ne, entries, margin),...]
    slice x4 -> x0, local copies, waits for them, and re-layouts: 4.58 us -> none  [the longest x1 1.34 us: emit(): strength = optical[column]]
    another operation x1 -> x0, other arithmetic: 3.86 us -> none  [emit(): return jnp.stack([sigma_less, sigma_more])]
    reshape x3 -> x1, local copies, waits for them, and re-layouts: 3.79 us -> 1.8 us  [per_device(): mixed = fused_tail(scalars, chunks, current.reshape(-1, lanes), past_inpu...]
  transfers between devices with their start and end apart: 2 -> 2, of which waited for: 0 -> 0; matrix products, arithmetic and copies ran while one was open for 15% -> 13% of each run, Pallas kernels for 0% -> 0%
where the time goes in v5:
time: 72.7 us; the launch traced here: 72.4 us
  Pallas kernels  50.5 us (69%)
  starting transfers between devices  9.71 us (13%)
  local copies, waits for them, and re-layouts  8.64 us (12%)
  matrix products  2.04 us (3%)
  other arithmetic  1.48 us (2%)
    pallas_call x1, Pallas kernels, fused_tail(): pl.pallas_call(functools.partial(_fused_kernel, nk, ne, entries, margin),...  50.5 us
    ppermute x1, starting transfers between devices, padded_2(): lax.ppermute(lax.slice_in_dim(block, 0, width, axis=dim), axis, backward)  5.64 us
    ppermute x1, starting transfers between devices, padded_2(): lax.ppermute(lax.slice_in_dim(block, block.shape[dim] - width, None, axis...  4.07 us
    dot_general x3, matrix products, per_device(): jnp.einsum('dkr,bre->dbke', stencil[:, :, part * group_len:(part + 1) * g...  2.04 us
    reshape x1, local copies, waits for them, and re-layouts, per_device(): past_residuals.reshape(HIST, -1, lanes)  1.98 us
    reshape x1, local copies, waits for them, and re-layouts, per_device(): past_inputs.reshape(HIST, -1, lanes)  1.96 us
    reshape x1, local copies, waits for them, and re-layouts, per_device(): current.reshape(-1, lanes)  1.84 us
    reshape x1, local copies, waits for them, and re-layouts, per_device(): mixed = fused_tail(scalars, chunks, current.reshape(-1, lanes), past_inpu...  1.8 us
  transfers between devices with their start and end apart: 2, of which 0 were waited for; matrix products, arithmetic and copies ran while one was open for 13% of the time, Pallas kernels for 0%

profile of v5, /device:TPU:1, one launch (start us, length us, event | category | flops | bytes accessed | tf_op | source)
XLA Modules:
  0.0 72.4 jit_solution(1629466355969785620)
XLA Ops:
  0.0 0.0 copy-start
  0.0 4.1 %collective-permute-start = (f32[2,2,2,64,128]{4,3,2,1,0:T(8,128)}, f32[2,2,2,64,128]{4,3,2,1,0:T(8,128)S(1)}, u32[]{:S(2)}, u32[]{:S(2)}) collective-permute-start(f32[2,2,2,64,128]{4,3,2,1,0:T(8,128)} %param.12), channel_id=1, source_target_pairs={{0,32},{32,64},{64,96},{96,128},{128,160},{160,192},{192,224},{224... | collective-permute-start | bytes 786440 | tf_op jit(solution)/shard_map/ppermute | solution.py:26
  4.1 5.6 %collective-permute-start.1 = (f32[2,2,2,64,128]{4,3,2,1,0:T(8,128)}, f32[2,2,2,64,128]{4,3,2,1,0:T(8,128)S(1)}, u32[]{:S(2)}, u32[]{:S(2)}) collective-permute-start(f32[2,2,2,64,128]{4,3,2,1,0:T(8,128)} %param.12), channel_id=1, source_target_pairs={{32,0},{64,32},{96,64},{128,96},{160,128},{192,160},{224,192},{256... | collective-permute-start | bytes 786440 | tf_op jit(solution)/shard_map/ppermute | solution.py:29
  9.7 0.7 add_select_fusion
  10.4 0.8 %select_reduce_fusion = f32[64,192]{1,0:T(8,128)S(1)} fusion(f32[5]{0:T(128)} %param.19, s32[64,5]{0,1:T(8,128)S(1)} %add_select_fusion), kind=kLoop, calls=%fused_computation.3 | loop fusion | flops 172032 | bytes 50452 | tf_op jit(solution)/shard_map/reduce_sum | solution.py:301
  11.3 0.1 fusion.5
  11.4 1.3 %fusion.3 = f32[32,2,8,128]{3,0,2,1:T(8,128)S(1)} fusion(f32[8,64,128,1]{2,1,0,3:T(8,128)} %bitcast.31, f32[32,2,64]{2,1,0:T(2,128)S(1)} %get-tuple-element.6), kind=kOutput, calls=%fused_computation.8 | convolution fusion | flops 50331648 | bytes 540672 | tf_op jit(solution)/shard_map/dkr,bre->dbke/dot_general | solution.py:314
  12.7 1.8 %reshape.34.cur_ref = f32[16,4096]{1,0:T(8,128)} reshape(f32[2,2,2,2,4096]{4,3,2,1,0:T(2,128)} %param.13) | data formatting | bytes 524288 | tf_op jit(solution)/shard_map/reshape | solution.py:327
  14.5 0.0 copy-done
  14.5 0.0 copy-start.1
  14.5 2.0 %reshape.35.pin_ref = f32[5,16,4096]{2,1,0:T(8,128)} reshape(f32[5,2,2,2,2,4096]{5,4,3,2,1,0:T(2,128)S(1)} %copy-done) | data formatting | bytes 2621440 | tf_op jit(solution)/shard_map/reshape | solution.py:328
  16.5 0.0 copy-done.1
  16.5 2.0 %reshape.36.pres_ref = f32[5,16,4096]{2,1,0:T(8,128)} reshape(f32[5,2,2,2,2,4096]{5,4,3,2,1,0:T(2,128)S(1)} %copy-done.1) | data formatting | bytes 2621440 | tf_op jit(solution)/shard_map/reshape | solution.py:329
  18.5 0.0 collective-permute-done.1
  18.5 0.4 fusion.2
  18.9 0.0 collective-permute-done
  18.9 0.4 fusion.1
  19.2 0.9 %copy.23 = f32[32,8,2,128]{3,2,1,0:T(2,128)} copy(f32[32,8,2,128]{3,0,1,2:T(8,128)S(1)} %fusion.1) | data formatting | bytes 524288 | tf_op jit(solution)/shard_map/add | solution.py:314
  20.1 50.5 %shard_map.118 = f32[16,4096]{1,0:T(8,128)} custom-call(s32[5]{0:T(128)} %slot_ref.1, s32[2]{0:T(128)} %shift_ref.1, s32[64]{0:T(128)} %class_ref.1, f32[2]{0:T(128)} %optical_ref.1, f32[2]{0:T(128)} %occ_ref.1, f32[4]{0:T(128)} %acoustic_ref.1, f32[32,16,128]{2,1,0:T(8,128)} %bitcast.30, f32[16,4096]{1,0:T(8,128)} %reshape.34.cur_ref, ...), custom_call_target="tpu_custom_call" | custom-call | tf_op jit(solution)/shard_map/pallas_call | solution.py:254
  70.6 1.8 %reshape.37 = f32[2,2,2,2,4096]{4,3,2,1,0:T(2,128)} reshape(f32[16,4096]{1,0:T(8,128)} %shard_map.118) | data formatting | bytes 524288 | tf_op jit(solution)/shard_map/reshape | solution.py:333
  (1 shorter events, 0.0 us)
Async XLA Ops:
  0.0 14.5 %copy-start = (f32[5,2,2,2,2,4096]{5,4,3,2,1,0:T(2,128)S(1)}, f32[5,2,2,2,2,4096]{5,4,3,2,1,0:T(2,128)}, u32[]{:S(2)}) copy-start(f32[5,2,2,2,2,4096]{5,4,3,2,1,0:T(2,128)} %param.14) | copy-start | bytes 3932164
  0.0 18.9 %collective-permute-start = (f32[2,2,2,64,128]{4,3,2,1,0:T(8,128)}, f32[2,2,2,64,128]{4,3,2,1,0:T(8,128)S(1)}, u32[]{:S(2)}, u32[]{:S(2)}) collective-permute-start(f32[2,2,2,64,128]{4,3,2,1,0:T(8,128)} %param.12), channel_id=1, source_target_pairs={{0,32},{32,64},{64,96},{96,128},{128,160},{160,192},{192,224},{224... | collective-permute-start | bytes 786440 | tf_op jit(solution)/shard_map/ppermute | solution.py:26
  4.1 14.4 %collective-permute-start.1 = (f32[2,2,2,64,128]{4,3,2,1,0:T(8,128)}, f32[2,2,2,64,128]{4,3,2,1,0:T(8,128)S(1)}, u32[]{:S(2)}, u32[]{:S(2)}) collective-permute-start(f32[2,2,2,64,128]{4,3,2,1,0:T(8,128)} %param.12), channel_id=1, source_target_pairs={{32,0},{64,32},{96,64},{128,96},{160,128},{192,160},{224,192},{256... | collective-permute-start | bytes 786440 | tf_op jit(solution)/shard_map/ppermute | solution.py:29
  14.5 2.0 %copy-start.1 = (f32[5,2,2,2,2,4096]{5,4,3,2,1,0:T(2,128)S(1)}, f32[5,2,2,2,2,4096]{5,4,3,2,1,0:T(2,128)}, u32[]{:S(2)}) copy-start(f32[5,2,2,2,2,4096]{5,4,3,2,1,0:T(2,128)} %param.15) | copy-start | bytes 3932164

commit v6 on v5

--- a/solution.py
+++ b/solution.py
@@ -126,7 +126,7 @@
     col = lax.broadcasted_iota(jnp.int32, shape, 1)
     prod = jnp.zeros(shape, jnp.float32)
     for i, j in pairs:
-        value = jnp.sum(vectors[i] * vectors[j], keepdims=True)
+        value = jnp.sum(vectors[i] * vectors[j]).reshape(1, 1)
         spot = ((row == i) & (col == j)) | ((row == j) & (col == i))
         prod = jnp.where(spot, value, prod)
     return prod
@@ -139,16 +139,16 @@
     mk = lax.axis_index("kgrp")
     me = lax.axis_index("energy")
     width = chunk_ref.shape[-1]
-    rows, padded_len = ypad.shape
+    lead, per_row, padded_len = ypad.shape
     length = padded_len - 2 * margin
     barrier = pltpu.get_barrier_semaphore()
     for s in range(nk - 1):
         pl.semaphore_signal(barrier, 1, device_id=((mk + s + 1) % nk, me), device_id_type=MESH)
     for s in range(ne - 1):
         pl.semaphore_signal(barrier, 1, device_id=(mk, (me + s + 1) % ne), device_id_type=MESH)
-    ypad[:, :margin] = jnp.zeros((rows, margin), jnp.float32)
-    ypad[:, margin + length :] = jnp.zeros((rows, margin), jnp.float32)
-    ypad[:, pl.ds(pl.multiple_of(margin + me * width, width), width)] = chunk_ref[me]
+    ypad[:, :, :margin] = jnp.zeros((lead, per_row, margin), jnp.float32)
+    ypad[:, :, margin + length :] = jnp.zeros((lead, per_row, margin), jnp.float32)
+    ypad[:, :, pl.ds(pl.multiple_of(margin + me * width, width), width)] = chunk_ref[me]
     pl.semaphore_wait(barrier, nk - 1 + ne - 1)
 
     copies = []
@@ -156,7 +156,7 @@
         peer = (me + s + 1) % ne
         c = pltpu.make_async_remote_copy(
             src_ref=chunk_ref.at[peer],
-            dst_ref=ypad.at[:, pl.ds(pl.multiple_of(margin + me * width, width), width)],
+            dst_ref=ypad.at[:, :, pl.ds(pl.multiple_of(margin + me * width, width), width)],
             send_sem=ts.at[s],
             recv_sem=tr.at[ne - 2 - s],
             device_id=(mk, peer),
@@ -164,13 +164,13 @@
         )
         c.start()
         copies.append(c)
-    history = [pres_ref[m] for m in range(HIST)]
+    history = [pres_ref[m * lead : (m + 1) * lead] for m in range(HIST)]
     gram = _pair_sums([None] + history, [(i, j) for i in range(1, HIST + 1) for j in range(i, HIST + 1)])
     for q in range(ne - 1):
         source = (me + q + 1) % ne
         pltpu.make_async_remote_copy(
             src_ref=chunk_ref.at[me],
-            dst_ref=ypad.at[:, pl.ds(pl.multiple_of(margin + source * width, width), width)],
+            dst_ref=ypad.at[:, :, pl.ds(pl.multiple_of(margin + source * width, width), width)],
             send_sem=ts.at[q],
             recv_sem=tr.at[q],
             device_id=(mk, source),
@@ -180,19 +180,18 @@
         copies[s].wait_send()
 
     y = ypad[...]
-    row = lax.broadcasted_iota(jnp.int32, (rows, 1), 0)
-    lesser = row < rows // 2
-    per_row = rows // 8
-    coupling = jnp.zeros((rows, 1), jnp.float32)
+    lesser = lax.broadcasted_iota(jnp.int32, (lead, 1, 1), 0) < lead // 2
+    row = lax.broadcasted_iota(jnp.int32, (1, per_row, 1), 1)
+    coupling = jnp.zeros((1, per_row, 1), jnp.float32)
     for r in range(per_row):
-        coupling = jnp.where(row % per_row == r, acoustic_ref[class_ref[me * per_row + r]], coupling)
-    sigma = coupling * y[:, margin : margin + length]
+        coupling = jnp.where(row == r, acoustic_ref[class_ref[me * per_row + r]], coupling)
+    sigma = coupling * y[:, :, margin : margin + length]
     for m in range(2):
         shift = shift_ref[m]
         strength = optical_ref[m]
         number = occ_ref[m]
-        ahead = pltpu.roll(y, padded_len - shift, 1)[:, margin : margin + length]
-        behind = pltpu.roll(y, shift, 1)[:, margin : margin + length]
+        ahead = pltpu.roll(y, padded_len - shift, 2)[:, :, margin : margin + length]
+        behind = pltpu.roll(y, shift, 2)[:, :, margin : margin + length]
         up = jnp.where(lesser, number + 1.0, number)
         down = jnp.where(lesser, number, number + 1.0)
         sigma = sigma + strength * (up * ahead + down * behind)
@@ -234,21 +233,25 @@
     weights = _weights_from_products(aged)[:, :1]
     row1 = lax.broadcasted_iota(jnp.int32, weights.shape, 0)
     slot_w = [None] * (HIST + 1)
+    row1 = lax.broadcasted_iota(jnp.int32, weights.shape, 0)
     for i in range(HIST + 1):
         w_i = _pick(row1 == i, weights, 0)
         for m in range(HIST + 1):
             term = jnp.where(perm[i] == m, w_i, 0.0)
             slot_w[m] = term if slot_w[m] is None else slot_w[m] + term
+    slot_w = [w.reshape(1, 1, 1) for w in slot_w]
     mixed = slot_w[0] * (cur_ref[...] + mixing_share * res)
     for m in range(HIST):
-        mixed = mixed + slot_w[m + 1] * (pin_ref[m] + mixing_share * pres_ref[m])
+        mixed = mixed + slot_w[m + 1] * (
+            pin_ref[m * lead : (m + 1) * lead] + mixing_share * history[m]
+        )
     out_ref[...] = mixed
 
 
 def fused_tail(scalars, chunks, cur, pin, pres, nk, ne, entries):
     tile = (8, 128)
     margin = 128
-    rows = chunks.shape[1]
+    lead, per_row = chunks.shape[1:3]
     smem = pl.BlockSpec(memory_space=pltpu.SMEM)
     vmem = pl.BlockSpec(memory_space=pltpu.VMEM)
     return pl.pallas_call(
@@ -257,7 +260,7 @@
         in_specs=[smem] * len(scalars) + [vmem] * 4,
         out_specs=vmem,
         scratch_shapes=[
-            pltpu.VMEM((rows, cur.shape[1] + 2 * margin), jnp.float32),
+            pltpu.VMEM((lead, per_row, cur.shape[-1] + 2 * margin), jnp.float32),
             pltpu.VMEM(tile, jnp.float32),
             pltpu.VMEM((nk - 1,) + tile, jnp.float32),
             pltpu.VMEM((ne - 1,) + tile, jnp.float32),
@@ -317,16 +320,15 @@
             flat(block),
             precision=lax.Precision.HIGHEST,
         )
-    chunks = chunks.reshape(ne, -1, greens.shape[4])
     lanes = current.shape[-1]
     entries = float(current.size * nk * ne)
     scalars = (slot_order, phonon_shift, momentum_class, optical_coupling, occupation, acoustic_coupling)
     mixed = fused_tail(
         scalars,
         chunks,
-        current.reshape(-1, lanes),
-        past_inputs.reshape(HIST, -1, lanes),
-        past_residuals.reshape(HIST, -1, lanes),
+        current.reshape(-1, rows_here, lanes),
+        past_inputs.reshape(-1, rows_here, lanes),
+        past_residuals.reshape(-1, rows_here, lanes),
         nk,
         ne,
         entries,

time: 72.7 us -> 75.5 us (1.039)
  Pallas kernels: 50.5 us -> 59 us
  local copies, waits for them, and re-layouts: 8.64 us -> 1.81 us
  other arithmetic: 1.48 us -> 2.75 us
    pallas_call x1, Pallas kernels: 50.5 us -> 59 us  [fused_tail(): pl.pallas_call(functools.partial(_fused_kernel, nk, ne, entries, margin),...]
    reshape x4 -> x0, local copies, waits for them, and re-layouts: 7.59 us -> none  [the longest x1 1.98 us: per_device(): past_residuals.reshape(HIST, -1, lanes)]
    unnamed x4 -> x1, local copies, waits for them, and re-layouts: 0.01 us -> 1.67 us
    add x0 -> x2, other arithmetic: none -> 1.27 us  [per_device(): chunks + jnp.einsum('dkr,bre->dbke', stencil[:, :, part * group_len:(part...]
    add x1 -> x0, local copies, waits for them, and re-layouts: 0.91 us -> none  [per_device(): chunks + jnp.einsum('dkr,bre->dbke', stencil[:, :, part * group_len:(part...]
  transfers between devices with their start and end apart: 2 -> 2, of which waited for: 0 -> 0; matrix products, arithmetic and copies ran while one was open for 13% -> 5% of each run, Pallas kernels for 0% -> 0%
where the time goes in v6:
time: 75.5 us; the launch traced here: 75.2 us
  Pallas kernels  59 us (78%)
  starting transfers between devices  9.58 us (13%)
  other arithmetic  2.75 us (4%)
  matrix products  2.02 us (3%)
  local copies, waits for them, and re-layouts  1.81 us (2%)
    pallas_call x1, Pallas kernels, fused_tail(): pl.pallas_call(functools.partial(_fused_kernel, nk, ne, entries, margin),...  59 us
    ppermute x1, starting transfers between devices, padded_2(): lax.ppermute(lax.slice_in_dim(block, 0, width, axis=dim), axis, backward)  5.64 us
    ppermute x1, starting transfers between devices, padded_2(): lax.ppermute(lax.slice_in_dim(block, block.shape[dim] - width, None, axis...  3.94 us
    dot_general x3, matrix products, per_device(): jnp.einsum('dkr,bre->dbke', stencil[:, :, part * group_len:(part + 1) * g...  2.02 us
    unnamed x1, local copies, waits for them, and re-layouts  1.67 us
  transfers between devices with their start and end apart: 2, of which 0 were waited for; matrix products, arithmetic and copies ran while one was open for 5% of the time, Pallas kernels for 0%

profile of v6, /device:TPU:1, one launch (start us, length us, event | category | flops | bytes accessed | tf_op | source)
XLA Modules:
  0.0 75.2 jit_solution(2157387922207718323)
XLA Ops:
  0.0 3.9 %collective-permute-start = (f32[2,2,2,64,128]{4,3,2,1,0:T(8,128)}, f32[2,2,2,64,128]{4,3,2,1,0:T(8,128)S(1)}, u32[]{:S(2)}, u32[]{:S(2)}) collective-permute-start(f32[2,2,2,64,128]{4,3,2,1,0:T(8,128)} %param.12), channel_id=1, source_target_pairs={{0,32},{32,64},{64,96},{96,128},{128,160},{160,192},{192,224},{224... | collective-permute-start | bytes 786440 | tf_op jit(solution)/shard_map/ppermute | solution.py:26
  3.9 5.6 %collective-permute-start.1 = (f32[2,2,2,64,128]{4,3,2,1,0:T(8,128)}, f32[2,2,2,64,128]{4,3,2,1,0:T(8,128)S(1)}, u32[]{:S(2)}, u32[]{:S(2)}) collective-permute-start(f32[2,2,2,64,128]{4,3,2,1,0:T(8,128)} %param.12), channel_id=1, source_target_pairs={{32,0},{64,32},{96,64},{128,96},{160,128},{192,160},{224,192},{256... | collective-permute-start | bytes 786440 | tf_op jit(solution)/shard_map/ppermute | solution.py:29
  9.6 0.7 add_select_fusion
  10.3 0.8 %select_reduce_fusion = f32[64,192]{1,0:T(8,128)S(1)} fusion(f32[5]{0:T(128)} %param.19, s32[64,5]{0,1:T(8,128)S(1)} %add_select_fusion), kind=kLoop, calls=%fused_computation | loop fusion | flops 172032 | bytes 50452 | tf_op jit(solution)/shard_map/reduce_sum | solution.py:304
  11.1 0.1 fusion.5
  11.2 1.3 %fusion.2 = f32[32,2,8,128]{3,0,2,1:T(8,128)S(1)} fusion(f32[8,64,128,1]{2,1,0,3:T(8,128)} %bitcast.36, f32[32,2,64]{2,1,0:T(2,128)S(1)} %get-tuple-element.6), kind=kOutput, calls=%fused_computation.8 | convolution fusion | flops 50331648 | bytes 540672 | tf_op jit(solution)/shard_map/dkr,bre->dbke/dot_general | solution.py:317
  12.5 0.0 collective-permute-done
  12.6 0.4 fusion.3
  12.9 0.3 copy_add_fusion.1
  13.2 0.0 collective-permute-done.1
  13.2 0.4 fusion.1
  13.6 1.0 %fusion.chunk_ref = f32[32,8,2,128]{3,2,1,0:T(2,128)} fusion(f32[32,2,8,128]{3,0,2,1:T(8,128)S(1)} %fusion.1, f32[32,2,8,128]{3,2,1,0:T(8,128)S(1)} %copy_add_fusion.1), kind=kLoop, calls=%fused_computation.3 | loop fusion | flops 65536 | bytes 786432 | tf_op jit(solution)/shard_map/add | solution.py:317
  14.6 59.0 %shard_map.118 = f32[8,2,4096]{2,1,0:T(2,128)} custom-call(s32[5]{0:T(128)} %slot_ref.1, s32[2]{0:T(128)} %shift_ref.1, s32[64]{0:T(128)} %class_ref.1, f32[2]{0:T(128)} %optical_ref.1, f32[2]{0:T(128)} %occ_ref.1, f32[4]{0:T(128)} %acoustic_ref.1, f32[32,8,2,128]{3,2,1,0:T(2,128)} %fusion.chunk_ref, f32[8,2,4096]{2,1,0:T(2,128)} %bitcast.39, ...), custom_call_target="tpu_custom_call" | custom-call | tf_op jit(solution)/shard_map/pallas_call | solution.py:257
  73.5 1.7 %copy.56 = f32[2,2,2,2,4096]{4,3,2,1,0:T(2,128)} copy(f32[2,2,2,2,4096]{4,3,2,1,0:T(2,128)} %bitcast.35) | data formatting | bytes 524288
  (1 shorter events, 0.0 us)
Async XLA Ops:
  0.0 12.5 %collective-permute-start = (f32[2,2,2,64,128]{4,3,2,1,0:T(8,128)}, f32[2,2,2,64,128]{4,3,2,1,0:T(8,128)S(1)}, u32[]{:S(2)}, u32[]{:S(2)}) collective-permute-start(f32[2,2,2,64,128]{4,3,2,1,0:T(8,128)} %param.12), channel_id=1, source_target_pairs={{0,32},{32,64},{64,96},{96,128},{128,160},{160,192},{192,224},{224... | collective-permute-start | bytes 786440 | tf_op jit(solution)/shard_map/ppermute | solution.py:26
  3.9 9.3 %collective-permute-start.1 = (f32[2,2,2,64,128]{4,3,2,1,0:T(8,128)}, f32[2,2,2,64,128]{4,3,2,1,0:T(8,128)S(1)}, u32[]{:S(2)}, u32[]{:S(2)}) collective-permute-start(f32[2,2,2,64,128]{4,3,2,1,0:T(8,128)} %param.12), channel_id=1, source_target_pairs={{32,0},{64,32},{96,64},{128,96},{160,128},{192,160},{224,192},{256... | collective-permute-start | bytes 786440 | tf_op jit(solution)/shard_map/ppermute | solution.py:29

commit v7 on v6

--- a/solution.py
+++ b/solution.py
@@ -135,7 +135,7 @@
 def _fused_kernel(nk, ne, entries, margin,
                   slot_ref, shift_ref, class_ref, optical_ref, occ_ref, acoustic_ref,
                   chunk_ref, cur_ref, pin_ref, pres_ref, out_ref,
-                  ypad, send1, recv1, recv2, acc1, ts, tr, ss1, rs1, ss2, rs2):
+                  ypad, bases, send1, recv1, recv2, acc1, ts, tr, ss1, rs1, ss2, rs2):
     mk = lax.axis_index("kgrp")
     me = lax.axis_index("energy")
     width = chunk_ref.shape[-1]
@@ -212,10 +212,13 @@
             )
             c.start()
             out.append(c)
-        for s in range(count - 1):
-            out[s].wait_recv()
-        for s in range(count - 1):
-            out[s].wait_send()
+        return out
+
+    def finish(out):
+        for c in out:
+            c.wait_recv()
+        for c in out:
+            c.wait_send()
 
     def total(own, recv, mine, count):
         acc = jnp.zeros_like(own)
@@ -224,9 +227,14 @@
             acc = acc + jnp.where(idx == mine, own, recv[slot])
         return acc
 
-    exchange(send1, recv1, ss1, rs1, nk, lambda s: ((mk + s + 1) % nk, me))
+    pending = exchange(send1, recv1, ss1, rs1, nk, lambda s: ((mk + s + 1) % nk, me))
+    for m in range(HIST):
+        bases[m + 1] = pin_ref[m * lead : (m + 1) * lead] + mixing_share * history[m]
+    finish(pending)
     acc1[...] = total(send1[...], recv1, mk, nk)
-    exchange(acc1, recv2, ss2, rs2, ne, lambda s: (mk, (me + s + 1) % ne))
+    pending = exchange(acc1, recv2, ss2, rs2, ne, lambda s: (mk, (me + s + 1) % ne))
+    bases[0] = cur_ref[...] + mixing_share * res
+    finish(pending)
     summed = total(acc1[...], recv2, me, ne)
     perm = [0] + [slot_ref[i] + 1 for i in range(HIST)]
     aged = _permute_square(summed / entries, perm)
@@ -240,11 +248,9 @@
             term = jnp.where(perm[i] == m, w_i, 0.0)
             slot_w[m] = term if slot_w[m] is None else slot_w[m] + term
     slot_w = [w.reshape(1, 1, 1) for w in slot_w]
-    mixed = slot_w[0] * (cur_ref[...] + mixing_share * res)
+    mixed = slot_w[0] * bases[0]
     for m in range(HIST):
-        mixed = mixed + slot_w[m + 1] * (
-            pin_ref[m * lead : (m + 1) * lead] + mixing_share * history[m]
-        )
+        mixed = mixed + slot_w[m + 1] * bases[m + 1]
     out_ref[...] = mixed
 
 
@@ -261,6 +267,7 @@
         out_specs=vmem,
         scratch_shapes=[
             pltpu.VMEM((lead, per_row, cur.shape[-1] + 2 * margin), jnp.float32),
+            pltpu.VMEM((HIST + 1,) + cur.shape, jnp.float32),
             pltpu.VMEM(tile, jnp.float32),
             pltpu.VMEM((nk - 1,) + tile, jnp.float32),
             pltpu.VMEM((ne - 1,) + tile, jnp.float32),

time: 75.5 us -> 75.3 us (level)
  no operation moved by 1% of the time
where the time goes in v7:
time: 75.3 us; the launch traced here: 75 us
  Pallas kernels  58.8 us (78%)
  starting transfers between devices  9.58 us (13%)
  other arithmetic  2.75 us (4%)
  matrix products  2.02 us (3%)
  local copies, waits for them, and re-layouts  1.81 us (2%)
    pallas_call x1, Pallas kernels, fused_tail(): pl.pallas_call(functools.partial(_fused_kernel, nk, ne, entries, margin),...  58.8 us
    ppermute x1, starting transfers between devices, padded_2(): lax.ppermute(lax.slice_in_dim(block, 0, width, axis=dim), axis, backward)  5.64 us
    ppermute x1, starting transfers between devices, padded_2(): lax.ppermute(lax.slice_in_dim(block, block.shape[dim] - width, None, axis...  3.94 us
    dot_general x3, matrix products, per_device(): jnp.einsum('dkr,bre->dbke', stencil[:, :, part * group_len:(part + 1) * g...  2.02 us
    unnamed x1, local copies, waits for them, and re-layouts  1.67 us
  transfers between devices with their start and end apart: 2, of which 0 were waited for; matrix products, arithmetic and copies ran while one was open for 5% of the time, Pallas kernels for 0%

profile of v7, /device:TPU:1, one launch (start us, length us, event | category | flops | bytes accessed | tf_op | source)
XLA Modules:
  0.0 75.0 jit_solution(16444705761125897110)
XLA Ops:
  0.0 3.9 %collective-permute-start = (f32[2,2,2,64,128]{4,3,2,1,0:T(8,128)}, f32[2,2,2,64,128]{4,3,2,1,0:T(8,128)S(1)}, u32[]{:S(2)}, u32[]{:S(2)}) collective-permute-start(f32[2,2,2,64,128]{4,3,2,1,0:T(8,128)} %param.12), channel_id=1, source_target_pairs={{0,32},{32,64},{64,96},{96,128},{128,160},{160,192},{192,224},{224... | collective-permute-start | bytes 786440 | tf_op jit(solution)/shard_map/ppermute | solution.py:26
  3.9 5.6 %collective-permute-start.1 = (f32[2,2,2,64,128]{4,3,2,1,0:T(8,128)}, f32[2,2,2,64,128]{4,3,2,1,0:T(8,128)S(1)}, u32[]{:S(2)}, u32[]{:S(2)}) collective-permute-start(f32[2,2,2,64,128]{4,3,2,1,0:T(8,128)} %param.12), channel_id=1, source_target_pairs={{32,0},{64,32},{96,64},{128,96},{160,128},{192,160},{224,192},{256... | collective-permute-start | bytes 786440 | tf_op jit(solution)/shard_map/ppermute | solution.py:29
  9.6 0.7 add_select_fusion
  10.3 0.8 %select_reduce_fusion = f32[64,192]{1,0:T(8,128)S(1)} fusion(f32[5]{0:T(128)} %param.19, s32[64,5]{0,1:T(8,128)S(1)} %add_select_fusion), kind=kLoop, calls=%fused_computation | loop fusion | flops 172032 | bytes 50452 | tf_op jit(solution)/shard_map/reduce_sum | solution.py:311
  11.1 0.1 fusion.5
  11.2 1.3 %fusion.2 = f32[32,2,8,128]{3,0,2,1:T(8,128)S(1)} fusion(f32[8,64,128,1]{2,1,0,3:T(8,128)} %bitcast.36, f32[32,2,64]{2,1,0:T(2,128)S(1)} %get-tuple-element.6), kind=kOutput, calls=%fused_computation.8 | convolution fusion | flops 50331648 | bytes 540672 | tf_op jit(solution)/shard_map/dkr,bre->dbke/dot_general | solution.py:324
  12.5 0.0 collective-permute-done
  12.6 0.4 fusion.3
  12.9 0.3 copy_add_fusion.1
  13.2 0.0 collective-permute-done.1
  13.2 0.4 fusion.1
  13.6 1.0 %fusion.chunk_ref = f32[32,8,2,128]{3,2,1,0:T(2,128)} fusion(f32[32,2,8,128]{3,0,2,1:T(8,128)S(1)} %fusion.1, f32[32,2,8,128]{3,2,1,0:T(8,128)S(1)} %copy_add_fusion.1), kind=kLoop, calls=%fused_computation.3 | loop fusion | flops 65536 | bytes 786432 | tf_op jit(solution)/shard_map/add | solution.py:324
  14.6 58.8 %shard_map.118 = f32[8,2,4096]{2,1,0:T(2,128)} custom-call(s32[5]{0:T(128)} %slot_ref.1, s32[2]{0:T(128)} %shift_ref.1, s32[64]{0:T(128)} %class_ref.1, f32[2]{0:T(128)} %optical_ref.1, f32[2]{0:T(128)} %occ_ref.1, f32[4]{0:T(128)} %acoustic_ref.1, f32[32,8,2,128]{3,2,1,0:T(2,128)} %fusion.chunk_ref, f32[8,2,4096]{2,1,0:T(2,128)} %bitcast.39, ...), custom_call_target="tpu_custom_call" | custom-call | tf_op jit(solution)/shard_map/pallas_call | solution.py:263
  73.4 1.7 %copy.56 = f32[2,2,2,2,4096]{4,3,2,1,0:T(2,128)} copy(f32[2,2,2,2,4096]{4,3,2,1,0:T(2,128)} %bitcast.35) | data formatting | bytes 524288
  (1 shorter events, 0.0 us)
Async XLA Ops:
  0.0 12.5 %collective-permute-start = (f32[2,2,2,64,128]{4,3,2,1,0:T(8,128)}, f32[2,2,2,64,128]{4,3,2,1,0:T(8,128)S(1)}, u32[]{:S(2)}, u32[]{:S(2)}) collective-permute-start(f32[2,2,2,64,128]{4,3,2,1,0:T(8,128)} %param.12), channel_id=1, source_target_pairs={{0,32},{32,64},{64,96},{96,128},{128,160},{160,192},{192,224},{224... | collective-permute-start | bytes 786440 | tf_op jit(solution)/shard_map/ppermute | solution.py:26
  3.9 9.3 %collective-permute-start.1 = (f32[2,2,2,64,128]{4,3,2,1,0:T(8,128)}, f32[2,2,2,64,128]{4,3,2,1,0:T(8,128)S(1)}, u32[]{:S(2)}, u32[]{:S(2)}) collective-permute-start(f32[2,2,2,64,128]{4,3,2,1,0:T(8,128)} %param.12), channel_id=1, source_target_pairs={{32,0},{64,32},{96,64},{128,96},{160,128},{192,160},{224,192},{256... | collective-permute-start | bytes 786440 | tf_op jit(solution)/shard_map/ppermute | solution.py:29

commit v8 on v7

--- a/solution.py
+++ b/solution.py
@@ -135,20 +135,22 @@
 def _fused_kernel(nk, ne, entries, margin,
                   slot_ref, shift_ref, class_ref, optical_ref, occ_ref, acoustic_ref,
                   chunk_ref, cur_ref, pin_ref, pres_ref, out_ref,
-                  ypad, bases, send1, recv1, recv2, acc1, ts, tr, ss1, rs1, ss2, rs2):
+                  ypad, cur16, hist16, bases, send1, recv1, recv2, acc1, ts, tr, ss1, rs1, ss2, rs2):
     mk = lax.axis_index("kgrp")
     me = lax.axis_index("energy")
     width = chunk_ref.shape[-1]
-    lead, per_row, padded_len = ypad.shape
+    rows, padded_len = ypad.shape
+    lead = cur_ref.shape[0]
+    per_row = rows // lead
     length = padded_len - 2 * margin
     barrier = pltpu.get_barrier_semaphore()
     for s in range(nk - 1):
         pl.semaphore_signal(barrier, 1, device_id=((mk + s + 1) % nk, me), device_id_type=MESH)
     for s in range(ne - 1):
         pl.semaphore_signal(barrier, 1, device_id=(mk, (me + s + 1) % ne), device_id_type=MESH)
-    ypad[:, :, :margin] = jnp.zeros((lead, per_row, margin), jnp.float32)
-    ypad[:, :, margin + length :] = jnp.zeros((lead, per_row, margin), jnp.float32)
-    ypad[:, :, pl.ds(pl.multiple_of(margin + me * width, width), width)] = chunk_ref[me]
+    ypad[:, :margin] = jnp.zeros((rows, margin), jnp.float32)
+    ypad[:, margin + length :] = jnp.zeros((rows, margin), jnp.float32)
+    ypad[:, pl.ds(pl.multiple_of(margin + me * width, width), width)] = chunk_ref[me]
     pl.semaphore_wait(barrier, nk - 1 + ne - 1)
 
     copies = []
@@ -156,7 +158,7 @@
         peer = (me + s + 1) % ne
         c = pltpu.make_async_remote_copy(
             src_ref=chunk_ref.at[peer],
-            dst_ref=ypad.at[:, :, pl.ds(pl.multiple_of(margin + me * width, width), width)],
+            dst_ref=ypad.at[:, pl.ds(pl.multiple_of(margin + me * width, width), width)],
             send_sem=ts.at[s],
             recv_sem=tr.at[ne - 2 - s],
             device_id=(mk, peer),
@@ -165,12 +167,16 @@
         c.start()
         copies.append(c)
     history = [pres_ref[m * lead : (m + 1) * lead] for m in range(HIST)]
-    gram = _pair_sums([None] + history, [(i, j) for i in range(1, HIST + 1) for j in range(i, HIST + 1)])
+    cur16[...] = cur_ref[...].reshape(rows, length)
+    for m in range(HIST):
+        hist16[m] = history[m].reshape(rows, length)
+    flat_hist = [hist16[m] for m in range(HIST)]
+    gram = _pair_sums([None] + flat_hist, [(i, j) for i in range(1, HIST + 1) for j in range(i, HIST + 1)])
     for q in range(ne - 1):
         source = (me + q + 1) % ne
         pltpu.make_async_remote_copy(
             src_ref=chunk_ref.at[me],
-            dst_ref=ypad.at[:, :, pl.ds(pl.multiple_of(margin + source * width, width), width)],
+            dst_ref=ypad.at[:, pl.ds(pl.multiple_of(margin + source * width, width), width)],
             send_sem=ts.at[q],
             recv_sem=tr.at[q],
             device_id=(mk, source),
@@ -180,23 +186,23 @@
         copies[s].wait_send()
 
     y = ypad[...]
-    lesser = lax.broadcasted_iota(jnp.int32, (lead, 1, 1), 0) < lead // 2
-    row = lax.broadcasted_iota(jnp.int32, (1, per_row, 1), 1)
-    coupling = jnp.zeros((1, per_row, 1), jnp.float32)
+    row = lax.broadcasted_iota(jnp.int32, (rows, 1), 0)
+    lesser = row < rows // 2
+    coupling = jnp.zeros((rows, 1), jnp.float32)
     for r in range(per_row):
-        coupling = jnp.where(row == r, acoustic_ref[class_ref[me * per_row + r]], coupling)
-    sigma = coupling * y[:, :, margin : margin + length]
+        coupling = jnp.where(row % per_row == r, acoustic_ref[class_ref[me * per_row + r]], coupling)
+    sigma = coupling * y[:, margin : margin + length]
     for m in range(2):
         shift = shift_ref[m]
         strength = optical_ref[m]
         number = occ_ref[m]
-        ahead = pltpu.roll(y, padded_len - shift, 2)[:, :, margin : margin + length]
-        behind = pltpu.roll(y, shift, 2)[:, :, margin : margin + length]
+        ahead = pltpu.roll(y, padded_len - shift, 1)[:, margin : margin + length]
+        behind = pltpu.roll(y, shift, 1)[:, margin : margin + length]
         up = jnp.where(lesser, number + 1.0, number)
         down = jnp.where(lesser, number, number + 1.0)
         sigma = sigma + strength * (up * ahead + down * behind)
-    res = sigma - cur_ref[...]
-    fresh = _pair_sums([res] + history, [(0, j) for j in range(HIST + 1)])
+    res = sigma - cur16[...]
+    fresh = _pair_sums([res] + [hist16[m] for m in range(HIST)], [(0, j) for j in range(HIST + 1)])
     send1[...] = fresh + gram
 
     def exchange(src, recv, ssem, rsem, count, peer):
@@ -233,7 +239,7 @@
     finish(pending)
     acc1[...] = total(send1[...], recv1, mk, nk)
     pending = exchange(acc1, recv2, ss2, rs2, ne, lambda s: (mk, (me + s + 1) % ne))
-    bases[0] = cur_ref[...] + mixing_share * res
+    bases[0] = (cur16[...] + mixing_share * res).reshape(cur_ref.shape)
     finish(pending)
     summed = total(acc1[...], recv2, me, ne)
     perm = [0] + [slot_ref[i] + 1 for i in range(HIST)]
@@ -257,7 +263,7 @@
 def fused_tail(scalars, chunks, cur, pin, pres, nk, ne, entries):
     tile = (8, 128)
     margin = 128
-    lead, per_row = chunks.shape[1:3]
+    rows = chunks.shape[1]
     smem = pl.BlockSpec(memory_space=pltpu.SMEM)
     vmem = pl.BlockSpec(memory_space=pltpu.VMEM)
     return pl.pallas_call(
@@ -266,7 +272,9 @@
         in_specs=[smem] * len(scalars) + [vmem] * 4,
         out_specs=vmem,
         scratch_shapes=[
-            pltpu.VMEM((lead, per_row, cur.shape[-1] + 2 * margin), jnp.float32),
+            pltpu.VMEM((rows, cur.shape[-1] + 2 * margin), jnp.float32),
+            pltpu.VMEM((rows, cur.shape[-1]), jnp.float32),
+            pltpu.VMEM((HIST, rows, cur.shape[-1]), jnp.float32),
             pltpu.VMEM((HIST + 1,) + cur.shape, jnp.float32),
             pltpu.VMEM(tile, jnp.float32),
             pltpu.VMEM((nk - 1,) + tile, jnp.float32),
@@ -327,6 +335,7 @@
             flat(block),
             precision=lax.Precision.HIGHEST,
         )
+    chunks = chunks.reshape(ne, -1, greens.shape[4])
     lanes = current.shape[-1]
     entries = float(current.size * nk * ne)
     scalars = (slot_order, phonon_shift, momentum_class, optical_coupling, occupation, acoustic_coupling)

time: 75.3 us -> 73.7 us (0.979)
  Pallas kernels: 58.8 us -> 50.7 us
  waiting for transfers between devices: 0.01 us -> 6.84 us
  other arithmetic: 2.75 us -> 1.48 us
  local copies, waits for them, and re-layouts: 1.81 us -> 2.72 us
    pallas_call x1, Pallas kernels: 58.8 us -> 50.7 us  [fused_tail(): pl.pallas_call(functools.partial(_fused_kernel, nk, ne, entries, margin),...]
    ppermute x1, waiting for transfers between devices: 0.01 us -> 6.66 us  [padded_2(): lax.ppermute(lax.slice_in_dim(block, block.shape[dim] - width, None, axis...]
    ppermute x1, starting transfers between devices: 3.94 us -> 1.92 us  [padded_2(): lax.ppermute(lax.slice_in_dim(block, block.shape[dim] - width, None, axis...]
    ppermute x1, starting transfers between devices: 5.64 us -> 7.66 us  [padded_2(): lax.ppermute(lax.slice_in_dim(block, 0, width, axis=dim), axis, backward)]
    add x2 -> x0, other arithmetic: 1.27 us -> none  [per_device(): chunks + jnp.einsum('dkr,bre->dbke', stencil[:, :, part * group_len:(part...]
    add x0 -> x1, local copies, waits for them, and re-layouts: none -> 0.91 us  [per_device(): chunks + jnp.einsum('dkr,bre->dbke', stencil[:, :, part * group_len:(part...]
  transfers between devices with their start and end apart: 2 -> 2, of which waited for: 0 -> 2; matrix products, arithmetic and copies ran while one was open for 5% -> 4% of each run, Pallas kernels for 0% -> 0%
where the time goes in v8:
time: 73.7 us; the launch traced here: 73.4 us
  Pallas kernels  50.7 us (69%)
  starting transfers between devices  9.58 us (13%)
  waiting for transfers between devices  6.84 us (9%)
  local copies, waits for them, and re-layouts  2.72 us (4%)
  matrix products  2.03 us (3%)
  other arithmetic  1.48 us (2%)
    pallas_call x1, Pallas kernels, fused_tail(): pl.pallas_call(functools.partial(_fused_kernel, nk, ne, entries, margin),...  50.7 us
    ppermute x1, starting transfers between devices, padded_2(): lax.ppermute(lax.slice_in_dim(block, 0, width, axis=dim), axis, backward)  7.66 us
    ppermute x1, waiting for transfers between devices, padded_2(): lax.ppermute(lax.slice_in_dim(block, block.shape[dim] - width, None, axis...  6.66 us
    dot_general x3, matrix products, per_device(): jnp.einsum('dkr,bre->dbke', stencil[:, :, part * group_len:(part + 1) * g...  2.03 us
    ppermute x1, starting transfers between devices, padded_2(): lax.ppermute(lax.slice_in_dim(block, block.shape[dim] - width, None, axis...  1.92 us
    unnamed x1, local copies, waits for them, and re-layouts  1.67 us
  transfers between devices with their start and end apart: 2, of which 2 were waited for; matrix products, arithmetic and copies ran while one was open for 4% of the time, Pallas kernels for 0%

profile of v8, /device:TPU:1, one launch (start us, length us, event | category | flops | bytes accessed | tf_op | source)
XLA Modules:
  0.0 73.4 jit_solution(10662671300803354047)
XLA Ops:
  0.0 7.7 %collective-permute-start.1 = (f32[2,2,2,64,128]{4,3,2,1,0:T(8,128)}, f32[2,2,2,64,128]{4,3,2,1,0:T(8,128)S(1)}, u32[]{:S(2)}, u32[]{:S(2)}) collective-permute-start(f32[2,2,2,64,128]{4,3,2,1,0:T(8,128)} %param.12), channel_id=1, source_target_pairs={{32,0},{64,32},{96,64},{128,96},{160,128},{192,160},{224,192},{256... | collective-permute-start | bytes 786440 | tf_op jit(solution)/shard_map/ppermute | solution.py:29
  7.7 1.9 %collective-permute-start = (f32[2,2,2,64,128]{4,3,2,1,0:T(8,128)}, f32[2,2,2,64,128]{4,3,2,1,0:T(8,128)S(1)}, u32[]{:S(2)}, u32[]{:S(2)}) collective-permute-start(f32[2,2,2,64,128]{4,3,2,1,0:T(8,128)} %param.12), channel_id=1, source_target_pairs={{0,32},{32,64},{64,96},{96,128},{128,160},{160,192},{192,224},{224... | collective-permute-start | bytes 786440 | tf_op jit(solution)/shard_map/ppermute | solution.py:26
  9.6 0.7 add_select_fusion
  10.3 0.8 %select_reduce_fusion = f32[64,192]{1,0:T(8,128)S(1)} fusion(f32[5]{0:T(128)} %param.19, s32[64,5]{0,1:T(8,128)S(1)} %add_select_fusion), kind=kLoop, calls=%fused_computation.3 | loop fusion | flops 172032 | bytes 50452 | tf_op jit(solution)/shard_map/reduce_sum | solution.py:319
  11.1 0.1 fusion.5
  11.2 1.3 %fusion.3 = f32[32,2,8,128]{3,0,2,1:T(8,128)S(1)} fusion(f32[8,64,128,1]{2,1,0,3:T(8,128)} %bitcast.38, f32[32,2,64]{2,1,0:T(2,128)S(1)} %get-tuple-element.6), kind=kOutput, calls=%fused_computation.8 | convolution fusion | flops 50331648 | bytes 540672 | tf_op jit(solution)/shard_map/dkr,bre->dbke/dot_general | solution.py:332
  12.5 0.2 collective-permute-done.1
  12.7 0.4 fusion.2
  13.1 6.7 %collective-permute-done = f32[2,2,2,64,128]{4,3,2,1,0:T(8,128)S(1)} collective-permute-done((f32[2,2,2,64,128]{4,3,2,1,0:T(8,128)}, f32[2,2,2,64,128]{4,3,2,1,0:T(8,128)S(1)}, u32[]{:S(2)}, u32[]{:S(2)}) %collective-permute-start) | collective-permute-done | bytes 262176 | tf_op jit(solution)/shard_map/ppermute | solution.py:26
  19.8 0.4 fusion.1
  20.1 0.9 %copy.23 = f32[32,8,2,128]{3,2,1,0:T(2,128)} copy(f32[32,8,2,128]{3,0,1,2:T(8,128)S(1)} %fusion.1) | data formatting | bytes 524288 | tf_op jit(solution)/shard_map/add | solution.py:332
  21.0 50.7 %shard_map.118 = f32[8,2,4096]{2,1,0:T(2,128)} custom-call(s32[5]{0:T(128)} %slot_ref.1, s32[2]{0:T(128)} %shift_ref.1, s32[64]{0:T(128)} %class_ref.1, f32[2]{0:T(128)} %optical_ref.1, f32[2]{0:T(128)} %occ_ref.1, f32[4]{0:T(128)} %acoustic_ref.1, f32[32,16,128]{2,1,0:T(8,128)} %bitcast.36, f32[8,2,4096]{2,1,0:T(2,128)} %bitcast.41, ...), custom_call_target="tpu_custom_call" | custom-call | tf_op jit(solution)/shard_map/pallas_call | solution.py:269
  71.8 1.7 %copy.37 = f32[2,2,2,2,4096]{4,3,2,1,0:T(2,128)} copy(f32[2,2,2,2,4096]{4,3,2,1,0:T(2,128)} %bitcast.37) | data formatting | bytes 524288
  (1 shorter events, 0.0 us)
Async XLA Ops:
  0.0 12.7 %collective-permute-start.1 = (f32[2,2,2,64,128]{4,3,2,1,0:T(8,128)}, f32[2,2,2,64,128]{4,3,2,1,0:T(8,128)S(1)}, u32[]{:S(2)}, u32[]{:S(2)}) collective-permute-start(f32[2,2,2,64,128]{4,3,2,1,0:T(8,128)} %param.12), channel_id=1, source_target_pairs={{32,0},{64,32},{96,64},{128,96},{160,128},{192,160},{224,192},{256... | collective-permute-start | bytes 786440 | tf_op jit(solution)/shard_map/ppermute | solution.py:29
  7.7 12.1 %collective-permute-start = (f32[2,2,2,64,128]{4,3,2,1,0:T(8,128)}, f32[2,2,2,64,128]{4,3,2,1,0:T(8,128)S(1)}, u32[]{:S(2)}, u32[]{:S(2)}) collective-permute-start(f32[2,2,2,64,128]{4,3,2,1,0:T(8,128)} %param.12), channel_id=1, source_target_pairs={{0,32},{32,64},{64,96},{96,128},{128,160},{160,192},{192,224},{224... | collective-permute-start | bytes 786440 | tf_op jit(solution)/shard_map/ppermute | solution.py:26

commit v9 on v8

--- a/solution.py
+++ b/solution.py
@@ -132,6 +132,44 @@
     return prod
 
 
+def _halo_kernel(nk, x_ref, low_ref, high_ref, ssem, rsem):
+    mk = lax.axis_index("kgrp")
+    me = lax.axis_index("energy")
+    before = (mk + nk - 1) % nk
+    after = (mk + 1) % nk
+    barrier = pltpu.get_barrier_semaphore()
+    pl.semaphore_signal(barrier, 1, device_id=(before, me), device_id_type=MESH)
+    pl.semaphore_signal(barrier, 1, device_id=(after, me), device_id_type=MESH)
+    pl.semaphore_wait(barrier, 2)
+    to_before = pltpu.make_async_remote_copy(
+        src_ref=x_ref, dst_ref=high_ref, send_sem=ssem.at[0], recv_sem=rsem.at[1],
+        device_id=(before, me), device_id_type=MESH,
+    )
+    to_after = pltpu.make_async_remote_copy(
+        src_ref=x_ref, dst_ref=low_ref, send_sem=ssem.at[1], recv_sem=rsem.at[0],
+        device_id=(after, me), device_id_type=MESH,
+    )
+    to_before.start()
+    to_after.start()
+    to_after.wait_recv()
+    to_before.wait_recv()
+    to_before.wait_send()
+    to_after.wait_send()
+
+
+def halo(block, nk):
+    vmem = pl.BlockSpec(memory_space=pltpu.VMEM)
+    shape = jax.ShapeDtypeStruct(block.shape, jnp.float32)
+    return pl.pallas_call(
+        functools.partial(_halo_kernel, nk),
+        out_shape=(shape, shape),
+        in_specs=[vmem],
+        out_specs=(vmem, vmem),
+        scratch_shapes=[pltpu.SemaphoreType.DMA((2,)), pltpu.SemaphoreType.DMA((2,))],
+        compiler_params=pltpu.CompilerParams(collective_id=1, has_side_effects=True),
+    )(block)
+
+
 def _fused_kernel(nk, ne, entries, margin,
                   slot_ref, shift_ref, class_ref, optical_ref, occ_ref, acoustic_ref,
                   chunk_ref, cur_ref, pin_ref, pres_ref, out_ref,
@@ -312,9 +350,7 @@
     nk = lax.axis_size("kgrp")
     ne = lax.axis_size("energy")
     total_k = group_len * nk
-    ends = padded_2(greens, (("kgrp", 3),), group_len, True)
-    low = ends[:, :, :, :group_len]
-    high = ends[:, :, :, 2 * group_len :]
+    low, high = halo(greens.reshape((-1,) + greens.shape[3:]), nk)
     local_index = (neighbour - group_id * group_len + group_len) % total_k
     stencil = jnp.sum(
         jnp.where(
@@ -328,7 +364,7 @@
     flat = lambda x: x.reshape((-1,) + x.shape[3:])
     stencil = stencil.reshape(ne, rows_here, 3 * group_len)
     chunks = jnp.zeros((ne, flat(greens).shape[0], rows_here, greens.shape[4]), jnp.float32)
-    for part, block in enumerate((low, greens, high)):
+    for part, block in enumerate((low.reshape(greens.shape), greens, high.reshape(greens.shape))):
         chunks = chunks + jnp.einsum(
             "dkr,bre->dbke",
             stencil[:, :, part * group_len : (part + 1) * group_len],

time: 73.7 us -> 73.7 us (level)
  Pallas kernels: 50.7 us -> 67.1 us
  starting transfers between devices: 9.58 us -> 0 us
  waiting for transfers between devices: 6.84 us -> 0 us
    pallas_call x0 -> x1, Pallas kernels: none -> 13 us  [halo(): pl.pallas_call(functools.partial(_halo_kernel, nk), out_shape=(shape, sha...]
    ppermute x2 -> x0, starting transfers between devices: 9.58 us -> none  [the longest x1 7.66 us: padded_2(): lax.ppermute(lax.slice_in_dim(block, 0, width, axis=dim), axis, backward)]
    ppermute x2 -> x0, waiting for transfers between devices: 6.84 us -> none  [the longest x1 6.66 us: padded_2(): lax.ppermute(lax.slice_in_dim(block, block.shape[dim] - width, None, axis...]
    pallas_call x1, Pallas kernels: 50.7 us -> 54.1 us  [fused_tail(): pl.pallas_call(functools.partial(_fused_kernel, nk, ne, entries, margin),...]
    unnamed x1 -> x5, local copies, waits for them, and re-layouts: 1.67 us -> 1.68 us
  transfers between devices with their start and end apart: 2 -> 0, of which waited for: 2 -> 0; matrix products, arithmetic and copies ran while one was open for 4% -> 0% of each run, Pallas kernels for 0% -> 0%
where the time goes in v9:
time: 73.7 us; the launch traced here: 73.5 us
  Pallas kernels  67.1 us (91%)
  local copies, waits for them, and re-layouts  2.73 us (4%)
  matrix products  2.07 us (3%)
  other arithmetic  1.52 us (2%)
    pallas_call x1, Pallas kernels, fused_tail(): pl.pallas_call(functools.partial(_fused_kernel, nk, ne, entries, margin),...  54.1 us
    pallas_call x1, Pallas kernels, halo(): pl.pallas_call(functools.partial(_halo_kernel, nk), out_shape=(shape, sha...  13 us
    dot_general x3, matrix products, per_device(): jnp.einsum('dkr,bre->dbke', stencil[:, :, part * group_len:(part + 1) * g...  2.07 us
    unnamed x5, local copies, waits for them, and re-layouts  1.68 us

profile of v9, /device:TPU:1, one launch (start us, length us, event | category | flops | bytes accessed | tf_op | source)
XLA Modules:
  0.0 73.5 jit_solution(1111033454374228932)
XLA Ops:
  0.0 0.0 copy-start
  0.0 0.7 %add_select_fusion = s32[64,5]{0,1:T(8,128)S(1)} fusion(s32[64,5]{0,1:T(8,128)} %param.17, s32[]{:T(128)S(6)} %mul.3), kind=kLoop, calls=%fused_computation.11 | loop fusion | flops 4160 | bytes 2564 | tf_op jit(solution)/shard_map/jit(remainder)/select_n | solution.py:354
  0.7 0.8 %select_reduce_fusion = f32[64,192]{1,0:T(8,128)S(1)} fusion(f32[5]{0:T(128)} %param.19, s32[64,5]{0,1:T(8,128)S(1)} %add_select_fusion), kind=kLoop, calls=%fused_computation.3 | loop fusion | flops 172032 | bytes 50452 | tf_op jit(solution)/shard_map/reduce_sum | solution.py:355
  1.6 0.1 fusion.5
  1.7 13.0 %shard_map.118 = (f32[8,64,128]{2,1,0:T(8,128)}, f32[8,64,128]{2,1,0:T(8,128)}) custom-call(f32[8,64,128]{2,1,0:T(8,128)} %bitcast.34), custom_call_target="tpu_custom_call" | custom-call | tf_op jit(solution)/shard_map/pallas_call | solution.py:163
  14.7 0.0 copy-start.1
  14.7 1.3 %fusion.2 = f32[32,2,8,128]{3,0,2,1:T(8,128)S(1)} fusion(f32[8,64,128]{2,1,0:T(8,128)} %get-tuple-element.7, f32[32,2,64]{2,1,0:T(2,128)S(1)} %get-tuple-element.11), kind=kOutput, calls=%fused_computation.6 | convolution fusion | flops 50331648 | bytes 540672 | tf_op jit(solution)/shard_map/dkr,bre->dbke/dot_general | solution.py:368
  16.0 0.0 copy-done
  16.1 0.4 convolution_add_fusion.1
  16.4 0.0 copy-done.1
  16.4 0.4 fusion
  16.8 0.9 %copy.23 = f32[32,8,2,128]{3,2,1,0:T(2,128)} copy(f32[32,8,2,128]{3,0,1,2:T(8,128)S(1)} %fusion) | data formatting | bytes 524288 | tf_op jit(solution)/shard_map/add | solution.py:368
  17.7 54.1 %shard_map.119 = f32[8,2,4096]{2,1,0:T(2,128)} custom-call(s32[5]{0:T(128)} %slot_ref.1, s32[2]{0:T(128)} %shift_ref.1, s32[64]{0:T(128)} %class_ref.1, f32[2]{0:T(128)} %optical_ref.1, f32[2]{0:T(128)} %occ_ref.1, f32[4]{0:T(128)} %acoustic_ref.1, f32[32,16,128]{2,1,0:T(8,128)} %bitcast.36, f32[8,2,4096]{2,1,0:T(2,128)} %bitcast.38, ...), custom_call_target="tpu_custom_call" | custom-call | tf_op jit(solution)/shard_map/pallas_call | solution.py:307
  71.8 1.7 %copy.37 = f32[2,2,2,2,4096]{4,3,2,1,0:T(2,128)} copy(f32[2,2,2,2,4096]{4,3,2,1,0:T(2,128)} %bitcast.37) | data formatting | bytes 524288
  (1 shorter events, 0.0 us)
Async XLA Ops:
  0.0 16.0 %copy-start = (f32[2,2,2,64,128]{4,3,2,1,0:T(8,128)S(1)}, f32[2,2,2,64,128]{4,3,2,1,0:T(8,128)}, u32[]{:S(2)}) copy-start(f32[2,2,2,64,128]{4,3,2,1,0:T(8,128)} %param.12) | copy-start | bytes 786436
  14.7 1.7 %copy-start.1 = (f32[8,64,128]{2,1,0:T(8,128)S(1)}, f32[8,64,128]{2,1,0:T(8,128)}, u32[]{:S(2)}) copy-start(f32[8,64,128]{2,1,0:T(8,128)} %get-tuple-element.8) | copy-start | bytes 786436

commit v10 on v5

--- a/solution.py
+++ b/solution.py
@@ -132,6 +132,25 @@
     return prod
 
 
+def _pack_rows(prod):
+    row = lax.broadcasted_iota(jnp.int32, prod.shape, 0)
+    packed = jnp.zeros((1, prod.shape[1]), jnp.float32)
+    for i in range(HIST + 1):
+        packed = packed + pltpu.roll(_pick(row == i, prod, 0), 8 * i, 1)
+    return packed
+
+
+def _unpack_rows(packed):
+    shape = (8, packed.shape[1])
+    row = lax.broadcasted_iota(jnp.int32, shape, 0)
+    col = lax.broadcasted_iota(jnp.int32, shape, 1)
+    prod = jnp.zeros(shape, jnp.float32)
+    for i in range(HIST + 1):
+        line = pltpu.roll(packed, (shape[1] - 8 * i) % shape[1], 1)
+        prod = jnp.where((row == i) & (col <= HIST), line, prod)
+    return prod
+
+
 def _fused_kernel(nk, ne, entries, margin,
                   slot_ref, shift_ref, class_ref, optical_ref, occ_ref, acoustic_ref,
                   chunk_ref, cur_ref, pin_ref, pres_ref, out_ref,
@@ -198,7 +217,7 @@
         sigma = sigma + strength * (up * ahead + down * behind)
     res = sigma - cur_ref[...]
     fresh = _pair_sums([res] + history, [(0, j) for j in range(HIST + 1)])
-    send1[...] = fresh + gram
+    send1[...] = _pack_rows(fresh + gram)
 
     def exchange(src, recv, ssem, rsem, count, peer):
         out = []
@@ -228,7 +247,7 @@
     exchange(send1, recv1, ss1, rs1, nk, lambda s: ((mk + s + 1) % nk, me))
     acc1[...] = total(send1[...], recv1, mk, nk)
     exchange(acc1, recv2, ss2, rs2, ne, lambda s: (mk, (me + s + 1) % ne))
-    summed = total(acc1[...], recv2, me, ne)
+    summed = _unpack_rows(total(acc1[...], recv2, me, ne))
     perm = [0] + [slot_ref[i] + 1 for i in range(HIST)]
     aged = _permute_square(summed / entries, perm)
     weights = _weights_from_products(aged)[:, :1]
@@ -246,7 +265,7 @@
 
 
 def fused_tail(scalars, chunks, cur, pin, pres, nk, ne, entries):
-    tile = (8, 128)
+    tile = (1, 128)
     margin = 128
     rows = chunks.shape[1]
     smem = pl.BlockSpec(memory_space=pltpu.SMEM)

time: 72.7 us -> 71.5 us (0.983)
  Pallas kernels: 50.5 us -> 49.3 us
    pallas_call x1, Pallas kernels: 50.5 us -> 49.3 us  [fused_tail(): pl.pallas_call(functools.partial(_fused_kernel, nk, ne, entries, margin),...]
where the time goes in v10:
time: 71.5 us; the launch traced here: 71.2 us
  Pallas kernels  49.3 us (69%)
  starting transfers between devices  9.71 us (14%)
  local copies, waits for them, and re-layouts  8.64 us (12%)
  matrix products  2.04 us (3%)
  other arithmetic  1.48 us (2%)
    pallas_call x1, Pallas kernels, fused_tail(): pl.pallas_call(functools.partial(_fused_kernel, nk, ne, entries, margin),...  49.3 us
    ppermute x1, starting transfers between devices, padded_2(): lax.ppermute(lax.slice_in_dim(block, 0, width, axis=dim), axis, backward)  5.64 us
    ppermute x1, starting transfers between devices, padded_2(): lax.ppermute(lax.slice_in_dim(block, block.shape[dim] - width, None, axis...  4.07 us
    dot_general x3, matrix products, per_device(): jnp.einsum('dkr,bre->dbke', stencil[:, :, part * group_len:(part + 1) * g...  2.04 us
    reshape x1, local copies, waits for them, and re-layouts, per_device(): past_residuals.reshape(HIST, -1, lanes)  1.98 us
    reshape x1, local copies, waits for them, and re-layouts, per_device(): past_inputs.reshape(HIST, -1, lanes)  1.96 us
    reshape x1, local copies, waits for them, and re-layouts, per_device(): current.reshape(-1, lanes)  1.84 us
    reshape x1, local copies, waits for them, and re-layouts, per_device(): mixed = fused_tail(scalars, chunks, current.reshape(-1, lanes), past_inpu...  1.8 us
  transfers between devices with their start and end apart: 2, of which 0 were waited for; matrix products, arithmetic and copies ran while one was open for 13% of the time, Pallas kernels for 0%

profile of v10, /device:TPU:1, one launch (start us, length us, event | category | flops | bytes accessed | tf_op | source)
XLA Modules:
  0.0 71.2 jit_solution(3570366943558214744)
XLA Ops:
  0.0 0.0 copy-start
  0.0 4.1 %collective-permute-start = (f32[2,2,2,64,128]{4,3,2,1,0:T(8,128)}, f32[2,2,2,64,128]{4,3,2,1,0:T(8,128)S(1)}, u32[]{:S(2)}, u32[]{:S(2)}) collective-permute-start(f32[2,2,2,64,128]{4,3,2,1,0:T(8,128)} %param.12), channel_id=1, source_target_pairs={{0,32},{32,64},{64,96},{96,128},{128,160},{160,192},{192,224},{224... | collective-permute-start | bytes 786440 | tf_op jit(solution)/shard_map/ppermute | solution.py:26
  4.1 5.6 %collective-permute-start.1 = (f32[2,2,2,64,128]{4,3,2,1,0:T(8,128)}, f32[2,2,2,64,128]{4,3,2,1,0:T(8,128)S(1)}, u32[]{:S(2)}, u32[]{:S(2)}) collective-permute-start(f32[2,2,2,64,128]{4,3,2,1,0:T(8,128)} %param.12), channel_id=1, source_target_pairs={{32,0},{64,32},{96,64},{128,96},{160,128},{192,160},{224,192},{256... | collective-permute-start | bytes 786440 | tf_op jit(solution)/shard_map/ppermute | solution.py:29
  9.7 0.7 add_select_fusion
  10.4 0.8 %select_reduce_fusion = f32[64,192]{1,0:T(8,128)S(1)} fusion(f32[5]{0:T(128)} %param.19, s32[64,5]{0,1:T(8,128)S(1)} %add_select_fusion), kind=kLoop, calls=%fused_computation.3 | loop fusion | flops 172032 | bytes 50452 | tf_op jit(solution)/shard_map/reduce_sum | solution.py:320
  11.3 0.1 fusion.5
  11.4 1.3 %fusion.3 = f32[32,2,8,128]{3,0,2,1:T(8,128)S(1)} fusion(f32[8,64,128,1]{2,1,0,3:T(8,128)} %bitcast.31, f32[32,2,64]{2,1,0:T(2,128)S(1)} %get-tuple-element.6), kind=kOutput, calls=%fused_computation.8 | convolution fusion | flops 50331648 | bytes 540672 | tf_op jit(solution)/shard_map/dkr,bre->dbke/dot_general | solution.py:333
  12.7 1.8 %reshape.34.cur_ref = f32[16,4096]{1,0:T(8,128)} reshape(f32[2,2,2,2,4096]{4,3,2,1,0:T(2,128)} %param.13) | data formatting | bytes 524288 | tf_op jit(solution)/shard_map/reshape | solution.py:346
  14.5 0.0 copy-done
  14.5 0.0 copy-start.1
  14.5 2.0 %reshape.35.pin_ref = f32[5,16,4096]{2,1,0:T(8,128)} reshape(f32[5,2,2,2,2,4096]{5,4,3,2,1,0:T(2,128)S(1)} %copy-done) | data formatting | bytes 2621440 | tf_op jit(solution)/shard_map/reshape | solution.py:347
  16.5 0.0 copy-done.1
  16.5 2.0 %reshape.36.pres_ref = f32[5,16,4096]{2,1,0:T(8,128)} reshape(f32[5,2,2,2,2,4096]{5,4,3,2,1,0:T(2,128)S(1)} %copy-done.1) | data formatting | bytes 2621440 | tf_op jit(solution)/shard_map/reshape | solution.py:348
  18.5 0.0 collective-permute-done.1
  18.5 0.4 fusion.2
  18.9 0.0 collective-permute-done
  18.9 0.4 fusion.1
  19.2 0.9 %copy.23 = f32[32,8,2,128]{3,2,1,0:T(2,128)} copy(f32[32,8,2,128]{3,0,1,2:T(8,128)S(1)} %fusion.1) | data formatting | bytes 524288 | tf_op jit(solution)/shard_map/add | solution.py:333
  20.1 49.3 %shard_map.118 = f32[16,4096]{1,0:T(8,128)} custom-call(s32[5]{0:T(128)} %slot_ref.1, s32[2]{0:T(128)} %shift_ref.1, s32[64]{0:T(128)} %class_ref.1, f32[2]{0:T(128)} %optical_ref.1, f32[2]{0:T(128)} %occ_ref.1, f32[4]{0:T(128)} %acoustic_ref.1, f32[32,16,128]{2,1,0:T(8,128)} %bitcast.30, f32[16,4096]{1,0:T(8,128)} %reshape.34.cur_ref, ...), custom_call_target="tpu_custom_call" | custom-call | tf_op jit(solution)/shard_map/pallas_call | solution.py:273
  69.4 1.8 %reshape.37 = f32[2,2,2,2,4096]{4,3,2,1,0:T(2,128)} reshape(f32[16,4096]{1,0:T(8,128)} %shard_map.118) | data formatting | bytes 524288 | tf_op jit(solution)/shard_map/reshape | solution.py:352
  (1 shorter events, 0.0 us)
Async XLA Ops:
  0.0 14.5 %copy-start = (f32[5,2,2,2,2,4096]{5,4,3,2,1,0:T(2,128)S(1)}, f32[5,2,2,2,2,4096]{5,4,3,2,1,0:T(2,128)}, u32[]{:S(2)}) copy-start(f32[5,2,2,2,2,4096]{5,4,3,2,1,0:T(2,128)} %param.14) | copy-start | bytes 3932164
  0.0 18.9 %collective-permute-start = (f32[2,2,2,64,128]{4,3,2,1,0:T(8,128)}, f32[2,2,2,64,128]{4,3,2,1,0:T(8,128)S(1)}, u32[]{:S(2)}, u32[]{:S(2)}) collective-permute-start(f32[2,2,2,64,128]{4,3,2,1,0:T(8,128)} %param.12), channel_id=1, source_target_pairs={{0,32},{32,64},{64,96},{96,128},{128,160},{160,192},{192,224},{224... | collective-permute-start | bytes 786440 | tf_op jit(solution)/shard_map/ppermute | solution.py:26
  4.1 14.4 %collective-permute-start.1 = (f32[2,2,2,64,128]{4,3,2,1,0:T(8,128)}, f32[2,2,2,64,128]{4,3,2,1,0:T(8,128)S(1)}, u32[]{:S(2)}, u32[]{:S(2)}) collective-permute-start(f32[2,2,2,64,128]{4,3,2,1,0:T(8,128)} %param.12), channel_id=1, source_target_pairs={{32,0},{64,32},{96,64},{128,96},{160,128},{192,160},{224,192},{256... | collective-permute-start | bytes 786440 | tf_op jit(solution)/shard_map/ppermute | solution.py:29
  14.5 2.0 %copy-start.1 = (f32[5,2,2,2,2,4096]{5,4,3,2,1,0:T(2,128)S(1)}, f32[5,2,2,2,2,4096]{5,4,3,2,1,0:T(2,128)}, u32[]{:S(2)}) copy-start(f32[5,2,2,2,2,4096]{5,4,3,2,1,0:T(2,128)} %param.15) | copy-start | bytes 3932164

commit v11 on v10

--- a/solution.py
+++ b/solution.py
@@ -154,7 +154,7 @@
 def _fused_kernel(nk, ne, entries, margin,
                   slot_ref, shift_ref, class_ref, optical_ref, occ_ref, acoustic_ref,
                   chunk_ref, cur_ref, pin_ref, pres_ref, out_ref,
-                  ypad, send1, recv1, recv2, acc1, ts, tr, ss1, rs1, ss2, rs2):
+                  ypad, bases, send1, recv1, recv2, acc1, ts, tr, ss1, rs1, ss2, rs2):
     mk = lax.axis_index("kgrp")
     me = lax.axis_index("energy")
     width = chunk_ref.shape[-1]
@@ -232,10 +232,13 @@
             )
             c.start()
             out.append(c)
-        for s in range(count - 1):
-            out[s].wait_recv()
-        for s in range(count - 1):
-            out[s].wait_send()
+        return out
+
+    def finish(out):
+        for c in out:
+            c.wait_recv()
+        for c in out:
+            c.wait_send()
 
     def total(own, recv, mine, count):
         acc = jnp.zeros_like(own)
@@ -244,9 +247,13 @@
             acc = acc + jnp.where(idx == mine, own, recv[slot])
         return acc
 
-    exchange(send1, recv1, ss1, rs1, nk, lambda s: ((mk + s + 1) % nk, me))
+    pending = exchange(send1, recv1, ss1, rs1, nk, lambda s: ((mk + s + 1) % nk, me))
+    lead = pin_ref.shape[0] // HIST
+    for m in range(HIST):
+        bases[m] = pin_ref[m * lead : (m + 1) * lead].reshape(rows, length) + mixing_share * history[m]
+    finish(pending)
     acc1[...] = total(send1[...], recv1, mk, nk)
-    exchange(acc1, recv2, ss2, rs2, ne, lambda s: (mk, (me + s + 1) % ne))
+    finish(exchange(acc1, recv2, ss2, rs2, ne, lambda s: (mk, (me + s + 1) % ne)))
     summed = _unpack_rows(total(acc1[...], recv2, me, ne))
     perm = [0] + [slot_ref[i] + 1 for i in range(HIST)]
     aged = _permute_square(summed / entries, perm)
@@ -260,7 +267,7 @@
             slot_w[m] = term if slot_w[m] is None else slot_w[m] + term
     mixed = slot_w[0] * (cur_ref[...] + mixing_share * res)
     for m in range(HIST):
-        mixed = mixed + slot_w[m + 1] * (pin_ref[m] + mixing_share * pres_ref[m])
+        mixed = mixed + slot_w[m + 1] * bases[m]
     out_ref[...] = mixed
 
 
@@ -277,6 +284,7 @@
         out_specs=vmem,
         scratch_shapes=[
             pltpu.VMEM((rows, cur.shape[1] + 2 * margin), jnp.float32),
+            pltpu.VMEM((HIST,) + cur.shape, jnp.float32),
             pltpu.VMEM(tile, jnp.float32),
             pltpu.VMEM((nk - 1,) + tile, jnp.float32),
             pltpu.VMEM((ne - 1,) + tile, jnp.float32),
@@ -344,7 +352,7 @@
         scalars,
         chunks,
         current.reshape(-1, lanes),
-        past_inputs.reshape(HIST, -1, lanes),
+        past_inputs.reshape(-1, rows_here, lanes),
         past_residuals.reshape(HIST, -1, lanes),
         nk,
         ne,

time: 71.5 us -> 71.5 us (level)
  local copies, waits for them, and re-layouts: 8.64 us -> 6.67 us
  Pallas kernels: 49.3 us -> 51.2 us
    reshape x1 -> x0, local copies, waits for them, and re-layouts: 1.96 us -> none  [per_device(): past_inputs.reshape(HIST, -1, lanes)]
    pallas_call x1, Pallas kernels: 49.3 us -> 51.2 us  [fused_tail(): pl.pallas_call(functools.partial(_fused_kernel, nk, ne, entries, margin),...]
  transfers between devices with their start and end apart: 2 -> 2, of which waited for: 0 -> 0; matrix products, arithmetic and copies ran while one was open for 13% -> 10% of each run, Pallas kernels for 0% -> 0%
where the time goes in v11:
time: 71.5 us; the launch traced here: 71.2 us
  Pallas kernels  51.2 us (72%)
  starting transfers between devices  9.71 us (14%)
  local copies, waits for them, and re-layouts  6.67 us (9%)
  matrix products  2.03 us (3%)
  other arithmetic  1.48 us (2%)
    pallas_call x1, Pallas kernels, fused_tail(): pl.pallas_call(functools.partial(_fused_kernel, nk, ne, entries, margin),...  51.2 us
    ppermute x1, starting transfers between devices, padded_2(): lax.ppermute(lax.slice_in_dim(block, 0, width, axis=dim), axis, backward)  5.64 us
    ppermute x1, starting transfers between devices, padded_2(): lax.ppermute(lax.slice_in_dim(block, block.shape[dim] - width, None, axis...  4.07 us
    dot_general x3, matrix products, per_device(): jnp.einsum('dkr,bre->dbke', stencil[:, :, part * group_len:(part + 1) * g...  2.03 us
    reshape x1, local copies, waits for them, and re-layouts, per_device(): past_residuals.reshape(HIST, -1, lanes)  1.97 us
    reshape x1, local copies, waits for them, and re-layouts, per_device(): current.reshape(-1, lanes)  1.85 us
    reshape x1, local copies, waits for them, and re-layouts, per_device(): mixed = fused_tail(scalars, chunks, current.reshape(-1, lanes), past_inpu...  1.8 us
  transfers between devices with their start and end apart: 2, of which 0 were waited for; matrix products, arithmetic and copies ran while one was open for 10% of the time, Pallas kernels for 0%

profile of v11, /device:TPU:1, one launch (start us, length us, event | category | flops | bytes accessed | tf_op | source)
XLA Modules:
  0.0 71.2 jit_solution(1034569635593771254)
XLA Ops:
  0.0 0.0 copy-start
  0.0 4.1 %collective-permute-start = (f32[2,2,2,64,128]{4,3,2,1,0:T(8,128)}, f32[2,2,2,64,128]{4,3,2,1,0:T(8,128)S(1)}, u32[]{:S(2)}, u32[]{:S(2)}) collective-permute-start(f32[2,2,2,64,128]{4,3,2,1,0:T(8,128)} %param.12), channel_id=1, source_target_pairs={{0,32},{32,64},{64,96},{96,128},{128,160},{160,192},{192,224},{224... | collective-permute-start | bytes 786440 | tf_op jit(solution)/shard_map/ppermute | solution.py:26
  4.1 5.6 %collective-permute-start.1 = (f32[2,2,2,64,128]{4,3,2,1,0:T(8,128)}, f32[2,2,2,64,128]{4,3,2,1,0:T(8,128)S(1)}, u32[]{:S(2)}, u32[]{:S(2)}) collective-permute-start(f32[2,2,2,64,128]{4,3,2,1,0:T(8,128)} %param.12), channel_id=1, source_target_pairs={{32,0},{64,32},{96,64},{128,96},{160,128},{192,160},{224,192},{256... | collective-permute-start | bytes 786440 | tf_op jit(solution)/shard_map/ppermute | solution.py:29
  9.7 0.7 add_select_fusion
  10.4 0.8 %select_reduce_fusion = f32[64,192]{1,0:T(8,128)S(1)} fusion(f32[5]{0:T(128)} %param.19, s32[64,5]{0,1:T(8,128)S(1)} %add_select_fusion), kind=kLoop, calls=%fused_computation.3 | loop fusion | flops 172032 | bytes 50452 | tf_op jit(solution)/shard_map/reduce_sum | solution.py:328
  11.3 0.1 fusion.5
  11.4 1.3 %fusion.3 = f32[32,2,8,128]{3,0,2,1:T(8,128)S(1)} fusion(f32[8,64,128,1]{2,1,0,3:T(8,128)} %bitcast.33, f32[32,2,64]{2,1,0:T(2,128)S(1)} %get-tuple-element.6), kind=kOutput, calls=%fused_computation.8 | convolution fusion | flops 50331648 | bytes 540672 | tf_op jit(solution)/shard_map/dkr,bre->dbke/dot_general | solution.py:341
  12.7 1.8 %reshape.34.cur_ref = f32[16,4096]{1,0:T(8,128)} reshape(f32[2,2,2,2,4096]{4,3,2,1,0:T(2,128)} %param.13) | data formatting | bytes 524288 | tf_op jit(solution)/shard_map/reshape | solution.py:354
  14.5 0.0 copy-done
  14.5 2.0 %reshape.36.pres_ref = f32[5,16,4096]{2,1,0:T(8,128)} reshape(f32[5,2,2,2,2,4096]{5,4,3,2,1,0:T(2,128)S(1)} %copy-done) | data formatting | bytes 2621440 | tf_op jit(solution)/shard_map/reshape | solution.py:356
  16.5 0.0 collective-permute-done.1
  16.5 0.4 fusion.2
  16.9 0.0 collective-permute-done
  16.9 0.4 fusion.1
  17.3 0.9 %copy.23 = f32[32,8,2,128]{3,2,1,0:T(2,128)} copy(f32[32,8,2,128]{3,0,1,2:T(8,128)S(1)} %fusion.1) | data formatting | bytes 524288 | tf_op jit(solution)/shard_map/add | solution.py:341
  18.2 51.2 %shard_map.118 = f32[16,4096]{1,0:T(8,128)} custom-call(s32[5]{0:T(128)} %slot_ref.1, s32[2]{0:T(128)} %shift_ref.1, s32[64]{0:T(128)} %class_ref.1, f32[2]{0:T(128)} %optical_ref.1, f32[2]{0:T(128)} %occ_ref.1, f32[4]{0:T(128)} %acoustic_ref.1, f32[32,16,128]{2,1,0:T(8,128)} %bitcast.32, f32[16,4096]{1,0:T(8,128)} %reshape.34.cur_ref, ...), custom_call_target="tpu_custom_call" | custom-call | tf_op jit(solution)/shard_map/pallas_call | solution.py:280
  69.4 1.8 %reshape.37 = f32[2,2,2,2,4096]{4,3,2,1,0:T(2,128)} reshape(f32[16,4096]{1,0:T(8,128)} %shard_map.118) | data formatting | bytes 524288 | tf_op jit(solution)/shard_map/reshape | solution.py:360
  (1 shorter events, 0.0 us)
Async XLA Ops:
  0.0 14.5 %copy-start = (f32[5,2,2,2,2,4096]{5,4,3,2,1,0:T(2,128)S(1)}, f32[5,2,2,2,2,4096]{5,4,3,2,1,0:T(2,128)}, u32[]{:S(2)}) copy-start(f32[5,2,2,2,2,4096]{5,4,3,2,1,0:T(2,128)} %param.15) | copy-start | bytes 3932164
  0.0 16.9 %collective-permute-start = (f32[2,2,2,64,128]{4,3,2,1,0:T(8,128)}, f32[2,2,2,64,128]{4,3,2,1,0:T(8,128)S(1)}, u32[]{:S(2)}, u32[]{:S(2)}) collective-permute-start(f32[2,2,2,64,128]{4,3,2,1,0:T(8,128)} %param.12), channel_id=1, source_target_pairs={{0,32},{32,64},{64,96},{96,128},{128,160},{160,192},{192,224},{224... | collective-permute-start | bytes 786440 | tf_op jit(solution)/shard_map/ppermute | solution.py:26
  4.1 12.4 %collective-permute-start.1 = (f32[2,2,2,64,128]{4,3,2,1,0:T(8,128)}, f32[2,2,2,64,128]{4,3,2,1,0:T(8,128)S(1)}, u32[]{:S(2)}, u32[]{:S(2)}) collective-permute-start(f32[2,2,2,64,128]{4,3,2,1,0:T(8,128)} %param.12), channel_id=1, source_target_pairs={{32,0},{64,32},{96,64},{128,96},{160,128},{192,160},{224,192},{256... | collective-permute-start | bytes 786440 | tf_op jit(solution)/shard_map/ppermute | solution.py:29

commit v12 on v11

--- a/solution.py
+++ b/solution.py
@@ -74,8 +74,11 @@
     a = system + jnp.where(eye, ridge, 0.0)
     lower = jnp.zeros_like(a)
     upper = jnp.zeros_like(a)
+    diagonal = []
     for j in range(size_n):
-        pivot = jnp.sqrt(_pick((row == j) & (col == j), a, None).reshape(1, 1))
+        head = _pick((row == j) & (col == j), a, None).reshape(1, 1)
+        pivot = jnp.sqrt(head)
+        diagonal.append(head / pivot)
         lcol = jnp.where(row[:, :1] >= j, _pick(col == j, a, 1) / pivot, 0.0)
         lrow = jnp.where(col[:1, :] >= j, _pick(row == j, a, 0) / pivot, 0.0)
         lower = lower + jnp.where(col == j, lcol, 0.0)
@@ -85,14 +88,14 @@
     rest = target
     forward = jnp.zeros_like(target)
     for i in range(size_n):
-        lii = _pick((row == i) & (col == i), lower, None).reshape(1, 1)
+        lii = diagonal[i]
         yi = _pick(row1 == i, rest, 0) / lii
         forward = forward + jnp.where(row1 == i, yi, 0.0)
         rest = rest - jnp.where(row1 > i, _pick(col == i, lower, 1), 0.0) * yi
     rest = forward
     gamma = jnp.zeros_like(target)
     for i in range(size_n - 1, -1, -1):
-        lii = _pick((row == i) & (col == i), lower, None).reshape(1, 1)
+        lii = diagonal[i]
         gi = _pick(row1 == i, rest, 0) / lii
         gamma = gamma + jnp.where(row1 == i, gi, 0.0)
         rest = rest - jnp.where(row1 < i, _pick(col == i, upper, 1), 0.0) * gi
@@ -167,14 +170,14 @@
         pl.semaphore_signal(barrier, 1, device_id=(mk, (me + s + 1) % ne), device_id_type=MESH)
     ypad[:, :margin] = jnp.zeros((rows, margin), jnp.float32)
     ypad[:, margin + length :] = jnp.zeros((rows, margin), jnp.float32)
-    ypad[:, pl.ds(pl.multiple_of(margin + me * width, width), width)] = chunk_ref[me]
+    ypad[:, pl.ds(pl.multiple_of(margin + me * width, width), width)] = chunk_ref[:, me, :]
     pl.semaphore_wait(barrier, nk - 1 + ne - 1)
 
     copies = []
     for s in range(ne - 1):
         peer = (me + s + 1) % ne
         c = pltpu.make_async_remote_copy(
-            src_ref=chunk_ref.at[peer],
+            src_ref=chunk_ref.at[:, peer, :],
             dst_ref=ypad.at[:, pl.ds(pl.multiple_of(margin + me * width, width), width)],
             send_sem=ts.at[s],
             recv_sem=tr.at[ne - 2 - s],
@@ -188,7 +191,7 @@
     for q in range(ne - 1):
         source = (me + q + 1) % ne
         pltpu.make_async_remote_copy(
-            src_ref=chunk_ref.at[me],
+            src_ref=chunk_ref.at[:, me, :],
             dst_ref=ypad.at[:, pl.ds(pl.multiple_of(margin + source * width, width), width)],
             send_sem=ts.at[q],
             recv_sem=tr.at[q],
@@ -200,11 +203,12 @@
 
     y = ypad[...]
     row = lax.broadcasted_iota(jnp.int32, (rows, 1), 0)
-    lesser = row < rows // 2
+    lead = 8
+    lesser = row % lead < lead // 2
     per_row = rows // 8
     coupling = jnp.zeros((rows, 1), jnp.float32)
     for r in range(per_row):
-        coupling = jnp.where(row % per_row == r, acoustic_ref[class_ref[me * per_row + r]], coupling)
+        coupling = jnp.where(row // lead == r, acoustic_ref[class_ref[me * per_row + r]], coupling)
     sigma = coupling * y[:, margin : margin + length]
     for m in range(2):
         shift = shift_ref[m]
@@ -248,9 +252,8 @@
         return acc
 
     pending = exchange(send1, recv1, ss1, rs1, nk, lambda s: ((mk + s + 1) % nk, me))
-    lead = pin_ref.shape[0] // HIST
     for m in range(HIST):
-        bases[m] = pin_ref[m * lead : (m + 1) * lead].reshape(rows, length) + mixing_share * history[m]
+        bases[m] = pin_ref[m] + mixing_share * history[m]
     finish(pending)
     acc1[...] = total(send1[...], recv1, mk, nk)
     finish(exchange(acc1, recv2, ss2, rs2, ne, lambda s: (mk, (me + s + 1) % ne)))
@@ -274,7 +277,7 @@
 def fused_tail(scalars, chunks, cur, pin, pres, nk, ne, entries):
     tile = (1, 128)
     margin = 128
-    rows = chunks.shape[1]
+    rows = chunks.shape[0]
     smem = pl.BlockSpec(memory_space=pltpu.SMEM)
     vmem = pl.BlockSpec(memory_space=pltpu.VMEM)
     return pl.pallas_call(
@@ -336,28 +339,33 @@
     lead = greens.shape[:3]
     flat = lambda x: x.reshape((-1,) + x.shape[3:])
     stencil = stencil.reshape(ne, rows_here, 3 * group_len)
-    chunks = jnp.zeros((ne, flat(greens).shape[0], rows_here, greens.shape[4]), jnp.float32)
+    chunks = jnp.zeros((rows_here, flat(greens).shape[0], ne, greens.shape[4]), jnp.float32)
     for part, block in enumerate((low, greens, high)):
         chunks = chunks + jnp.einsum(
-            "dkr,bre->dbke",
+            "dkr,bre->kbde",
             stencil[:, :, part * group_len : (part + 1) * group_len],
             flat(block),
             precision=lax.Precision.HIGHEST,
         )
-    chunks = chunks.reshape(ne, -1, greens.shape[4])
+    chunks = chunks.reshape(-1, ne, greens.shape[4])
     lanes = current.shape[-1]
     entries = float(current.size * nk * ne)
     scalars = (slot_order, phonon_shift, momentum_class, optical_coupling, occupation, acoustic_coupling)
+    def to_rows(x):
+        x = x.reshape((-1, flat(greens).shape[0], rows_here, lanes))
+        return jnp.swapaxes(x, 1, 2).reshape((-1, rows_here * flat(greens).shape[0], lanes))
+
     mixed = fused_tail(
         scalars,
         chunks,
-        current.reshape(-1, lanes),
-        past_inputs.reshape(-1, rows_here, lanes),
-        past_residuals.reshape(HIST, -1, lanes),
+        to_rows(current)[0],
+        to_rows(past_inputs),
+        to_rows(past_residuals),
         nk,
         ne,
         entries,
-    ).reshape(current.shape)
+    )
+    mixed = jnp.swapaxes(mixed.reshape(rows_here, -1, lanes), 0, 1).reshape(current.shape)
     return mixed
 
 

time: 71.5 us -> 71.1 us (level)
  local copies, waits for them, and re-layouts: 6.67 us -> 7.78 us
  Pallas kernels: 51.2 us -> 50.1 us
    transpose x0 -> x1, local copies, waits for them, and re-layouts: none -> 1.86 us  [per_device(): jnp.swapaxes(mixed.reshape(rows_here, -1, lanes), 0, 1)]
    pallas_call x1, Pallas kernels: 51.2 us -> 50.1 us  [fused_tail(): pl.pallas_call(functools.partial(_fused_kernel, nk, ne, entries, margin),...]
    add x1 -> x0, local copies, waits for them, and re-layouts: 0.91 us -> none  [per_device(): chunks + jnp.einsum('dkr,bre->dbke', stencil[:, :, part * group_len:(part...]
    reshape x3 -> x2, local copies, waits for them, and re-layouts: 5.62 us -> 5.77 us  [the longest x1 4.91 us: to_rows(): jnp.swapaxes(x, 1, 2)]
  transfers between devices with their start and end apart: 2 -> 2, of which waited for: 0 -> 0; matrix products, arithmetic and copies ran while one was open for 10% -> 11% of each run, Pallas kernels for 0% -> 0%
where the time goes in v12:
time: 71.1 us; the launch traced here: 70.8 us
  Pallas kernels  50.1 us (70%)
  starting transfers between devices  9.58 us (13%)
  local copies, waits for them, and re-layouts  7.78 us (11%)
  matrix products  1.78 us (3%)
  other arithmetic  1.48 us (2%)
    pallas_call x1, Pallas kernels, fused_tail(): pl.pallas_call(functools.partial(_fused_kernel, nk, ne, entries, margin),...  50.1 us
    ppermute x1, starting transfers between devices, padded_2(): lax.ppermute(lax.slice_in_dim(block, 0, width, axis=dim), axis, backward)  5.64 us
    reshape x1, local copies, waits for them, and re-layouts, to_rows(): jnp.swapaxes(x, 1, 2)  4.91 us
    ppermute x1, starting transfers between devices, padded_2(): lax.ppermute(lax.slice_in_dim(block, block.shape[dim] - width, None, axis...  3.94 us
    transpose x1, local copies, waits for them, and re-layouts, per_device(): jnp.swapaxes(mixed.reshape(rows_here, -1, lanes), 0, 1)  1.86 us
    dot_general x3, matrix products, per_device(): jnp.einsum('dkr,bre->kbde', stencil[:, :, part * group_len:(part + 1) * g...  1.78 us
  transfers between devices with their start and end apart: 2, of which 0 were waited for; matrix products, arithmetic and copies ran while one was open for 11% of the time, Pallas kernels for 0%

profile of v12, /device:TPU:1, one launch (start us, length us, event | category | flops | bytes accessed | tf_op | source)
XLA Modules:
  0.0 70.8 jit_solution(13570405243544823872)
XLA Ops:
  0.0 3.9 %collective-permute-start = (f32[2,2,2,64,128]{4,3,2,1,0:T(8,128)}, f32[2,2,2,64,128]{4,3,2,1,0:T(8,128)S(1)}, u32[]{:S(2)}, u32[]{:S(2)}) collective-permute-start(f32[2,2,2,64,128]{4,3,2,1,0:T(8,128)} %param.12), channel_id=1, source_target_pairs={{0,32},{32,64},{64,96},{96,128},{128,160},{160,192},{192,224},{224... | collective-permute-start | bytes 786440 | tf_op jit(solution)/shard_map/ppermute | solution.py:26
  3.9 5.6 %collective-permute-start.1 = (f32[2,2,2,64,128]{4,3,2,1,0:T(8,128)}, f32[2,2,2,64,128]{4,3,2,1,0:T(8,128)S(1)}, u32[]{:S(2)}, u32[]{:S(2)}) collective-permute-start(f32[2,2,2,64,128]{4,3,2,1,0:T(8,128)} %param.12), channel_id=1, source_target_pairs={{32,0},{64,32},{96,64},{128,96},{160,128},{192,160},{224,192},{256... | collective-permute-start | bytes 786440 | tf_op jit(solution)/shard_map/ppermute | solution.py:29
  9.6 0.7 add_select_fusion
  10.3 0.8 %select_reduce_fusion = f32[64,192]{1,0:T(8,128)S(1)} fusion(f32[5]{0:T(128)} %param.19, s32[64,5]{0,1:T(8,128)S(1)} %add_select_fusion), kind=kLoop, calls=%fused_computation.4 | loop fusion | flops 172032 | bytes 50452 | tf_op jit(solution)/shard_map/reduce_sum | solution.py:331
  11.1 0.0 copy-start.1
  11.1 0.0 copy-start
  11.2 4.9 %copy_bitcast_fusion = (f32[5,16,4096]{2,1,0:T(8,128)}, f32[5,16,4096]{2,1,0:T(8,128)}) fusion(f32[5,8,2,4096]{3,2,1,0:T(2,128)} %bitcast.50, f32[5,8,2,4096]{3,2,1,0:T(2,128)} %bitcast.51), kind=kLoop, calls=%fused_computation | loop fusion | bytes 5242880 | tf_op jit(solution)/shard_map/reshape | solution.py:356
  16.1 0.1 fusion.4
  16.2 0.0 copy-done.1
  16.2 0.4 fusion.2
  16.5 0.0 copy-done
  16.6 0.9 %copy.48 = f32[1,8,2,4096]{3,1,2,0:T(8,128)} copy(f32[1,8,2,4096]{3,2,1,0:T(2,128)S(1)} %bitcast.55) | data formatting | bytes 524288 | tf_op jit(solution)/shard_map/reshape | solution.py:355
  17.4 0.0 collective-permute-done.1
  17.4 0.4 fusion.1
  17.8 0.0 collective-permute-done
  17.8 1.1 %fusion = f32[32,2,8,128]{3,0,2,1:T(8,128)} fusion(f32[32,2,8,128]{3,0,2,1:T(8,128)S(1)} %fusion.1, f32[32,2,8,128]{3,0,2,1:T(8,128)S(1)} %fusion.2, f32[8,64,128,1]{2,1,0,3:T(8,128)S(1)} %bitcast.58, f32[32,2,64]{2,1,0:T(2,128)S(1)} %get-tuple-element.5), kind=kOutput, calls=%fused_computation.3 | convolution fusion | flops 50462720 | bytes 1064960 | tf_op jit(solution)/shard_map/dkr,bre->kbde/dot_general | solution.py:344
  18.9 50.1 %shard_map.118 = f32[16,4096]{1,0:T(8,128)} custom-call(s32[5]{0:T(128)} %slot_ref.1, s32[2]{0:T(128)} %shift_ref.1, s32[64]{0:T(128)} %class_ref.1, f32[2]{0:T(128)} %optical_ref.1, f32[2]{0:T(128)} %occ_ref.1, f32[4]{0:T(128)} %acoustic_ref.1, f32[16,32,128]{2,1,0:T(8,128)} %bitcast.54, f32[16,4096]{1,0:T(8,128)} %bitcast.52, ...), custom_call_target="tpu_custom_call" | custom-call | tf_op jit(solution)/shard_map/pallas_call | solution.py:283
  69.0 1.9 %copy.32 = f32[8,2,4096]{2,1,0:T(2,128)} copy(f32[8,2,4096]{2,0,1:T(8,128)} %bitcast.53) | data formatting | bytes 524288 | tf_op jit(solution)/shard_map/transpose | solution.py:368
  (1 shorter events, 0.0 us)
Async XLA Ops:
  0.0 17.8 %collective-permute-start = (f32[2,2,2,64,128]{4,3,2,1,0:T(8,128)}, f32[2,2,2,64,128]{4,3,2,1,0:T(8,128)S(1)}, u32[]{:S(2)}, u32[]{:S(2)}) collective-permute-start(f32[2,2,2,64,128]{4,3,2,1,0:T(8,128)} %param.12), channel_id=1, source_target_pairs={{0,32},{32,64},{64,96},{96,128},{128,160},{160,192},{192,224},{224... | collective-permute-start | bytes 786440 | tf_op jit(solution)/shard_map/ppermute | solution.py:26
  3.9 13.5 %collective-permute-start.1 = (f32[2,2,2,64,128]{4,3,2,1,0:T(8,128)}, f32[2,2,2,64,128]{4,3,2,1,0:T(8,128)S(1)}, u32[]{:S(2)}, u32[]{:S(2)}) collective-permute-start(f32[2,2,2,64,128]{4,3,2,1,0:T(8,128)} %param.12), channel_id=1, source_target_pairs={{32,0},{64,32},{96,64},{128,96},{160,128},{192,160},{224,192},{256... | collective-permute-start | bytes 786440 | tf_op jit(solution)/shard_map/ppermute | solution.py:29
  11.1 5.0 %copy-start.1 = (f32[2,2,2,64,128]{4,3,2,1,0:T(8,128)S(1)}, f32[2,2,2,64,128]{4,3,2,1,0:T(8,128)}, u32[]{:S(2)}) copy-start(f32[2,2,2,64,128]{4,3,2,1,0:T(8,128)} %param.12) | copy-start | bytes 786436
  11.1 5.4 %copy-start = (f32[2,2,2,2,4096]{4,3,2,1,0:T(2,128)S(1)}, f32[2,2,2,2,4096]{4,3,2,1,0:T(2,128)}, u32[]{:S(2)}) copy-start(f32[2,2,2,2,4096]{4,3,2,1,0:T(2,128)} %param.13) | copy-start | bytes 786436

commit v13 on v12

--- a/solution.py
+++ b/solution.py
@@ -156,8 +156,8 @@
 
 def _fused_kernel(nk, ne, entries, margin,
                   slot_ref, shift_ref, class_ref, optical_ref, occ_ref, acoustic_ref,
-                  chunk_ref, cur_ref, pin_ref, pres_ref, out_ref,
-                  ypad, bases, send1, recv1, recv2, acc1, ts, tr, ss1, rs1, ss2, rs2):
+                  low_ref, mid_ref, high_ref, cur_ref, pin_ref, pres_ref, out_ref,
+                  chunk_ref, ypad, bases, send1, recv1, recv2, acc1, ts, tr, ss1, rs1, ss2, rs2):
     mk = lax.axis_index("kgrp")
     me = lax.axis_index("energy")
     width = chunk_ref.shape[-1]
@@ -168,6 +168,7 @@
         pl.semaphore_signal(barrier, 1, device_id=((mk + s + 1) % nk, me), device_id_type=MESH)
     for s in range(ne - 1):
         pl.semaphore_signal(barrier, 1, device_id=(mk, (me + s + 1) % ne), device_id_type=MESH)
+    chunk_ref[...] = low_ref[...] + mid_ref[...] + high_ref[...]
     ypad[:, :margin] = jnp.zeros((rows, margin), jnp.float32)
     ypad[:, margin + length :] = jnp.zeros((rows, margin), jnp.float32)
     ypad[:, pl.ds(pl.multiple_of(margin + me * width, width), width)] = chunk_ref[:, me, :]
@@ -274,7 +275,8 @@
     out_ref[...] = mixed
 
 
-def fused_tail(scalars, chunks, cur, pin, pres, nk, ne, entries):
+def fused_tail(scalars, parts, cur, pin, pres, nk, ne, entries):
+    chunks = parts[0]
     tile = (1, 128)
     margin = 128
     rows = chunks.shape[0]
@@ -283,9 +285,10 @@
     return pl.pallas_call(
         functools.partial(_fused_kernel, nk, ne, entries, margin),
         out_shape=jax.ShapeDtypeStruct(cur.shape, jnp.float32),
-        in_specs=[smem] * len(scalars) + [vmem] * 4,
+        in_specs=[smem] * len(scalars) + [vmem] * 6,
         out_specs=vmem,
         scratch_shapes=[
+            pltpu.VMEM(chunks.shape, jnp.float32),
             pltpu.VMEM((rows, cur.shape[1] + 2 * margin), jnp.float32),
             pltpu.VMEM((HIST,) + cur.shape, jnp.float32),
             pltpu.VMEM(tile, jnp.float32),
@@ -300,7 +303,7 @@
             pltpu.SemaphoreType.DMA((ne - 1,)),
         ],
         compiler_params=pltpu.CompilerParams(collective_id=0, has_side_effects=True),
-    )(*scalars, chunks, cur, pin, pres)
+    )(*scalars, *parts, cur, pin, pres)
 
 
 def per_device(
@@ -339,15 +342,16 @@
     lead = greens.shape[:3]
     flat = lambda x: x.reshape((-1,) + x.shape[3:])
     stencil = stencil.reshape(ne, rows_here, 3 * group_len)
-    chunks = jnp.zeros((rows_here, flat(greens).shape[0], ne, greens.shape[4]), jnp.float32)
-    for part, block in enumerate((low, greens, high)):
-        chunks = chunks + jnp.einsum(
-            "dkr,bre->kbde",
-            stencil[:, :, part * group_len : (part + 1) * group_len],
-            flat(block),
-            precision=lax.Precision.HIGHEST,
-        )
-    chunks = chunks.reshape(-1, ne, greens.shape[4])
+    parts = []
+    for part, block in enumerate((low.reshape(greens.shape), greens, high.reshape(greens.shape))):
+        parts.append(
+            jnp.einsum(
+                "dkr,bre->kbde",
+                stencil[:, :, part * group_len : (part + 1) * group_len],
+                flat(block),
+                precision=lax.Precision.HIGHEST,
+            ).reshape(-1, ne, greens.shape[4])
+        )
     lanes = current.shape[-1]
     entries = float(current.size * nk * ne)
     scalars = (slot_order, phonon_shift, momentum_class, optical_coupling, occupation, acoustic_coupling)
@@ -357,7 +361,7 @@
 
     mixed = fused_tail(
         scalars,
-        chunks,
+        parts,
         to_rows(current)[0],
         to_rows(past_inputs),
         to_rows(past_residuals),

time: 71.1 us -> 71.3 us (level)
  matrix products: 1.78 us -> 3.21 us
  Pallas kernels: 50.1 us -> 48.9 us
    dot_general x3, matrix products: 1.78 us -> 3.21 us  [per_device(): jnp.einsum('dkr,bre->kbde', stencil[:, :, part * group_len:(part + 1) * g...]
    pallas_call x1, Pallas kernels: 50.1 us -> 48.9 us  [fused_tail(): pl.pallas_call(functools.partial(_fused_kernel, nk, ne, entries, margin),...]
  transfers between devices with their start and end apart: 2 -> 2, of which waited for: 0 -> 0; matrix products, arithmetic and copies ran while one was open for 11% -> 13% of each run, Pallas kernels for 0% -> 0%
where the time goes in v13:
time: 71.3 us; the launch traced here: 71 us
  Pallas kernels  48.9 us (69%)
  starting transfers between devices  9.58 us (13%)
  local copies, waits for them, and re-layouts  7.77 us (11%)
  matrix products  3.21 us (5%)
  other arithmetic  1.48 us (2%)
    pallas_call x1, Pallas kernels, fused_tail(): pl.pallas_call(functools.partial(_fused_kernel, nk, ne, entries, margin),...  48.9 us
    ppermute x1, starting transfers between devices, padded_2(): lax.ppermute(lax.slice_in_dim(block, 0, width, axis=dim), axis, backward)  5.64 us
    reshape x1, local copies, waits for them, and re-layouts, to_rows(): jnp.swapaxes(x, 1, 2)  4.91 us
    ppermute x1, starting transfers between devices, padded_2(): lax.ppermute(lax.slice_in_dim(block, block.shape[dim] - width, None, axis...  3.94 us
    dot_general x3, matrix products, per_device(): jnp.einsum('dkr,bre->kbde', stencil[:, :, part * group_len:(part + 1) * g...  3.21 us
    transpose x1, local copies, waits for them, and re-layouts, per_device(): jnp.swapaxes(mixed.reshape(rows_here, -1, lanes), 0, 1)  1.86 us
  transfers between devices with their start and end apart: 2, of which 0 were waited for; matrix products, arithmetic and copies ran while one was open for 13% of the time, Pallas kernels for 0%

profile of v13, /device:TPU:1, one launch (start us, length us, event | category | flops | bytes accessed | tf_op | source)
XLA Modules:
  0.0 71.0 jit_solution(5753186998879184390)
XLA Ops:
  0.0 3.9 %collective-permute-start = (f32[2,2,2,64,128]{4,3,2,1,0:T(8,128)}, f32[2,2,2,64,128]{4,3,2,1,0:T(8,128)S(1)}, u32[]{:S(2)}, u32[]{:S(2)}) collective-permute-start(f32[2,2,2,64,128]{4,3,2,1,0:T(8,128)} %param.12), channel_id=1, source_target_pairs={{0,32},{32,64},{64,96},{96,128},{128,160},{160,192},{192,224},{224... | collective-permute-start | bytes 786440 | tf_op jit(solution)/shard_map/ppermute | solution.py:26
  3.9 5.6 %collective-permute-start.1 = (f32[2,2,2,64,128]{4,3,2,1,0:T(8,128)}, f32[2,2,2,64,128]{4,3,2,1,0:T(8,128)S(1)}, u32[]{:S(2)}, u32[]{:S(2)}) collective-permute-start(f32[2,2,2,64,128]{4,3,2,1,0:T(8,128)} %param.12), channel_id=1, source_target_pairs={{32,0},{64,32},{96,64},{128,96},{160,128},{192,160},{224,192},{256... | collective-permute-start | bytes 786440 | tf_op jit(solution)/shard_map/ppermute | solution.py:29
  9.6 0.7 add_select_fusion
  10.3 0.8 %select_reduce_fusion = f32[64,192]{1,0:T(8,128)S(1)} fusion(f32[5]{0:T(128)} %param.19, s32[64,5]{0,1:T(8,128)S(1)} %add_select_fusion), kind=kLoop, calls=%fused_computation.2 | loop fusion | flops 172032 | bytes 50452 | tf_op jit(solution)/shard_map/reduce_sum | solution.py:334
  11.1 0.0 copy-start.1
  11.1 0.0 copy-start
  11.2 4.9 %copy_bitcast_fusion = (f32[5,16,4096]{2,1,0:T(8,128)}, f32[5,16,4096]{2,1,0:T(8,128)}) fusion(f32[5,8,2,4096]{3,2,1,0:T(2,128)} %bitcast.56, f32[5,8,2,4096]{3,2,1,0:T(2,128)} %bitcast.57), kind=kLoop, calls=%fused_computation | loop fusion | bytes 5242880 | tf_op jit(solution)/shard_map/reshape | solution.py:360
  16.1 0.1 fusion.4
  16.2 0.0 copy-done.1
  16.2 1.1 %fusion.1 = f32[32,2,8,128]{3,0,2,1:T(8,128)} fusion(f32[8,64,128,1]{2,1,0,3:T(8,128)S(1)} %bitcast.64, f32[32,2,64]{2,1,0:T(2,128)S(1)} %get-tuple-element.6), kind=kOutput, calls=%fused_computation.8 | convolution fusion | flops 50331648 | bytes 540672 | tf_op jit(solution)/shard_map/dkr,bre->kbde/dot_general | solution.py:348
  17.2 0.0 copy-done
  17.2 0.8 %copy.48 = f32[1,8,2,4096]{3,1,2,0:T(8,128)} copy(f32[1,8,2,4096]{3,2,1,0:T(2,128)S(1)} %bitcast.63) | data formatting | bytes 524288 | tf_op jit(solution)/shard_map/reshape | solution.py:359
  18.1 0.0 collective-permute-done
  18.1 1.1 %fusion.2 = f32[32,2,8,128]{3,0,2,1:T(8,128)} fusion(f32[8,64,128,1]{2,1,0,3:T(8,128)S(1)} %bitcast.66, f32[32,2,64]{2,1,0:T(2,128)S(1)} %get-tuple-element.7), kind=kOutput, calls=%fused_computation.10 | convolution fusion | flops 50331648 | bytes 540672 | tf_op jit(solution)/shard_map/dkr,bre->kbde/dot_general | solution.py:348
  19.2 0.0 collective-permute-done.1
  19.2 1.1 %fusion = f32[32,2,8,128]{3,0,2,1:T(8,128)} fusion(f32[8,64,128,1]{2,1,0,3:T(8,128)S(1)} %bitcast.65, f32[32,2,64]{2,1,0:T(2,128)S(1)} %get-tuple-element.5), kind=kOutput, calls=%fused_computation.6 | convolution fusion | flops 50331648 | bytes 540672 | tf_op jit(solution)/shard_map/dkr,bre->kbde/dot_general | solution.py:348
  20.2 48.9 %shard_map.118 = f32[16,4096]{1,0:T(8,128)} custom-call(s32[5]{0:T(128)} %slot_ref.1, s32[2]{0:T(128)} %shift_ref.1, s32[64]{0:T(128)} %class_ref.1, f32[2]{0:T(128)} %optical_ref.1, f32[2]{0:T(128)} %occ_ref.1, f32[4]{0:T(128)} %acoustic_ref.1, f32[16,32,128]{2,1,0:T(8,128)} %bitcast.60, f32[16,32,128]{2,1,0:T(8,128)} %bitcast.58, f32[16,32,128]{2,1,0:T(8,128)} %bitcast.61, ...), custom_call_target="tpu_custom_call" | custom-call | tf_op jit(solution)/shard_map/pallas_call | solution.py:285
  69.2 1.9 %copy.32 = f32[8,2,4096]{2,1,0:T(2,128)} copy(f32[8,2,4096]{2,0,1:T(8,128)} %bitcast.62) | data formatting | bytes 524288 | tf_op jit(solution)/shard_map/transpose | solution.py:372
  (1 shorter events, 0.0 us)
Async XLA Ops:
  0.0 18.1 %collective-permute-start = (f32[2,2,2,64,128]{4,3,2,1,0:T(8,128)}, f32[2,2,2,64,128]{4,3,2,1,0:T(8,128)S(1)}, u32[]{:S(2)}, u32[]{:S(2)}) collective-permute-start(f32[2,2,2,64,128]{4,3,2,1,0:T(8,128)} %param.12), channel_id=1, source_target_pairs={{0,32},{32,64},{64,96},{96,128},{128,160},{160,192},{192,224},{224... | collective-permute-start | bytes 786440 | tf_op jit(solution)/shard_map/ppermute | solution.py:26
  3.9 15.2 %collective-permute-start.1 = (f32[2,2,2,64,128]{4,3,2,1,0:T(8,128)}, f32[2,2,2,64,128]{4,3,2,1,0:T(8,128)S(1)}, u32[]{:S(2)}, u32[]{:S(2)}) collective-permute-start(f32[2,2,2,64,128]{4,3,2,1,0:T(8,128)} %param.12), channel_id=1, source_target_pairs={{32,0},{64,32},{96,64},{128,96},{160,128},{192,160},{224,192},{256... | collective-permute-start | bytes 786440 | tf_op jit(solution)/shard_map/ppermute | solution.py:29
  11.1 5.0 %copy-start.1 = (f32[2,2,2,64,128]{4,3,2,1,0:T(8,128)S(1)}, f32[2,2,2,64,128]{4,3,2,1,0:T(8,128)}, u32[]{:S(2)}) copy-start(f32[2,2,2,64,128]{4,3,2,1,0:T(8,128)} %param.12) | copy-start | bytes 786436
  11.1 6.1 %copy-start = (f32[2,2,2,2,4096]{4,3,2,1,0:T(2,128)S(1)}, f32[2,2,2,2,4096]{4,3,2,1,0:T(2,128)}, u32[]{:S(2)}) copy-start(f32[2,2,2,2,4096]{4,3,2,1,0:T(2,128)} %param.13) | copy-start | bytes 786436

commit v14 on v12

--- a/solution.py
+++ b/solution.py
@@ -154,6 +154,10 @@
     return prod
 
 
+def _far_first(count):
+    return sorted(range(count - 1), key=lambda s: (-min(s + 1, count - s - 1), s))
+
+
 def _fused_kernel(nk, ne, entries, margin,
                   slot_ref, shift_ref, class_ref, optical_ref, occ_ref, acoustic_ref,
                   chunk_ref, cur_ref, pin_ref, pres_ref, out_ref,
@@ -164,17 +168,17 @@
     rows, padded_len = ypad.shape
     length = padded_len - 2 * margin
     barrier = pltpu.get_barrier_semaphore()
-    for s in range(nk - 1):
+    for s in _far_first(ne):
+        pl.semaphore_signal(barrier, 1, device_id=(mk, (me + s + 1) % ne), device_id_type=MESH)
+    for s in _far_first(nk):
         pl.semaphore_signal(barrier, 1, device_id=((mk + s + 1) % nk, me), device_id_type=MESH)
-    for s in range(ne - 1):
-        pl.semaphore_signal(barrier, 1, device_id=(mk, (me + s + 1) % ne), device_id_type=MESH)
     ypad[:, :margin] = jnp.zeros((rows, margin), jnp.float32)
     ypad[:, margin + length :] = jnp.zeros((rows, margin), jnp.float32)
     ypad[:, pl.ds(pl.multiple_of(margin + me * width, width), width)] = chunk_ref[:, me, :]
     pl.semaphore_wait(barrier, nk - 1 + ne - 1)
 
-    copies = []
-    for s in range(ne - 1):
+    copies = [None] * (ne - 1)
+    for s in _far_first(ne):
         peer = (me + s + 1) % ne
         c = pltpu.make_async_remote_copy(
             src_ref=chunk_ref.at[:, peer, :],
@@ -185,7 +189,7 @@
             device_id_type=MESH,
         )
         c.start()
-        copies.append(c)
+        copies[s] = c
     history = [pres_ref[m] for m in range(HIST)]
     gram = _pair_sums([None] + history, [(i, j) for i in range(1, HIST + 1) for j in range(i, HIST + 1)])
     for q in range(ne - 1):
@@ -224,8 +228,8 @@
     send1[...] = _pack_rows(fresh + gram)
 
     def exchange(src, recv, ssem, rsem, count, peer):
-        out = []
-        for s in range(count - 1):
+        out = [None] * (count - 1)
+        for s in _far_first(count):
             c = pltpu.make_async_remote_copy(
                 src_ref=src,
                 dst_ref=recv.at[count - 2 - s],
@@ -235,7 +239,7 @@
                 device_id_type=MESH,
             )
             c.start()
-            out.append(c)
+            out[s] = c
         return out
 
     def finish(out):

time: 71.1 us -> 68.2 us (0.959)
  Pallas kernels: 50.1 us -> 47.3 us
    pallas_call x1, Pallas kernels: 50.1 us -> 47.3 us  [fused_tail(): pl.pallas_call(functools.partial(_fused_kernel, nk, ne, entries, margin),...]
  transfers between devices with their start and end apart: 2 -> 2, of which waited for: 0 -> 0; matrix products, arithmetic and copies ran while one was open for 11% -> 12% of each run, Pallas kernels for 0% -> 0%
where the time goes in v14:
time: 68.2 us; the launch traced here: 68 us
  Pallas kernels  47.3 us (69%)
  starting transfers between devices  9.58 us (14%)
  local copies, waits for them, and re-layouts  7.78 us (11%)
  matrix products  1.78 us (3%)
  other arithmetic  1.48 us (2%)
    pallas_call x1, Pallas kernels, fused_tail(): pl.pallas_call(functools.partial(_fused_kernel, nk, ne, entries, margin),...  47.3 us
    ppermute x1, starting transfers between devices, padded_2(): lax.ppermute(lax.slice_in_dim(block, 0, width, axis=dim), axis, backward)  5.64 us
    reshape x1, local copies, waits for them, and re-layouts, to_rows(): jnp.swapaxes(x, 1, 2)  4.91 us
    ppermute x1, starting transfers between devices, padded_2(): lax.ppermute(lax.slice_in_dim(block, block.shape[dim] - width, None, axis...  3.94 us
    transpose x1, local copies, waits for them, and re-layouts, per_device(): jnp.swapaxes(mixed.reshape(rows_here, -1, lanes), 0, 1)  1.86 us
    dot_general x3, matrix products, per_device(): jnp.einsum('dkr,bre->kbde', stencil[:, :, part * group_len:(part + 1) * g...  1.78 us
  transfers between devices with their start and end apart: 2, of which 0 were waited for; matrix products, arithmetic and copies ran while one was open for 12% of the time, Pallas kernels for 0%

profile of v14, /device:TPU:1, one launch (start us, length us, event | category | flops | bytes accessed | tf_op | source)
XLA Modules:
  0.0 68.0 jit_solution(6204978603678137046)
XLA Ops:
  0.0 3.9 %collective-permute-start = (f32[2,2,2,64,128]{4,3,2,1,0:T(8,128)}, f32[2,2,2,64,128]{4,3,2,1,0:T(8,128)S(1)}, u32[]{:S(2)}, u32[]{:S(2)}) collective-permute-start(f32[2,2,2,64,128]{4,3,2,1,0:T(8,128)} %param.12), channel_id=1, source_target_pairs={{0,32},{32,64},{64,96},{96,128},{128,160},{160,192},{192,224},{224... | collective-permute-start | bytes 786440 | tf_op jit(solution)/shard_map/ppermute | solution.py:26
  3.9 5.6 %collective-permute-start.1 = (f32[2,2,2,64,128]{4,3,2,1,0:T(8,128)}, f32[2,2,2,64,128]{4,3,2,1,0:T(8,128)S(1)}, u32[]{:S(2)}, u32[]{:S(2)}) collective-permute-start(f32[2,2,2,64,128]{4,3,2,1,0:T(8,128)} %param.12), channel_id=1, source_target_pairs={{32,0},{64,32},{96,64},{128,96},{160,128},{192,160},{224,192},{256... | collective-permute-start | bytes 786440 | tf_op jit(solution)/shard_map/ppermute | solution.py:29
  9.6 0.7 %add_select_fusion = s32[64,5]{0,1:T(8,128)S(1)} fusion(s32[64,5]{0,1:T(8,128)} %param.17, s32[]{:T(128)S(6)} %mul.3), kind=kLoop, calls=%fused_computation.12 | loop fusion | flops 4160 | bytes 2564 | tf_op jit(solution)/shard_map/jit(remainder)/select_n | solution.py:334
  10.3 0.8 %select_reduce_fusion = f32[64,192]{1,0:T(8,128)S(1)} fusion(f32[5]{0:T(128)} %param.19, s32[64,5]{0,1:T(8,128)S(1)} %add_select_fusion), kind=kLoop, calls=%fused_computation.4 | loop fusion | flops 172032 | bytes 50452 | tf_op jit(solution)/shard_map/reduce_sum | solution.py:335
  11.1 0.0 copy-start.1
  11.1 0.0 copy-start
  11.2 4.9 %copy_bitcast_fusion = (f32[5,16,4096]{2,1,0:T(8,128)}, f32[5,16,4096]{2,1,0:T(8,128)}) fusion(f32[5,8,2,4096]{3,2,1,0:T(2,128)} %bitcast.50, f32[5,8,2,4096]{3,2,1,0:T(2,128)} %bitcast.51), kind=kLoop, calls=%fused_computation | loop fusion | bytes 5242880 | tf_op jit(solution)/shard_map/reshape | solution.py:360
  16.1 0.1 fusion.4
  16.2 0.0 copy-done.1
  16.2 0.4 fusion.2
  16.5 0.0 copy-done
  16.6 0.9 %copy.48 = f32[1,8,2,4096]{3,1,2,0:T(8,128)} copy(f32[1,8,2,4096]{3,2,1,0:T(2,128)S(1)} %bitcast.55) | data formatting | bytes 524288 | tf_op jit(solution)/shard_map/reshape | solution.py:359
  17.4 0.0 collective-permute-done.1
  17.4 0.4 fusion.1
  17.8 0.0 collective-permute-done
  17.8 1.1 %fusion = f32[32,2,8,128]{3,0,2,1:T(8,128)} fusion(f32[32,2,8,128]{3,0,2,1:T(8,128)S(1)} %fusion.1, f32[32,2,8,128]{3,0,2,1:T(8,128)S(1)} %fusion.2, f32[8,64,128,1]{2,1,0,3:T(8,128)S(1)} %bitcast.58, f32[32,2,64]{2,1,0:T(2,128)S(1)} %get-tuple-element.5), kind=kOutput, calls=%fused_computation.3 | convolution fusion | flops 50462720 | bytes 1064960 | tf_op jit(solution)/shard_map/dkr,bre->kbde/dot_general | solution.py:348
  18.9 47.3 %shard_map.118 = f32[16,4096]{1,0:T(8,128)} custom-call(s32[5]{0:T(128)} %slot_ref.1, s32[2]{0:T(128)} %shift_ref.1, s32[64]{0:T(128)} %class_ref.1, f32[2]{0:T(128)} %optical_ref.1, f32[2]{0:T(128)} %occ_ref.1, f32[4]{0:T(128)} %acoustic_ref.1, f32[16,32,128]{2,1,0:T(8,128)} %bitcast.54, f32[16,4096]{1,0:T(8,128)} %bitcast.52, ...), custom_call_target="tpu_custom_call" | custom-call | tf_op jit(solution)/shard_map/pallas_call | solution.py:287
  66.1 1.9 %copy.32 = f32[8,2,4096]{2,1,0:T(2,128)} copy(f32[8,2,4096]{2,0,1:T(8,128)} %bitcast.53) | data formatting | bytes 524288 | tf_op jit(solution)/shard_map/transpose | solution.py:372
  (1 shorter events, 0.0 us)
Async XLA Ops:
  0.0 17.8 %collective-permute-start = (f32[2,2,2,64,128]{4,3,2,1,0:T(8,128)}, f32[2,2,2,64,128]{4,3,2,1,0:T(8,128)S(1)}, u32[]{:S(2)}, u32[]{:S(2)}) collective-permute-start(f32[2,2,2,64,128]{4,3,2,1,0:T(8,128)} %param.12), channel_id=1, source_target_pairs={{0,32},{32,64},{64,96},{96,128},{128,160},{160,192},{192,224},{224... | collective-permute-start | bytes 786440 | tf_op jit(solution)/shard_map/ppermute | solution.py:26
  3.9 13.5 %collective-permute-start.1 = (f32[2,2,2,64,128]{4,3,2,1,0:T(8,128)}, f32[2,2,2,64,128]{4,3,2,1,0:T(8,128)S(1)}, u32[]{:S(2)}, u32[]{:S(2)}) collective-permute-start(f32[2,2,2,64,128]{4,3,2,1,0:T(8,128)} %param.12), channel_id=1, source_target_pairs={{32,0},{64,32},{96,64},{128,96},{160,128},{192,160},{224,192},{256... | collective-permute-start | bytes 786440 | tf_op jit(solution)/shard_map/ppermute | solution.py:29
  11.1 5.0 %copy-start.1 = (f32[2,2,2,64,128]{4,3,2,1,0:T(8,128)S(1)}, f32[2,2,2,64,128]{4,3,2,1,0:T(8,128)}, u32[]{:S(2)}) copy-start(f32[2,2,2,64,128]{4,3,2,1,0:T(8,128)} %param.12) | copy-start | bytes 786436
  11.1 5.4 %copy-start = (f32[2,2,2,2,4096]{4,3,2,1,0:T(2,128)S(1)}, f32[2,2,2,2,4096]{4,3,2,1,0:T(2,128)}, u32[]{:S(2)}) copy-start(f32[2,2,2,2,4096]{4,3,2,1,0:T(2,128)} %param.13) | copy-start | bytes 786436

commit v15 on v14

--- a/solution.py
+++ b/solution.py
@@ -158,6 +158,20 @@
     return sorted(range(count - 1), key=lambda s: (-min(s + 1, count - s - 1), s))
 
 
+def _far_first_grid(count, inner):
+    if count % inner:
+        return _far_first(count)
+
+    def ring(d, size):
+        return min(d % size, size - d % size)
+
+    outer = count // inner
+    return sorted(
+        range(count - 1),
+        key=lambda s: (-(ring(s + 1, inner) + ring((s + 1) // inner, outer)), s),
+    )
+
+
 def _fused_kernel(nk, ne, entries, margin,
                   slot_ref, shift_ref, class_ref, optical_ref, occ_ref, acoustic_ref,
                   chunk_ref, cur_ref, pin_ref, pres_ref, out_ref,
@@ -170,7 +184,7 @@
     barrier = pltpu.get_barrier_semaphore()
     for s in _far_first(ne):
         pl.semaphore_signal(barrier, 1, device_id=(mk, (me + s + 1) % ne), device_id_type=MESH)
-    for s in _far_first(nk):
+    for s in _far_first_grid(nk, 4):
         pl.semaphore_signal(barrier, 1, device_id=((mk + s + 1) % nk, me), device_id_type=MESH)
     ypad[:, :margin] = jnp.zeros((rows, margin), jnp.float32)
     ypad[:, margin + length :] = jnp.zeros((rows, margin), jnp.float32)
@@ -227,9 +241,9 @@
     fresh = _pair_sums([res] + history, [(0, j) for j in range(HIST + 1)])
     send1[...] = _pack_rows(fresh + gram)
 
-    def exchange(src, recv, ssem, rsem, count, peer):
+    def exchange(src, recv, ssem, rsem, count, peer, order):
         out = [None] * (count - 1)
-        for s in _far_first(count):
+        for s in order:
             c = pltpu.make_async_remote_copy(
                 src_ref=src,
                 dst_ref=recv.at[count - 2 - s],
@@ -255,12 +269,12 @@
             acc = acc + jnp.where(idx == mine, own, recv[slot])
         return acc
 
-    pending = exchange(send1, recv1, ss1, rs1, nk, lambda s: ((mk + s + 1) % nk, me))
+    pending = exchange(send1, recv1, ss1, rs1, nk, lambda s: ((mk + s + 1) % nk, me), _far_first_grid(nk, 4))
     for m in range(HIST):
         bases[m] = pin_ref[m] + mixing_share * history[m]
     finish(pending)
     acc1[...] = total(send1[...], recv1, mk, nk)
-    finish(exchange(acc1, recv2, ss2, rs2, ne, lambda s: (mk, (me + s + 1) % ne)))
+    finish(exchange(acc1, recv2, ss2, rs2, ne, lambda s: (mk, (me + s + 1) % ne), _far_first(ne)))
     summed = _unpack_rows(total(acc1[...], recv2, me, ne))
     perm = [0] + [slot_ref[i] + 1 for i in range(HIST)]
     aged = _permute_square(summed / entries, perm)

time: 68.2 us -> 68.2 us (level)
  no operation moved by 1% of the time
where the time goes in v15:
time: 68.2 us; the launch traced here: 68 us
  Pallas kernels  47.2 us (69%)
  starting transfers between devices  9.58 us (14%)
  local copies, waits for them, and re-layouts  7.78 us (11%)
  matrix products  1.78 us (3%)
  other arithmetic  1.48 us (2%)
    pallas_call x1, Pallas kernels, fused_tail(): pl.pallas_call(functools.partial(_fused_kernel, nk, ne, entries, margin),...  47.2 us
    ppermute x1, starting transfers between devices, padded_2(): lax.ppermute(lax.slice_in_dim(block, 0, width, axis=dim), axis, backward)  5.64 us
    reshape x1, local copies, waits for them, and re-layouts, to_rows(): jnp.swapaxes(x, 1, 2)  4.91 us
    ppermute x1, starting transfers between devices, padded_2(): lax.ppermute(lax.slice_in_dim(block, block.shape[dim] - width, None, axis...  3.94 us
    transpose x1, local copies, waits for them, and re-layouts, per_device(): jnp.swapaxes(mixed.reshape(rows_here, -1, lanes), 0, 1)  1.86 us
    dot_general x3, matrix products, per_device(): jnp.einsum('dkr,bre->kbde', stencil[:, :, part * group_len:(part + 1) * g...  1.78 us
  transfers between devices with their start and end apart: 2, of which 0 were waited for; matrix products, arithmetic and copies ran while one was open for 12% of the time, Pallas kernels for 0%

profile of v15, /device:TPU:1, one launch (start us, length us, event | category | flops | bytes accessed | tf_op | source)
XLA Modules:
  0.0 68.0 jit_solution(1660634214827937708)
XLA Ops:
  0.0 3.9 %collective-permute-start = (f32[2,2,2,64,128]{4,3,2,1,0:T(8,128)}, f32[2,2,2,64,128]{4,3,2,1,0:T(8,128)S(1)}, u32[]{:S(2)}, u32[]{:S(2)}) collective-permute-start(f32[2,2,2,64,128]{4,3,2,1,0:T(8,128)} %param.12), channel_id=1, source_target_pairs={{0,32},{32,64},{64,96},{96,128},{128,160},{160,192},{192,224},{224... | collective-permute-start | bytes 786440 | tf_op jit(solution)/shard_map/ppermute | solution.py:26
  3.9 5.6 %collective-permute-start.1 = (f32[2,2,2,64,128]{4,3,2,1,0:T(8,128)}, f32[2,2,2,64,128]{4,3,2,1,0:T(8,128)S(1)}, u32[]{:S(2)}, u32[]{:S(2)}) collective-permute-start(f32[2,2,2,64,128]{4,3,2,1,0:T(8,128)} %param.12), channel_id=1, source_target_pairs={{32,0},{64,32},{96,64},{128,96},{160,128},{192,160},{224,192},{256... | collective-permute-start | bytes 786440 | tf_op jit(solution)/shard_map/ppermute | solution.py:29
  9.6 0.7 %add_select_fusion = s32[64,5]{0,1:T(8,128)S(1)} fusion(s32[64,5]{0,1:T(8,128)} %param.17, s32[]{:T(128)S(6)} %mul.3), kind=kLoop, calls=%fused_computation.12 | loop fusion | flops 4160 | bytes 2564 | tf_op jit(solution)/shard_map/jit(remainder)/select_n | solution.py:348
  10.3 0.8 %select_reduce_fusion = f32[64,192]{1,0:T(8,128)S(1)} fusion(f32[5]{0:T(128)} %param.19, s32[64,5]{0,1:T(8,128)S(1)} %add_select_fusion), kind=kLoop, calls=%fused_computation.4 | loop fusion | flops 172032 | bytes 50452 | tf_op jit(solution)/shard_map/reduce_sum | solution.py:349
  11.1 0.0 copy-start.1
  11.1 0.0 copy-start
  11.2 4.9 %copy_bitcast_fusion = (f32[5,16,4096]{2,1,0:T(8,128)}, f32[5,16,4096]{2,1,0:T(8,128)}) fusion(f32[5,8,2,4096]{3,2,1,0:T(2,128)} %bitcast.50, f32[5,8,2,4096]{3,2,1,0:T(2,128)} %bitcast.51), kind=kLoop, calls=%fused_computation | loop fusion | bytes 5242880 | tf_op jit(solution)/shard_map/reshape | solution.py:374
  16.1 0.1 fusion.4
  16.2 0.0 copy-done.1
  16.2 0.4 fusion.2
  16.5 0.0 copy-done
  16.6 0.9 %copy.48 = f32[1,8,2,4096]{3,1,2,0:T(8,128)} copy(f32[1,8,2,4096]{3,2,1,0:T(2,128)S(1)} %bitcast.55) | data formatting | bytes 524288 | tf_op jit(solution)/shard_map/reshape | solution.py:373
  17.4 0.0 collective-permute-done.1
  17.4 0.4 fusion.1
  17.8 0.0 collective-permute-done
  17.8 1.1 %fusion = f32[32,2,8,128]{3,0,2,1:T(8,128)} fusion(f32[32,2,8,128]{3,0,2,1:T(8,128)S(1)} %fusion.1, f32[32,2,8,128]{3,0,2,1:T(8,128)S(1)} %fusion.2, f32[8,64,128,1]{2,1,0,3:T(8,128)S(1)} %bitcast.58, f32[32,2,64]{2,1,0:T(2,128)S(1)} %get-tuple-element.5), kind=kOutput, calls=%fused_computation.3 | convolution fusion | flops 50462720 | bytes 1064960 | tf_op jit(solution)/shard_map/dkr,bre->kbde/dot_general | solution.py:362
  18.9 47.2 %shard_map.118 = f32[16,4096]{1,0:T(8,128)} custom-call(s32[5]{0:T(128)} %slot_ref.1, s32[2]{0:T(128)} %shift_ref.1, s32[64]{0:T(128)} %class_ref.1, f32[2]{0:T(128)} %optical_ref.1, f32[2]{0:T(128)} %occ_ref.1, f32[4]{0:T(128)} %acoustic_ref.1, f32[16,32,128]{2,1,0:T(8,128)} %bitcast.54, f32[16,4096]{1,0:T(8,128)} %bitcast.52, ...), custom_call_target="tpu_custom_call" | custom-call | tf_op jit(solution)/shard_map/pallas_call | solution.py:301
  66.1 1.9 %copy.32 = f32[8,2,4096]{2,1,0:T(2,128)} copy(f32[8,2,4096]{2,0,1:T(8,128)} %bitcast.53) | data formatting | bytes 524288 | tf_op jit(solution)/shard_map/transpose | solution.py:386
  (1 shorter events, 0.0 us)
Async XLA Ops:
  0.0 17.8 %collective-permute-start = (f32[2,2,2,64,128]{4,3,2,1,0:T(8,128)}, f32[2,2,2,64,128]{4,3,2,1,0:T(8,128)S(1)}, u32[]{:S(2)}, u32[]{:S(2)}) collective-permute-start(f32[2,2,2,64,128]{4,3,2,1,0:T(8,128)} %param.12), channel_id=1, source_target_pairs={{0,32},{32,64},{64,96},{96,128},{128,160},{160,192},{192,224},{224... | collective-permute-start | bytes 786440 | tf_op jit(solution)/shard_map/ppermute | solution.py:26
  3.9 13.5 %collective-permute-start.1 = (f32[2,2,2,64,128]{4,3,2,1,0:T(8,128)}, f32[2,2,2,64,128]{4,3,2,1,0:T(8,128)S(1)}, u32[]{:S(2)}, u32[]{:S(2)}) collective-permute-start(f32[2,2,2,64,128]{4,3,2,1,0:T(8,128)} %param.12), channel_id=1, source_target_pairs={{32,0},{64,32},{96,64},{128,96},{160,128},{192,160},{224,192},{256... | collective-permute-start | bytes 786440 | tf_op jit(solution)/shard_map/ppermute | solution.py:29
  11.1 5.0 %copy-start.1 = (f32[2,2,2,64,128]{4,3,2,1,0:T(8,128)S(1)}, f32[2,2,2,64,128]{4,3,2,1,0:T(8,128)}, u32[]{:S(2)}) copy-start(f32[2,2,2,64,128]{4,3,2,1,0:T(8,128)} %param.12) | copy-start | bytes 786436
  11.1 5.4 %copy-start = (f32[2,2,2,2,4096]{4,3,2,1,0:T(2,128)S(1)}, f32[2,2,2,2,4096]{4,3,2,1,0:T(2,128)}, u32[]{:S(2)}) copy-start(f32[2,2,2,2,4096]{4,3,2,1,0:T(2,128)} %param.13) | copy-start | bytes 786436

commit v16 on v14

--- a/solution.py
+++ b/solution.py
@@ -178,13 +178,15 @@
     pl.semaphore_wait(barrier, nk - 1 + ne - 1)
 
     copies = [None] * (ne - 1)
+    odd = me % 2
     for s in _far_first(ne):
-        peer = (me + s + 1) % ne
+        mirrored = odd * (ne - 2 - s) + (1 - odd) * s
+        peer = (me + mirrored + 1) % ne
         c = pltpu.make_async_remote_copy(
             src_ref=chunk_ref.at[:, peer, :],
             dst_ref=ypad.at[:, pl.ds(pl.multiple_of(margin + me * width, width), width)],
-            send_sem=ts.at[s],
-            recv_sem=tr.at[ne - 2 - s],
+            send_sem=ts.at[mirrored],
+            recv_sem=tr.at[ne - 2 - mirrored],
             device_id=(mk, peer),
             device_id_type=MESH,
         )

time: 68.2 us -> 68.2 us (level)
  no operation moved by 1% of the time
where the time goes in v16:
time: 68.2 us; the launch traced here: 68 us
  Pallas kernels  47.3 us (69%)
  starting transfers between devices  9.58 us (14%)
  local copies, waits for them, and re-layouts  7.78 us (11%)
  matrix products  1.78 us (3%)
  other arithmetic  1.48 us (2%)
    pallas_call x1, Pallas kernels, fused_tail(): pl.pallas_call(functools.partial(_fused_kernel, nk, ne, entries, margin),...  47.3 us
    ppermute x1, starting transfers between devices, padded_2(): lax.ppermute(lax.slice_in_dim(block, 0, width, axis=dim), axis, backward)  5.64 us
    reshape x1, local copies, waits for them, and re-layouts, to_rows(): jnp.swapaxes(x, 1, 2)  4.91 us
    ppermute x1, starting transfers between devices, padded_2(): lax.ppermute(lax.slice_in_dim(block, block.shape[dim] - width, None, axis...  3.94 us
    transpose x1, local copies, waits for them, and re-layouts, per_device(): jnp.swapaxes(mixed.reshape(rows_here, -1, lanes), 0, 1)  1.86 us
    dot_general x3, matrix products, per_device(): jnp.einsum('dkr,bre->kbde', stencil[:, :, part * group_len:(part + 1) * g...  1.78 us
  transfers between devices with their start and end apart: 2, of which 0 were waited for; matrix products, arithmetic and copies ran while one was open for 12% of the time, Pallas kernels for 0%

profile of v16, /device:TPU:1, one launch (start us, length us, event | category | flops | bytes accessed | tf_op | source)
XLA Modules:
  0.0 68.0 jit_solution(11350003034772131264)
XLA Ops:
  0.0 3.9 %collective-permute-start = (f32[2,2,2,64,128]{4,3,2,1,0:T(8,128)}, f32[2,2,2,64,128]{4,3,2,1,0:T(8,128)S(1)}, u32[]{:S(2)}, u32[]{:S(2)}) collective-permute-start(f32[2,2,2,64,128]{4,3,2,1,0:T(8,128)} %param.12), channel_id=1, source_target_pairs={{0,32},{32,64},{64,96},{96,128},{128,160},{160,192},{192,224},{224... | collective-permute-start | bytes 786440 | tf_op jit(solution)/shard_map/ppermute | solution.py:26
  3.9 5.6 %collective-permute-start.1 = (f32[2,2,2,64,128]{4,3,2,1,0:T(8,128)}, f32[2,2,2,64,128]{4,3,2,1,0:T(8,128)S(1)}, u32[]{:S(2)}, u32[]{:S(2)}) collective-permute-start(f32[2,2,2,64,128]{4,3,2,1,0:T(8,128)} %param.12), channel_id=1, source_target_pairs={{32,0},{64,32},{96,64},{128,96},{160,128},{192,160},{224,192},{256... | collective-permute-start | bytes 786440 | tf_op jit(solution)/shard_map/ppermute | solution.py:29
  9.6 0.7 %add_select_fusion = s32[64,5]{0,1:T(8,128)S(1)} fusion(s32[64,5]{0,1:T(8,128)} %param.17, s32[]{:T(128)S(6)} %mul.3), kind=kLoop, calls=%fused_computation.12 | loop fusion | flops 4160 | bytes 2564 | tf_op jit(solution)/shard_map/jit(remainder)/select_n | solution.py:336
  10.3 0.8 %select_reduce_fusion = f32[64,192]{1,0:T(8,128)S(1)} fusion(f32[5]{0:T(128)} %param.19, s32[64,5]{0,1:T(8,128)S(1)} %add_select_fusion), kind=kLoop, calls=%fused_computation.4 | loop fusion | flops 172032 | bytes 50452 | tf_op jit(solution)/shard_map/reduce_sum | solution.py:337
  11.1 0.0 copy-start.1
  11.1 0.0 copy-start
  11.2 4.9 %copy_bitcast_fusion = (f32[5,16,4096]{2,1,0:T(8,128)}, f32[5,16,4096]{2,1,0:T(8,128)}) fusion(f32[5,8,2,4096]{3,2,1,0:T(2,128)} %bitcast.50, f32[5,8,2,4096]{3,2,1,0:T(2,128)} %bitcast.51), kind=kLoop, calls=%fused_computation | loop fusion | bytes 5242880 | tf_op jit(solution)/shard_map/reshape | solution.py:362
  16.1 0.1 fusion.4
  16.2 0.0 copy-done.1
  16.2 0.4 fusion.2
  16.5 0.0 copy-done
  16.6 0.9 %copy.48 = f32[1,8,2,4096]{3,1,2,0:T(8,128)} copy(f32[1,8,2,4096]{3,2,1,0:T(2,128)S(1)} %bitcast.55) | data formatting | bytes 524288 | tf_op jit(solution)/shard_map/reshape | solution.py:361
  17.4 0.0 collective-permute-done.1
  17.4 0.4 fusion.1
  17.8 0.0 collective-permute-done
  17.8 1.1 %fusion = f32[32,2,8,128]{3,0,2,1:T(8,128)} fusion(f32[32,2,8,128]{3,0,2,1:T(8,128)S(1)} %fusion.1, f32[32,2,8,128]{3,0,2,1:T(8,128)S(1)} %fusion.2, f32[8,64,128,1]{2,1,0,3:T(8,128)S(1)} %bitcast.58, f32[32,2,64]{2,1,0:T(2,128)S(1)} %get-tuple-element.5), kind=kOutput, calls=%fused_computation.3 | convolution fusion | flops 50462720 | bytes 1064960 | tf_op jit(solution)/shard_map/dkr,bre->kbde/dot_general | solution.py:350
  18.9 47.3 %shard_map.118 = f32[16,4096]{1,0:T(8,128)} custom-call(s32[5]{0:T(128)} %slot_ref.1, s32[2]{0:T(128)} %shift_ref.1, s32[64]{0:T(128)} %class_ref.1, f32[2]{0:T(128)} %optical_ref.1, f32[2]{0:T(128)} %occ_ref.1, f32[4]{0:T(128)} %acoustic_ref.1, f32[16,32,128]{2,1,0:T(8,128)} %bitcast.54, f32[16,4096]{1,0:T(8,128)} %bitcast.52, ...), custom_call_target="tpu_custom_call" | custom-call | tf_op jit(solution)/shard_map/pallas_call | solution.py:289
  66.1 1.9 %copy.32 = f32[8,2,4096]{2,1,0:T(2,128)} copy(f32[8,2,4096]{2,0,1:T(8,128)} %bitcast.53) | data formatting | bytes 524288 | tf_op jit(solution)/shard_map/transpose | solution.py:374
  (1 shorter events, 0.0 us)
Async XLA Ops:
  0.0 17.8 %collective-permute-start = (f32[2,2,2,64,128]{4,3,2,1,0:T(8,128)}, f32[2,2,2,64,128]{4,3,2,1,0:T(8,128)S(1)}, u32[]{:S(2)}, u32[]{:S(2)}) collective-permute-start(f32[2,2,2,64,128]{4,3,2,1,0:T(8,128)} %param.12), channel_id=1, source_target_pairs={{0,32},{32,64},{64,96},{96,128},{128,160},{160,192},{192,224},{224... | collective-permute-start | bytes 786440 | tf_op jit(solution)/shard_map/ppermute | solution.py:26
  3.9 13.5 %collective-permute-start.1 = (f32[2,2,2,64,128]{4,3,2,1,0:T(8,128)}, f32[2,2,2,64,128]{4,3,2,1,0:T(8,128)S(1)}, u32[]{:S(2)}, u32[]{:S(2)}) collective-permute-start(f32[2,2,2,64,128]{4,3,2,1,0:T(8,128)} %param.12), channel_id=1, source_target_pairs={{32,0},{64,32},{96,64},{128,96},{160,128},{192,160},{224,192},{256... | collective-permute-start | bytes 786440 | tf_op jit(solution)/shard_map/ppermute | solution.py:29
  11.1 5.0 %copy-start.1 = (f32[2,2,2,64,128]{4,3,2,1,0:T(8,128)S(1)}, f32[2,2,2,64,128]{4,3,2,1,0:T(8,128)}, u32[]{:S(2)}) copy-start(f32[2,2,2,64,128]{4,3,2,1,0:T(8,128)} %param.12) | copy-start | bytes 786436
  11.1 5.4 %copy-start = (f32[2,2,2,2,4096]{4,3,2,1,0:T(2,128)S(1)}, f32[2,2,2,2,4096]{4,3,2,1,0:T(2,128)}, u32[]{:S(2)}) copy-start(f32[2,2,2,2,4096]{4,3,2,1,0:T(2,128)} %param.13) | copy-start | bytes 786436
